TPU v7x, 128 devices: a whole 4x4x4 slice. The times are simulated.
128 devices in a mesh: rows: 32 (over x, y, core), feat: 4 (over z).
Axes of the slice: x: 4, y: 4, z: 4, core: 2. Of those that a mesh axis runs over, the one named last changes fastest.
Arguments:
- design: bfloat16 [8192, 65536], P('rows', 'feat')
- labels: int32 [8192], P('rows'), may hold values from -1 to 1, as said below
- start_position: float32 [16, 65536], P(None, 'feat')
- momenta: float32 [8, 4, 65536], P(None, None, 'feat'), may hold values from -6 to 6
- lag_offsets: int32 [8], replicated, may hold values from 0 to 2, as said below
- accept_bits: int32 [2, 16], replicated, may hold values 0 or 1
- step_sizes: float32 [8], replicated, may hold values from 0.1 to 0.3
Outputs:
- final_position: float32 [16, 65536], P(None, 'feat')
- final_momentum: float32 [16, 65536], P(None, 'feat')
- log_likelihood: float32 [2, 16], replicated
- distance: float32 [2, 8], replicated
Inputs may be any that keep to these rules, and one draw needn't show every extreme that they name: `labels`: each entry is -1 or 1. `lag_offsets`: some pair has lag 0 and some pair has lag 2.
All inputs are finite; a program needn't handle non-finite values.
Results may differ from a plain program's by a relative error of at most 0.00043.
Values may be sent and summed in bfloat16 or wider, within the bound.
No kernel may reach another device: no remote copies, remote signals or barrier semaphores. Data moves between devices by JAX's collectives and lax.ppermute only.
A program may use at most 64 MiB of HBM per device.

v0:
```python
import jax
import jax.numpy as jnp
from jax import lax
from jax.experimental import pallas as pl
from jax.experimental.pallas import tpu as pltpu
from jax.sharding import PartitionSpec as P

FEATURES = 65536
TRANS = 2
LEAP = 5
PAIRS = 8
CHAINS = 16
EXTRA = 128
CHUNKS = 4
GROUP = 4
WIDE = 8

F32 = jnp.float32
BF16 = jnp.bfloat16
VMEM = pl.BlockSpec(memory_space=pltpu.VMEM)
HBM = pl.BlockSpec(memory_space=pltpu.HBM)
SMEM = pl.BlockSpec(memory_space=pltpu.SMEM)
CROSS = (((1,), (1,)), ((), ()))


def limit(mib):
    return pltpu.CompilerParams(vmem_limit_bytes=mib * 1024 * 1024)


def call(body, name, ins, outs, scratch=(), flops=0, mib=6):
    return pl.pallas_call(
        body,
        in_specs=[spec for _, spec in ins],
        out_specs=[VMEM] * len(outs),
        out_shape=[jax.ShapeDtypeStruct(*o) for o in outs],
        scratch_shapes=list(scratch),
        compiler_params=limit(mib),
        cost_estimate=pl.CostEstimate(flops=flops, bytes_accessed=flops // 16, transcendentals=0),
        name=name,
    )(*[a for a, _ in ins])


def vmem(*arrays):
    return [(a, VMEM) for a in arrays]


def prepare(design, start):
    rows, width = design.shape
    half = width // 2
    step = half // CHUNKS

    def body(start_ref, design_ref, margins_ref, own_ref, away_ref, q_ref, far_ref, sems):
        core = lax.rem(lax.axis_index("rows"), 2)
        near = core * half
        far = (1 - core) * half
        count = [0]

        def fetch(source, target):
            copy = pltpu.make_async_copy(source, target, sems.at[count[0]])
            count[0] += 1
            copy.start()
            return copy

        def cols(offset, size):
            return pl.ds(pl.multiple_of(offset, step), size)

        first = [
            fetch(start_ref.at[:, cols(far, half)], far_ref),
            fetch(start_ref.at[:, cols(near, half)], q_ref),
        ]
        pieces = []
        for offset, target, coefs in ((far, away_ref, far_ref), (near, own_ref, q_ref)):
            for i in range(CHUNKS):
                here = slice(i * step, (i + 1) * step)
                copy = fetch(
                    design_ref.at[:, cols(offset + i * step, step)],
                    target.at[:, pl.ds(i * step, step)],
                )
                pieces.append((copy, target, coefs, here))
        for copy in first:
            copy.wait()
        total = jnp.zeros((CHAINS, rows), F32)
        for copy, target, coefs, here in pieces:
            copy.wait()
            total = total + lax.dot_general(
                coefs[:, here].astype(BF16), target[:, here], CROSS, preferred_element_type=F32
            )
        margins_ref[...] = total

    piece = ((rows, half), design.dtype)
    return call(
        body,
        "prepare",
        [(start, HBM), (design, HBM)],
        [((CHAINS, rows), F32), piece, piece, ((CHAINS, half), F32)],
        [pltpu.VMEM((CHAINS, half), F32), pltpu.SemaphoreType.DMA((2 + 2 * CHUNKS,))],
        2 * CHAINS * rows * width,
        38,
    )


def draw(labels, momenta, lag_offsets, accept_bits, step_sizes):
    rows = labels.shape[0]
    slots, width = momenta.shape[1:]
    half = width // 2

    def body(lag_ref, accept_ref, steps_ref, label_ref, bank_ref, *refs):
        mom0_ref, mom1_ref, h_ref, keep0_ref, keep1_ref, sign_ref, draws_ref, sem = refs
        core = lax.rem(lax.axis_index("rows"), 2)
        cols = pl.ds(pl.multiple_of(core * half, half), half)
        copy = pltpu.make_async_copy(bank_ref.at[:, :, cols], draws_ref, sem)
        copy.start()
        row = lax.broadcasted_iota(jnp.int32, (CHAINS, EXTRA), 0)
        h = jnp.zeros((CHAINS, EXTRA), F32)
        for k in range(PAIRS):
            h = jnp.where(row // 2 == k, steps_ref[k], h)
        h_ref[...] = h
        for s, keep_ref in enumerate((keep0_ref, keep1_ref)):
            keep = jnp.zeros((CHAINS, EXTRA), F32)
            for k in range(CHAINS):
                keep = jnp.where(row == k, accept_ref[s, k].astype(F32), keep)
            keep_ref[...] = keep
        sign_ref[...] = jnp.broadcast_to(label_ref[...].astype(F32), (8, rows))
        copy.wait()
        for s, out_ref in enumerate((mom0_ref, mom1_ref)):
            for k in range(PAIRS):
                out_ref[2 * k : 2 * k + 1] = draws_ref[k, pl.ds(s + lag_ref[k], 1)]
                out_ref[2 * k + 1 : 2 * k + 2] = draws_ref[k, s : s + 1]

    small = ((CHAINS, EXTRA), F32)
    state = ((CHAINS, half), F32)
    return call(
        body,
        "draw",
        [
            (lag_offsets, SMEM),
            (accept_bits, SMEM),
            (step_sizes, SMEM),
            (labels[None, :], VMEM),
            (momenta, HBM),
        ],
        [state, state, small, small, small, ((8, rows), F32)],
        [pltpu.VMEM((PAIRS, slots, half), F32), pltpu.SemaphoreType.DMA],
        0,
        8,
    )


def pair_start(mine, other):
    rows = mine.shape[1]

    def body(mine_ref, other_ref, margins_ref):
        margins_ref[:, :rows] = mine_ref[...]
        margins_ref[:, rows:] = other_ref[...]

    return call(body, "pair_start", vmem(mine, other), [((CHAINS, 2 * rows), F32)])[0]


def pair_sum(mine, other, rows):
    def body(mine_ref, other_ref, out_ref):
        out_ref[:, :rows] = mine_ref[:, :rows] + other_ref[:, rows : 2 * rows]
        out_ref[:, rows : 2 * rows] = mine_ref[:, rows : 2 * rows] + other_ref[:, :rows]
        if mine.shape[1] > 2 * rows:
            out_ref[:, 2 * rows :] = mine_ref[:, 2 * rows :] + other_ref[:, 2 * rows :]

    return call(body, "pair_sum", vmem(mine, other), [(mine.shape, F32)])[0]


def assemble(mine, other):
    half = mine.shape[1]

    def body(mine_ref, other_ref, out_ref, sems):
        core = lax.rem(lax.axis_index("rows"), 2)
        copies = []
        for i, (ref, at) in enumerate(((mine_ref, core), (other_ref, 1 - core))):
            cols = pl.ds(pl.multiple_of(at * half, half), half)
            copies.append(pltpu.make_async_copy(ref, out_ref.at[:, cols], sems.at[i]))
            copies[-1].start()
        for copy in copies:
            copy.wait()

    return pl.pallas_call(
        body,
        in_specs=[VMEM, VMEM],
        out_specs=HBM,
        out_shape=jax.ShapeDtypeStruct((CHAINS, 2 * half), F32),
        scratch_shapes=[pltpu.SemaphoreType.DMA((2,))],
        compiler_params=limit(6),
        name="assemble",
    )(mine, other)


def square_gap(position):
    gap = position - pltpu.roll(position, CHAINS - 1, 0)
    return jnp.sum(gap * gap, axis=1, keepdims=True)


def margins_kernel(mode, held, arrived, h, state):
    rows, width = held[0].shape
    blocks, _, block = arrived.shape
    names = list(state)
    wide = ((CHAINS, width), F32)
    outs = {"margins": ((CHAINS, 2 * rows + (EXTRA if mode == "last" else 0)), F32), "q": wide, "p": wide}
    if mode == "turn":
        outs["pos"] = wide
        outs["gap"] = ((CHAINS, EXTRA), F32)
    if mode == "last":
        outs["pos"] = wide

    def body(own_ref, other_ref, arrived_ref, h_ref, *refs):
        ins = dict(zip(names, refs))
        out = dict(zip(outs, refs[len(names) :]))
        h_col = h_ref[...]
        h_wide = jnp.broadcast_to(h_col[:, :1], (CHAINS, block))
        if mode in ("turn", "last"):
            keep = jnp.broadcast_to(ins["keep"][:, :1], (CHAINS, block)) != 0.0

        def one(b, cols, own, other, gap):
            g = arrived_ref[b].astype(F32)
            q = ins["q"][:, cols]
            if mode == "first":
                p = ins["mom"][:, cols] + 0.5 * h_wide * (g - q)
            elif mode == "turn":
                q0 = ins["q0"][:, cols]
                pos = jnp.where(keep, q, q0)
                gradient = jnp.where(keep, g - q, ins["g0"][b].astype(F32) - q0)
                p = ins["mom"][:, cols] + 0.5 * h_wide * gradient
                q = pos
                out["pos"][:, cols] = pos
                gap = gap + square_gap(pos)
            else:
                p = ins["p"][:, cols] + h_wide * (g - q)
            q = q + h_wide * p
            out["p"][:, cols] = p
            out["q"][:, cols] = q
            if mode == "last":
                pos = jnp.where(keep, q, ins["pos"][:, cols])
                out["pos"][:, cols] = pos
                gap = gap + square_gap(pos)
            rounded = q.astype(BF16)
            own = own + lax.dot_general(
                rounded, own_ref[:, cols], CROSS, preferred_element_type=F32
            )
            other = other + lax.dot_general(
                rounded, other_ref[:, cols], CROSS, preferred_element_type=F32
            )
            return own, other, gap

        def group(i, carry):
            for j in range(GROUP):
                b = i * GROUP + j
                carry = one(b, pl.ds(pl.multiple_of(b * block, block), block), *carry)
            return carry

        zero = jnp.zeros((CHAINS, rows), F32)
        *total, gap = lax.fori_loop(
            0, blocks // GROUP, group, (zero, zero, jnp.zeros((CHAINS, 1), F32))
        )
        if mode == "turn":
            out["gap"][...] = jnp.broadcast_to(gap, (CHAINS, EXTRA))
        if mode == "last":
            lanes = lax.broadcasted_iota(jnp.int32, (CHAINS, EXTRA), 1)
            out["margins"][:, 2 * rows :] = jnp.where(lanes == 0, ins["gap"][...], gap)
        out["margins"][:, :rows] = total[0]
        out["margins"][:, rows : 2 * rows] = total[1]

    result = call(
        body,
        "margins_" + mode,
        vmem(*held, arrived, h, *state.values()),
        list(outs.values()),
        flops=4 * CHAINS * rows * width,
    )
    return dict(zip(outs, result))


def split3(column, first_lane):
    lanes = lax.broadcasted_iota(jnp.int32, (CHAINS, EXTRA), 1) - first_lane
    high = column.astype(BF16).astype(F32)
    middle = (column - high).astype(BF16).astype(F32)
    low = column - high - middle
    out = jnp.where(lanes == 0, high, jnp.zeros((CHAINS, EXTRA), F32))
    out = jnp.where(lanes == 1, middle, out)
    return jnp.where(lanes == 2, low, out)


def terms_kernel(partials, signs, held, blocks, likes, earlier):
    rows, width = held[0].shape
    block = width // blocks
    extended = earlier is not None

    def body(*refs):
        own, one, two, three, mine_ref, theirs_ref, near_ref, far_ref = refs[:8]
        rest = list(refs[8:])
        earlier_ref = rest.pop(0) if extended else None
        out_ref = rest.pop(0)
        total = (own[...] + two[...]) + (one[...] + three[...])
        sign = jnp.concatenate([mine_ref[:1], theirs_ref[:1]], axis=1)
        signed = sign * total[:, : 2 * rows]
        weights = (sign * jax.nn.sigmoid(-signed)).astype(BF16)
        if likes:
            terms = jnp.minimum(signed, 0.0) - jnp.log1p(jnp.exp(-jnp.abs(signed)))
            like = jnp.sum(terms, axis=1, keepdims=True)
            if extended:
                side = split3(earlier_ref[...][:, :1], 0) + split3(like, 3)
                side = side.astype(BF16)
                for b in range(blocks):
                    out_ref[b, :, block:] = side
                squares = total[:, 2 * rows :].T[:2]
                chain = lax.broadcasted_iota(jnp.int32, (CHAINS, PAIRS), 0)
                pair = lax.broadcasted_iota(jnp.int32, (CHAINS, PAIRS), 1)
                leaders = (chain == 2 * pair).astype(F32)
                picked = jnp.dot(
                    squares, leaders, precision=lax.Precision.HIGHEST, preferred_element_type=F32
                )
                rest[0][...] = jnp.sqrt(picked / FEATURES + 1e-06)
            else:
                rest[0][...] = jnp.broadcast_to(like, (CHAINS, EXTRA))
        def group(i, carry):
            for j in range(WIDE):
                b = i * WIDE + j
                cols = pl.ds(pl.multiple_of(b * block, block), block)
                terms = jnp.dot(weights[:, :rows], near_ref[:, cols], preferred_element_type=F32)
                far = jnp.dot(weights[:, rows:], far_ref[:, cols], preferred_element_type=F32)
                out_ref[b, :, :block] = (terms + far).astype(BF16)
            return carry

        lax.fori_loop(0, blocks // WIDE, group, 0)

    outs = [((blocks, CHAINS, block + (EXTRA if extended else 0)), BF16)]
    if likes:
        outs.append(((TRANS, PAIRS) if extended else (CHAINS, EXTRA), F32))
    return call(
        body,
        "terms",
        vmem(*partials, *signs, *held, *([earlier] if extended else [])),
        outs,
        flops=4 * CHAINS * rows * width,
    )


def sum_kernel(arrived, residual, block, observations):
    blocks = arrived.shape[0]
    carried = residual is not None

    def body(*refs):
        arrived_ref = refs[0]
        send_ref, residual_ref = refs[2 if carried else 1 :][:2]
        parts = [arrived_ref[b, :, :block].astype(F32) for b in range(blocks)]
        while len(parts) > 1:
            parts = [parts[i] + parts[i + 1] for i in range(0, len(parts), 2)]
        exact = parts[0] + refs[1][...] if carried else parts[0]
        send = exact.astype(BF16)
        residual_ref[...] = exact - send.astype(F32)
        for b in range(blocks):
            send_ref[b] = send
        if observations:
            side = jnp.zeros((CHAINS, EXTRA), F32)
            for b in range(blocks):
                side = side + arrived_ref[b, :, block:].astype(F32)
            side = side.T
            for s in range(TRANS):
                like = (side[3 * s : 3 * s + 1] + side[3 * s + 1 : 3 * s + 2]) + side[3 * s + 2 : 3 * s + 3]
                refs[-1][s : s + 1] = like / observations

    outs = [((blocks, CHAINS, block), BF16), ((CHAINS, block), F32)]
    if observations:
        outs.append(((TRANS, CHAINS), F32))
    return call(body, "sum", vmem(arrived, *([residual] if carried else [])), outs)


def finish_kernel(arrived, h, p, q):
    blocks, _, block = arrived.shape

    def body(arrived_ref, h_ref, p_ref, q_ref, out_ref):
        half = 0.5 * jnp.broadcast_to(h_ref[...][:, :1], (CHAINS, block))
        for b in range(blocks):
            cols = slice(b * block, (b + 1) * block)
            out_ref[:, cols] = p_ref[:, cols] + half * (arrived_ref[b].astype(F32) - q_ref[:, cols])

    return call(body, "finish", vmem(arrived, h, p, q), [((CHAINS, blocks * block), F32)])[0]


def on_device(design, labels, start_position, momenta, lag_offsets, accept_bits, step_sizes):
    rows, _ = design.shape
    devices = lax.axis_size("rows")
    ring = lax.axis_size("feat")
    blocks = devices // 2
    chips = [[2 * k + core for k in range(blocks)] for core in range(2)]
    swap = [(i, i ^ 1) for i in range(devices)]

    def exchange(blocked):
        return lax.all_to_all(blocked, "rows", 0, 0, axis_index_groups=chips)

    def across(value):
        return lax.ppermute(value, "rows", swap)

    def around(margins):
        moved = {
            k: lax.ppermute(margins, "feat", [(i, (i + k) % ring) for i in range(ring)])
            for k in (1, 3, 2)
        }
        return [margins, moved[1], moved[2], moved[3]]

    def gradient(margins, residual, likes=False, earlier=None):
        last = earlier is not None
        out, *side = terms_kernel(around(margins), signs, held, blocks, likes, earlier)
        block = out.shape[2] - (EXTRA if last else 0)
        send, residual, *totals = sum_kernel(
            exchange(out), residual, block, rows * devices if last else 0
        )
        return exchange(send), residual, side + totals

    def paired(margins):
        return pair_sum(margins, across(margins), rows)

    margins, own, away, start = prepare(design, start_position)
    swapped = across(margins)
    away, swapped = lax.optimization_barrier((away, swapped))
    margins = pair_start(margins, swapped)
    held = (own, across(away))
    mom0, mom1, h, keep0, keep1, sign = draw(labels, momenta, lag_offsets, accept_bits, step_sizes)
    signs = (sign, across(sign))
    g0, residual, _ = gradient(margins, None)
    g = g0
    now = {"q": start}
    for leap in range(LEAP):
        if leap == 0:
            now = margins_kernel("first", held, g, h, {"q": start, "mom": mom0})
        else:
            now = margins_kernel("mid", held, g, h, {"q": now["q"], "p": now["p"]})
        g, residual, side = gradient(paired(now["margins"]), residual, likes=leap + 1 == LEAP)
    (like,) = side
    for leap in range(LEAP):
        last = leap + 1 == LEAP
        if leap == 0:
            state = {"q": now["q"], "q0": start, "g0": g0, "mom": mom1, "keep": keep0}
            now = margins_kernel("turn", held, g, h, state)
            position, gap = now["pos"], now["gap"]
        elif not last:
            now = margins_kernel("mid", held, g, h, {"q": now["q"], "p": now["p"]})
        else:
            state = {"q": now["q"], "p": now["p"], "pos": position, "gap": gap, "keep": keep1}
            now = margins_kernel("last", held, g, h, state)
            final_position = assemble(now["pos"], across(now["pos"]))
            sign, final_position = lax.optimization_barrier((sign, final_position))
            signs = (sign, signs[1])
        g, residual, side = gradient(paired(now["margins"]), residual, last, like if last else None)
    distances, likes = side
    momentum = finish_kernel(g, h, now["p"], now["q"])
    return (final_position, assemble(momentum, across(momentum)), likes, distances)


def solution(mesh):
    return jax.shard_map(
        on_device,
        mesh=mesh,
        in_specs=(
            P("rows", "feat"),
            P("rows"),
            P(None, "feat"),
            P(None, None, "feat"),
            P(),
            P(),
            P(),
        ),
        out_specs=(P(None, "feat"), P(None, "feat"), P(), P()),
        check_vma=False,
    )
```

profile of v0, /device:TPU:1, one launch (start us, length us, event | category | flops | bytes accessed | tf_op | source)
XLA Modules:
  0.0 420.9 jit_solution(15198286829217997372)
XLA Ops:
  0.7 1.4 copy-done.1
  2.0 6.3 %prepare.1 = (f32[16,256]{1,0:T(8,128)S(1)}, bf16[256,8192]{1,0:T(8,128)(2,1)S(1)}, bf16[256,8192]{1,0:T(8,128)(2,1)S(1)}, f32[16,8192]{1,0:T(8,128)S(1)}) custom-call(f32[16,16384]{1,0:T(8,128)S(1)} %copy-done.1, bf16[256,16384]{1,0:T(8,128)(2,1)} %design_ref.1), custom_call_target="tpu_custom_call" | custom-call | flops 134217728 | bytes 8388608 | tf_op jit(solution)/shard_map/prepare/pallas_call | solution.py:31
  8.3 1.5 collective-permute-start
  11.0 1.7 collective-permute-start.2
  12.7 3.3 collective-permute-start.3
  21.0 14.0 %all_to_all.110.refs_0_ = bf16[16,16,512]{2,1,0:T(8,128)(2,1)S(1)} all-to-all(bf16[16,16,512]{2,1,0:T(8,128)(2,1)S(1)} %terms.11), channel_id=1, replica_groups={{0,8,16,24,32,40,48,56,64,72,80,88,96,104,112,120},{4,12,20,28,36,44,52..., dimensions={0} | all-to-all | bytes 524288 | tf_op jit(solution)/shard_map/all_to_all | solution.py:393
  35.1 10.8 %all_to_all.111.arrived_ref.refs_2_ = bf16[16,16,512]{2,1,0:T(8,128)(2,1)S(1)} all-to-all(bf16[16,16,512]{2,1,0:T(8,128)(2,1)S(1)} %get-tuple-element.82), channel_id=1, replica_groups={{0,8,16,24,32,40,48,56,64,72,80,88,96,104,112,120},{4,12,20,28,36,44,52..., dimensions={0} | all-to-all | bytes 524288 | tf_op jit(solution)/shard_map/all_to_all | solution.py:393
  45.9 2.7 margins_first.1
  48.6 3.4 collective-permute-start.6
  53.3 2.7 collective-permute-start.8
  60.3 10.6 %all_to_all.112.refs_0_ = bf16[16,16,512]{2,1,0:T(8,128)(2,1)S(1)} all-to-all(bf16[16,16,512]{2,1,0:T(8,128)(2,1)S(1)} %terms.12), channel_id=1, replica_groups={{0,8,16,24,32,40,48,56,64,72,80,88,96,104,112,120},{4,12,20,28,36,44,52..., dimensions={0} | all-to-all | bytes 524288 | tf_op jit(solution)/shard_map/all_to_all | solution.py:393
  70.9 10.8 %all_to_all.113.arrived_ref = bf16[16,16,512]{2,1,0:T(8,128)(2,1)S(1)} all-to-all(bf16[16,16,512]{2,1,0:T(8,128)(2,1)S(1)} %get-tuple-element.88), channel_id=1, replica_groups={{0,8,16,24,32,40,48,56,64,72,80,88,96,104,112,120},{4,12,20,28,36,44,52..., dimensions={0} | all-to-all | bytes 524288 | tf_op jit(solution)/shard_map/all_to_all | solution.py:393
  81.7 2.7 margins_mid.7
  84.4 4.5 %collective-permute-start.10 = (f32[16,512]{1,0:T(8,128)S(1)}, f32[16,512]{1,0:T(8,128)S(1)}, u32[]{:S(2)}, u32[]{:S(2)}) collective-permute-start(f32[16,512]{1,0:T(8,128)S(1)} %get-tuple-element.91.mine_ref), channel_id=1, source_target_pairs={{0,4},{4,0},{8,12},{12,8},{16,20},{20,16},{24,28},{28,24},{32,36},... | collective-permute-start | bytes 98312 | tf_op jit(solution)/shard_map/ppermute | solution.py:396
  89.8 2.7 collective-permute-start.12
  94.2 1.4 collective-permute-done.13.refs_3_
  97.0 10.6 %all_to_all.114.refs_0_ = bf16[16,16,512]{2,1,0:T(8,128)(2,1)S(1)} all-to-all(bf16[16,16,512]{2,1,0:T(8,128)(2,1)S(1)} %terms.13), channel_id=1, replica_groups={{0,8,16,24,32,40,48,56,64,72,80,88,96,104,112,120},{4,12,20,28,36,44,52..., dimensions={0} | all-to-all | bytes 524288 | tf_op jit(solution)/shard_map/all_to_all | solution.py:393
  107.6 10.8 %all_to_all.115.arrived_ref = bf16[16,16,512]{2,1,0:T(8,128)(2,1)S(1)} all-to-all(bf16[16,16,512]{2,1,0:T(8,128)(2,1)S(1)} %get-tuple-element.93), channel_id=1, replica_groups={{0,8,16,24,32,40,48,56,64,72,80,88,96,104,112,120},{4,12,20,28,36,44,52..., dimensions={0} | all-to-all | bytes 524288 | tf_op jit(solution)/shard_map/all_to_all | solution.py:393
  118.4 2.7 margins_mid.8
  121.1 4.3 %collective-permute-start.14 = (f32[16,512]{1,0:T(8,128)S(1)}, f32[16,512]{1,0:T(8,128)S(1)}, u32[]{:S(2)}, u32[]{:S(2)}) collective-permute-start(f32[16,512]{1,0:T(8,128)S(1)} %get-tuple-element.96.mine_ref), channel_id=1, source_target_pairs={{0,4},{4,0},{8,12},{12,8},{16,20},{20,16},{24,28},{28,24},{32,36},... | collective-permute-start | bytes 98312 | tf_op jit(solution)/shard_map/ppermute | solution.py:396
  126.6 2.5 collective-permute-start.16
  133.6 10.5 %all_to_all.116.refs_0_ = bf16[16,16,512]{2,1,0:T(8,128)(2,1)S(1)} all-to-all(bf16[16,16,512]{2,1,0:T(8,128)(2,1)S(1)} %terms.14), channel_id=1, replica_groups={{0,8,16,24,32,40,48,56,64,72,80,88,96,104,112,120},{4,12,20,28,36,44,52..., dimensions={0} | all-to-all | bytes 524288 | tf_op jit(solution)/shard_map/all_to_all | solution.py:393
  144.2 10.8 %all_to_all.117.arrived_ref = bf16[16,16,512]{2,1,0:T(8,128)(2,1)S(1)} all-to-all(bf16[16,16,512]{2,1,0:T(8,128)(2,1)S(1)} %get-tuple-element.98), channel_id=1, replica_groups={{0,8,16,24,32,40,48,56,64,72,80,88,96,104,112,120},{4,12,20,28,36,44,52..., dimensions={0} | all-to-all | bytes 524288 | tf_op jit(solution)/shard_map/all_to_all | solution.py:393
  155.0 2.7 margins_mid.9
  157.7 4.2 %collective-permute-start.18 = (f32[16,512]{1,0:T(8,128)S(1)}, f32[16,512]{1,0:T(8,128)S(1)}, u32[]{:S(2)}, u32[]{:S(2)}) collective-permute-start(f32[16,512]{1,0:T(8,128)S(1)} %get-tuple-element.101.mine_ref), channel_id=1, source_target_pairs={{0,4},{4,0},{8,12},{12,8},{16,20},{20,16},{24,28},{28,24},{32,36},... | collective-permute-start | bytes 98312 | tf_op jit(solution)/shard_map/ppermute | solution.py:396
  163.2 2.5 collective-permute-start.20
  170.2 10.5 %all_to_all.118.refs_0_ = bf16[16,16,512]{2,1,0:T(8,128)(2,1)S(1)} all-to-all(bf16[16,16,512]{2,1,0:T(8,128)(2,1)S(1)} %terms.15), channel_id=1, replica_groups={{0,8,16,24,32,40,48,56,64,72,80,88,96,104,112,120},{4,12,20,28,36,44,52..., dimensions={0} | all-to-all | bytes 524288 | tf_op jit(solution)/shard_map/all_to_all | solution.py:393
  180.8 10.8 %all_to_all.119.arrived_ref = bf16[16,16,512]{2,1,0:T(8,128)(2,1)S(1)} all-to-all(bf16[16,16,512]{2,1,0:T(8,128)(2,1)S(1)} %get-tuple-element.103), channel_id=1, replica_groups={{0,8,16,24,32,40,48,56,64,72,80,88,96,104,112,120},{4,12,20,28,36,44,52..., dimensions={0} | all-to-all | bytes 524288 | tf_op jit(solution)/shard_map/all_to_all | solution.py:393
  191.6 3.3 margins_mid.10
  194.9 4.2 %collective-permute-start.22 = (f32[16,512]{1,0:T(8,128)S(1)}, f32[16,512]{1,0:T(8,128)S(1)}, u32[]{:S(2)}, u32[]{:S(2)}) collective-permute-start(f32[16,512]{1,0:T(8,128)S(1)} %get-tuple-element.106.mine_ref), channel_id=1, source_target_pairs={{0,4},{4,0},{8,12},{12,8},{16,20},{20,16},{24,28},{28,24},{32,36},... | collective-permute-start | bytes 98312 | tf_op jit(solution)/shard_map/ppermute | solution.py:396
  200.4 2.5 collective-permute-start.24
  204.7 1.4 collective-permute-done.25.refs_3_
  206.1 1.4 terms.16
  207.5 10.5 %all_to_all.120.refs_0_ = bf16[16,16,512]{2,1,0:T(8,128)(2,1)S(1)} all-to-all(bf16[16,16,512]{2,1,0:T(8,128)(2,1)S(1)} %get-tuple-element.107), channel_id=1, replica_groups={{0,8,16,24,32,40,48,56,64,72,80,88,96,104,112,120},{4,12,20,28,36,44,52..., dimensions={0} | all-to-all | bytes 524288 | tf_op jit(solution)/shard_map/all_to_all | solution.py:393
  218.1 10.8 %all_to_all.121.arrived_ref = bf16[16,16,512]{2,1,0:T(8,128)(2,1)S(1)} all-to-all(bf16[16,16,512]{2,1,0:T(8,128)(2,1)S(1)} %get-tuple-element.109), channel_id=1, replica_groups={{0,8,16,24,32,40,48,56,64,72,80,88,96,104,112,120},{4,12,20,28,36,44,52..., dimensions={0} | all-to-all | bytes 524288 | tf_op jit(solution)/shard_map/all_to_all | solution.py:393
  228.9 2.7 margins_turn.1
  231.6 4.2 %collective-permute-start.26 = (f32[16,512]{1,0:T(8,128)S(1)}, f32[16,512]{1,0:T(8,128)S(1)}, u32[]{:S(2)}, u32[]{:S(2)}) collective-permute-start(f32[16,512]{1,0:T(8,128)S(1)} %get-tuple-element.113.mine_ref), channel_id=1, source_target_pairs={{0,4},{4,0},{8,12},{12,8},{16,20},{20,16},{24,28},{28,24},{32,36},... | collective-permute-start | bytes 98312 | tf_op jit(solution)/shard_map/ppermute | solution.py:396
  237.1 2.5 collective-permute-start.28
  244.0 10.5 %all_to_all.122.refs_0_ = bf16[16,16,512]{2,1,0:T(8,128)(2,1)S(1)} all-to-all(bf16[16,16,512]{2,1,0:T(8,128)(2,1)S(1)} %terms.17), channel_id=1, replica_groups={{0,8,16,24,32,40,48,56,64,72,80,88,96,104,112,120},{4,12,20,28,36,44,52..., dimensions={0} | all-to-all | bytes 524288 | tf_op jit(solution)/shard_map/all_to_all | solution.py:393
  254.6 10.8 %all_to_all.123.arrived_ref = bf16[16,16,512]{2,1,0:T(8,128)(2,1)S(1)} all-to-all(bf16[16,16,512]{2,1,0:T(8,128)(2,1)S(1)} %get-tuple-element.115), channel_id=1, replica_groups={{0,8,16,24,32,40,48,56,64,72,80,88,96,104,112,120},{4,12,20,28,36,44,52..., dimensions={0} | all-to-all | bytes 524288 | tf_op jit(solution)/shard_map/all_to_all | solution.py:393
  265.4 2.7 margins_mid.11
  268.1 4.2 %collective-permute-start.30 = (f32[16,512]{1,0:T(8,128)S(1)}, f32[16,512]{1,0:T(8,128)S(1)}, u32[]{:S(2)}, u32[]{:S(2)}) collective-permute-start(f32[16,512]{1,0:T(8,128)S(1)} %get-tuple-element.118.mine_ref), channel_id=1, source_target_pairs={{0,4},{4,0},{8,12},{12,8},{16,20},{20,16},{24,28},{28,24},{32,36},... | collective-permute-start | bytes 98312 | tf_op jit(solution)/shard_map/ppermute | solution.py:396
  273.6 2.5 collective-permute-start.32
  280.6 10.5 %all_to_all.124.refs_0_ = bf16[16,16,512]{2,1,0:T(8,128)(2,1)S(1)} all-to-all(bf16[16,16,512]{2,1,0:T(8,128)(2,1)S(1)} %terms.18), channel_id=1, replica_groups={{0,8,16,24,32,40,48,56,64,72,80,88,96,104,112,120},{4,12,20,28,36,44,52..., dimensions={0} | all-to-all | bytes 524288 | tf_op jit(solution)/shard_map/all_to_all | solution.py:393
  291.2 10.8 %all_to_all.125.arrived_ref = bf16[16,16,512]{2,1,0:T(8,128)(2,1)S(1)} all-to-all(bf16[16,16,512]{2,1,0:T(8,128)(2,1)S(1)} %get-tuple-element.120), channel_id=1, replica_groups={{0,8,16,24,32,40,48,56,64,72,80,88,96,104,112,120},{4,12,20,28,36,44,52..., dimensions={0} | all-to-all | bytes 524288 | tf_op jit(solution)/shard_map/all_to_all | solution.py:393
  302.0 2.7 margins_mid.12
  304.7 4.2 %collective-permute-start.34 = (f32[16,512]{1,0:T(8,128)S(1)}, f32[16,512]{1,0:T(8,128)S(1)}, u32[]{:S(2)}, u32[]{:S(2)}) collective-permute-start(f32[16,512]{1,0:T(8,128)S(1)} %get-tuple-element.123.mine_ref), channel_id=1, source_target_pairs={{0,4},{4,0},{8,12},{12,8},{16,20},{20,16},{24,28},{28,24},{32,36},... | collective-permute-start | bytes 98312 | tf_op jit(solution)/shard_map/ppermute | solution.py:396
  310.2 2.5 collective-permute-start.36
  317.2 10.5 %all_to_all.126.refs_0_ = bf16[16,16,512]{2,1,0:T(8,128)(2,1)S(1)} all-to-all(bf16[16,16,512]{2,1,0:T(8,128)(2,1)S(1)} %terms.19), channel_id=1, replica_groups={{0,8,16,24,32,40,48,56,64,72,80,88,96,104,112,120},{4,12,20,28,36,44,52..., dimensions={0} | all-to-all | bytes 524288 | tf_op jit(solution)/shard_map/all_to_all | solution.py:393
  327.7 10.8 %all_to_all.127.arrived_ref = bf16[16,16,512]{2,1,0:T(8,128)(2,1)S(1)} all-to-all(bf16[16,16,512]{2,1,0:T(8,128)(2,1)S(1)} %get-tuple-element.125), channel_id=1, replica_groups={{0,8,16,24,32,40,48,56,64,72,80,88,96,104,112,120},{4,12,20,28,36,44,52..., dimensions={0} | all-to-all | bytes 524288 | tf_op jit(solution)/shard_map/all_to_all | solution.py:393
  338.5 2.7 margins_mid.13
  341.2 4.2 %collective-permute-start.38 = (f32[16,512]{1,0:T(8,128)S(1)}, f32[16,512]{1,0:T(8,128)S(1)}, u32[]{:S(2)}, u32[]{:S(2)}) collective-permute-start(f32[16,512]{1,0:T(8,128)S(1)} %get-tuple-element.128.mine_ref), channel_id=1, source_target_pairs={{0,4},{4,0},{8,12},{12,8},{16,20},{20,16},{24,28},{28,24},{32,36},... | collective-permute-start | bytes 98312 | tf_op jit(solution)/shard_map/ppermute | solution.py:396
  346.7 2.5 collective-permute-start.40
  353.7 10.5 %all_to_all.128.refs_0_ = bf16[16,16,512]{2,1,0:T(8,128)(2,1)S(1)} all-to-all(bf16[16,16,512]{2,1,0:T(8,128)(2,1)S(1)} %terms.20), channel_id=1, replica_groups={{0,8,16,24,32,40,48,56,64,72,80,88,96,104,112,120},{4,12,20,28,36,44,52..., dimensions={0} | all-to-all | bytes 524288 | tf_op jit(solution)/shard_map/all_to_all | solution.py:393
  364.3 10.8 %all_to_all.129.arrived_ref = bf16[16,16,512]{2,1,0:T(8,128)(2,1)S(1)} all-to-all(bf16[16,16,512]{2,1,0:T(8,128)(2,1)S(1)} %get-tuple-element.130), channel_id=1, replica_groups={{0,8,16,24,32,40,48,56,64,72,80,88,96,104,112,120},{4,12,20,28,36,44,52..., dimensions={0} | all-to-all | bytes 524288 | tf_op jit(solution)/shard_map/all_to_all | solution.py:393
  375.1 2.7 margins_last.1
  377.8 4.2 %collective-permute-start.42 = (f32[16,8192]{1,0:T(8,128)S(1)}, f32[16,8192]{1,0:T(8,128)S(1)}, u32[]{:S(2)}, u32[]{:S(2)}) collective-permute-start(f32[16,8192]{1,0:T(8,128)S(1)} %get-tuple-element.136.mine_ref), channel_id=1, source_target_pairs={{0,4},{4,0},{8,12},{12,8},{16,20},{20,16},{24,28},{28,24},{32,36},... | collective-permute-start | bytes 1572872 | tf_op jit(solution)/shard_map/ppermute | solution.py:396
  382.2 1.5 collective-permute-done.43.other_ref
  384.1 2.5 collective-permute-start.45
  389.8 1.6 terms.21
  391.4 10.9 %all_to_all.130.refs_0_ = bf16[16,16,640]{2,1,0:T(8,128)(2,1)S(1)} all-to-all(bf16[16,16,640]{2,1,0:T(8,128)(2,1)S(1)} %get-tuple-element.141), channel_id=1, replica_groups={{0,8,16,24,32,40,48,56,64,72,80,88,96,104,112,120},{4,12,20,28,36,44,52..., dimensions={0} | all-to-all | bytes 655360 | tf_op jit(solution)/shard_map/all_to_all | solution.py:393
  403.0 10.8 %all_to_all.131.arrived_ref = bf16[16,16,512]{2,1,0:T(8,128)(2,1)S(1)} all-to-all(bf16[16,16,512]{2,1,0:T(8,128)(2,1)S(1)} %get-tuple-element.143), channel_id=1, replica_groups={{0,8,16,24,32,40,48,56,64,72,80,88,96,104,112,120},{4,12,20,28,36,44,52..., dimensions={0} | all-to-all | bytes 524288 | tf_op jit(solution)/shard_map/all_to_all | solution.py:393
  413.9 4.3 %collective-permute-start.47 = (f32[16,8192]{1,0:T(8,128)S(1)}, f32[16,8192]{1,0:T(8,128)S(1)}, u32[]{:S(2)}, u32[]{:S(2)}) collective-permute-start(f32[16,8192]{1,0:T(8,128)S(1)} %finish.1.mine_ref), channel_id=1, source_target_pairs={{0,4},{4,0},{8,12},{12,8},{16,20},{20,16},{24,28},{28,24},{32,36},... | collective-permute-start | bytes 1572872 | tf_op jit(solution)/shard_map/ppermute | solution.py:396
  418.2 1.5 collective-permute-done.47.other_ref
  (114 shorter events, 59.3 us)
Async XLA Ops:
  0.6 16.1 %copy-start = (f32[8,4,16384]{2,1,0:T(4,128)S(1)}, f32[8,4,16384]{2,1,0:T(4,128)}, u32[]{:S(2)}) copy-start(f32[8,4,16384]{2,1,0:T(4,128)} %bank_ref.1) | copy-start | bytes 6291460
  0.6 1.4 copy-start.1
  2.0 14.7 %copy-start.2 = (s32[2,16]{1,0:T(2,128)S(1)}, s32[2,16]{1,0:T(2,128)}, u32[]{:S(2)}) copy-start(s32[2,16]{1,0:T(2,128)} %accept_ref.1) | copy-start | bytes 388
  2.0 14.7 %copy-start.3 = (s32[256]{0:T(256)S(1)}, s32[256]{0:T(256)}, u32[]{:S(2)}) copy-start(s32[256]{0:T(256)} %param.8) | copy-start | bytes 3076
  2.0 14.7 %copy-start.4 = (s32[8]{0:T(128)S(1)}, s32[8]{0:T(128)}, u32[]{:S(2)}) copy-start(s32[8]{0:T(128)} %lag_ref.1) | copy-start | bytes 100
  2.0 14.7 %copy-start.5 = (f32[8]{0:T(128)S(1)}, f32[8]{0:T(128)}, u32[]{:S(2)}) copy-start(f32[8]{0:T(128)} %steps_ref.1) | copy-start | bytes 100
  8.3 2.3 collective-permute-start
  10.6 9.0 %collective-permute-start.1 = (bf16[256,8192]{1,0:T(8,128)(2,1)S(1)}, bf16[256,8192]{1,0:T(8,128)(2,1)S(1)}, u32[]{:S(2)}, u32[]{:S(2)}) collective-permute-start(bf16[256,8192]{1,0:T(8,128)(2,1)S(1)} %get-tuple-element.80), channel_id=1, source_target_pairs={{0,4},{4,0},{8,12},{12,8},{16,20},{20,16},{24,28},{28,24},{32,36},... | collective-permute-start | bytes 12582920 | tf_op jit(solution)/shard_map/ppermute | solution.py:396
  11.0 8.7 %collective-permute-start.2 = (f32[16,512]{1,0:T(8,128)S(1)}, f32[16,512]{1,0:T(8,128)S(1)}, u32[]{:S(2)}, u32[]{:S(2)}) collective-permute-start(f32[16,512]{1,0:T(8,128)S(1)} %pair_start.1.refs_0_), channel_id=1, source_target_pairs={{0,1},{1,2},{2,3},{3,0},{4,5},{5,6},{6,7},{7,4},{8,9},{9,10},{10,1... | collective-permute-start | bytes 98312 | tf_op jit(solution)/shard_map/ppermute | solution.py:400
  12.7 6.9 %collective-permute-start.3 = (f32[16,512]{1,0:T(8,128)S(1)}, f32[16,512]{1,0:T(8,128)S(1)}, u32[]{:S(2)}, u32[]{:S(2)}) collective-permute-start(f32[16,512]{1,0:T(8,128)S(1)} %pair_start.1.refs_0_), channel_id=1, source_target_pairs={{0,2},{1,3},{2,0},{3,1},{4,6},{5,7},{6,4},{7,5},{8,10},{9,11},{10,... | collective-permute-start | bytes 98312 | tf_op jit(solution)/shard_map/ppermute | solution.py:400
  16.0 3.6 collective-permute-start.4
  17.7 1.9 collective-permute-start.5
  48.6 4.3 %collective-permute-start.6 = (f32[16,512]{1,0:T(8,128)S(1)}, f32[16,512]{1,0:T(8,128)S(1)}, u32[]{:S(2)}, u32[]{:S(2)}) collective-permute-start(f32[16,512]{1,0:T(8,128)S(1)} %get-tuple-element.86.mine_ref), channel_id=1, source_target_pairs={{0,4},{4,0},{8,12},{12,8},{16,20},{20,16},{24,28},{28,24},{32,36},... | collective-permute-start | bytes 98312 | tf_op jit(solution)/shard_map/ppermute | solution.py:396
  52.9 4.0 collective-permute-start.7
  53.3 4.4 %collective-permute-start.8 = (f32[16,512]{1,0:T(8,128)S(1)}, f32[16,512]{1,0:T(8,128)S(1)}, u32[]{:S(2)}, u32[]{:S(2)}) collective-permute-start(f32[16,512]{1,0:T(8,128)S(1)} %pair_sum.10.refs_0_), channel_id=1, source_target_pairs={{0,2},{1,3},{2,0},{3,1},{4,6},{5,7},{6,4},{7,5},{8,10},{9,11},{10,... | collective-permute-start | bytes 98312 | tf_op jit(solution)/shard_map/ppermute | solution.py:400
  56.0 2.9 collective-permute-start.9
  84.4 5.3 %collective-permute-start.10 = (f32[16,512]{1,0:T(8,128)S(1)}, f32[16,512]{1,0:T(8,128)S(1)}, u32[]{:S(2)}, u32[]{:S(2)}) collective-permute-start(f32[16,512]{1,0:T(8,128)S(1)} %get-tuple-element.91.mine_ref), channel_id=1, source_target_pairs={{0,4},{4,0},{8,12},{12,8},{16,20},{20,16},{24,28},{28,24},{32,36},... | collective-permute-start | bytes 98312 | tf_op jit(solution)/shard_map/ppermute | solution.py:396
  89.7 4.0 collective-permute-start.11
  89.8 4.4 %collective-permute-start.12 = (f32[16,512]{1,0:T(8,128)S(1)}, f32[16,512]{1,0:T(8,128)S(1)}, u32[]{:S(2)}, u32[]{:S(2)}) collective-permute-start(f32[16,512]{1,0:T(8,128)S(1)} %pair_sum.11.refs_0_), channel_id=1, source_target_pairs={{0,2},{1,3},{2,0},{3,1},{4,6},{5,7},{6,4},{7,5},{8,10},{9,11},{10,... | collective-permute-start | bytes 98312 | tf_op jit(solution)/shard_map/ppermute | solution.py:400
  92.6 3.1 collective-permute-start.13
  121.1 5.2 %collective-permute-start.14 = (f32[16,512]{1,0:T(8,128)S(1)}, f32[16,512]{1,0:T(8,128)S(1)}, u32[]{:S(2)}, u32[]{:S(2)}) collective-permute-start(f32[16,512]{1,0:T(8,128)S(1)} %get-tuple-element.96.mine_ref), channel_id=1, source_target_pairs={{0,4},{4,0},{8,12},{12,8},{16,20},{20,16},{24,28},{28,24},{32,36},... | collective-permute-start | bytes 98312 | tf_op jit(solution)/shard_map/ppermute | solution.py:396
  126.3 4.0 collective-permute-start.15
  126.6 4.3 %collective-permute-start.16 = (f32[16,512]{1,0:T(8,128)S(1)}, f32[16,512]{1,0:T(8,128)S(1)}, u32[]{:S(2)}, u32[]{:S(2)}) collective-permute-start(f32[16,512]{1,0:T(8,128)S(1)} %pair_sum.12.refs_0_), channel_id=1, source_target_pairs={{0,2},{1,3},{2,0},{3,1},{4,6},{5,7},{6,4},{7,5},{8,10},{9,11},{10,... | collective-permute-start | bytes 98312 | tf_op jit(solution)/shard_map/ppermute | solution.py:400
  129.1 3.2 collective-permute-start.17
  157.7 5.1 %collective-permute-start.18 = (f32[16,512]{1,0:T(8,128)S(1)}, f32[16,512]{1,0:T(8,128)S(1)}, u32[]{:S(2)}, u32[]{:S(2)}) collective-permute-start(f32[16,512]{1,0:T(8,128)S(1)} %get-tuple-element.101.mine_ref), channel_id=1, source_target_pairs={{0,4},{4,0},{8,12},{12,8},{16,20},{20,16},{24,28},{28,24},{32,36},... | collective-permute-start | bytes 98312 | tf_op jit(solution)/shard_map/ppermute | solution.py:396
  162.8 4.0 collective-permute-start.19
  163.2 4.3 %collective-permute-start.20 = (f32[16,512]{1,0:T(8,128)S(1)}, f32[16,512]{1,0:T(8,128)S(1)}, u32[]{:S(2)}, u32[]{:S(2)}) collective-permute-start(f32[16,512]{1,0:T(8,128)S(1)} %pair_sum.13.refs_0_), channel_id=1, source_target_pairs={{0,2},{1,3},{2,0},{3,1},{4,6},{5,7},{6,4},{7,5},{8,10},{9,11},{10,... | collective-permute-start | bytes 98312 | tf_op jit(solution)/shard_map/ppermute | solution.py:400
  165.7 3.2 collective-permute-start.21
  194.9 5.1 %collective-permute-start.22 = (f32[16,512]{1,0:T(8,128)S(1)}, f32[16,512]{1,0:T(8,128)S(1)}, u32[]{:S(2)}, u32[]{:S(2)}) collective-permute-start(f32[16,512]{1,0:T(8,128)S(1)} %get-tuple-element.106.mine_ref), channel_id=1, source_target_pairs={{0,4},{4,0},{8,12},{12,8},{16,20},{20,16},{24,28},{28,24},{32,36},... | collective-permute-start | bytes 98312 | tf_op jit(solution)/shard_map/ppermute | solution.py:396
  200.0 4.0 collective-permute-start.23
  200.4 4.3 %collective-permute-start.24 = (f32[16,512]{1,0:T(8,128)S(1)}, f32[16,512]{1,0:T(8,128)S(1)}, u32[]{:S(2)}, u32[]{:S(2)}) collective-permute-start(f32[16,512]{1,0:T(8,128)S(1)} %pair_sum.14.refs_0_), channel_id=1, source_target_pairs={{0,2},{1,3},{2,0},{3,1},{4,6},{5,7},{6,4},{7,5},{8,10},{9,11},{10,... | collective-permute-start | bytes 98312 | tf_op jit(solution)/shard_map/ppermute | solution.py:400
  202.9 3.2 collective-permute-start.25
  231.6 5.1 %collective-permute-start.26 = (f32[16,512]{1,0:T(8,128)S(1)}, f32[16,512]{1,0:T(8,128)S(1)}, u32[]{:S(2)}, u32[]{:S(2)}) collective-permute-start(f32[16,512]{1,0:T(8,128)S(1)} %get-tuple-element.113.mine_ref), channel_id=1, source_target_pairs={{0,4},{4,0},{8,12},{12,8},{16,20},{20,16},{24,28},{28,24},{32,36},... | collective-permute-start | bytes 98312 | tf_op jit(solution)/shard_map/ppermute | solution.py:396
  236.7 4.0 collective-permute-start.27
  237.1 4.3 %collective-permute-start.28 = (f32[16,512]{1,0:T(8,128)S(1)}, f32[16,512]{1,0:T(8,128)S(1)}, u32[]{:S(2)}, u32[]{:S(2)}) collective-permute-start(f32[16,512]{1,0:T(8,128)S(1)} %pair_sum.15.refs_0_), channel_id=1, source_target_pairs={{0,2},{1,3},{2,0},{3,1},{4,6},{5,7},{6,4},{7,5},{8,10},{9,11},{10,... | collective-permute-start | bytes 98312 | tf_op jit(solution)/shard_map/ppermute | solution.py:400
  239.5 3.2 collective-permute-start.29
  268.1 5.1 %collective-permute-start.30 = (f32[16,512]{1,0:T(8,128)S(1)}, f32[16,512]{1,0:T(8,128)S(1)}, u32[]{:S(2)}, u32[]{:S(2)}) collective-permute-start(f32[16,512]{1,0:T(8,128)S(1)} %get-tuple-element.118.mine_ref), channel_id=1, source_target_pairs={{0,4},{4,0},{8,12},{12,8},{16,20},{20,16},{24,28},{28,24},{32,36},... | collective-permute-start | bytes 98312 | tf_op jit(solution)/shard_map/ppermute | solution.py:396
  273.2 4.0 collective-permute-start.31
  273.6 4.3 %collective-permute-start.32 = (f32[16,512]{1,0:T(8,128)S(1)}, f32[16,512]{1,0:T(8,128)S(1)}, u32[]{:S(2)}, u32[]{:S(2)}) collective-permute-start(f32[16,512]{1,0:T(8,128)S(1)} %pair_sum.16.refs_0_), channel_id=1, source_target_pairs={{0,2},{1,3},{2,0},{3,1},{4,6},{5,7},{6,4},{7,5},{8,10},{9,11},{10,... | collective-permute-start | bytes 98312 | tf_op jit(solution)/shard_map/ppermute | solution.py:400
  276.1 3.2 collective-permute-start.33
  304.7 5.1 %collective-permute-start.34 = (f32[16,512]{1,0:T(8,128)S(1)}, f32[16,512]{1,0:T(8,128)S(1)}, u32[]{:S(2)}, u32[]{:S(2)}) collective-permute-start(f32[16,512]{1,0:T(8,128)S(1)} %get-tuple-element.123.mine_ref), channel_id=1, source_target_pairs={{0,4},{4,0},{8,12},{12,8},{16,20},{20,16},{24,28},{28,24},{32,36},... | collective-permute-start | bytes 98312 | tf_op jit(solution)/shard_map/ppermute | solution.py:396
  309.8 4.0 collective-permute-start.35
  310.2 4.3 %collective-permute-start.36 = (f32[16,512]{1,0:T(8,128)S(1)}, f32[16,512]{1,0:T(8,128)S(1)}, u32[]{:S(2)}, u32[]{:S(2)}) collective-permute-start(f32[16,512]{1,0:T(8,128)S(1)} %pair_sum.17.refs_0_), channel_id=1, source_target_pairs={{0,2},{1,3},{2,0},{3,1},{4,6},{5,7},{6,4},{7,5},{8,10},{9,11},{10,... | collective-permute-start | bytes 98312 | tf_op jit(solution)/shard_map/ppermute | solution.py:400
  312.7 3.2 collective-permute-start.37
  341.2 5.1 %collective-permute-start.38 = (f32[16,512]{1,0:T(8,128)S(1)}, f32[16,512]{1,0:T(8,128)S(1)}, u32[]{:S(2)}, u32[]{:S(2)}) collective-permute-start(f32[16,512]{1,0:T(8,128)S(1)} %get-tuple-element.128.mine_ref), channel_id=1, source_target_pairs={{0,4},{4,0},{8,12},{12,8},{16,20},{20,16},{24,28},{28,24},{32,36},... | collective-permute-start | bytes 98312 | tf_op jit(solution)/shard_map/ppermute | solution.py:396
  346.3 4.0 collective-permute-start.39
  346.7 4.3 %collective-permute-start.40 = (f32[16,512]{1,0:T(8,128)S(1)}, f32[16,512]{1,0:T(8,128)S(1)}, u32[]{:S(2)}, u32[]{:S(2)}) collective-permute-start(f32[16,512]{1,0:T(8,128)S(1)} %pair_sum.18.refs_0_), channel_id=1, source_target_pairs={{0,2},{1,3},{2,0},{3,1},{4,6},{5,7},{6,4},{7,5},{8,10},{9,11},{10,... | collective-permute-start | bytes 98312 | tf_op jit(solution)/shard_map/ppermute | solution.py:400
  349.2 3.2 collective-permute-start.41
  377.8 9.1 %collective-permute-start.42 = (f32[16,8192]{1,0:T(8,128)S(1)}, f32[16,8192]{1,0:T(8,128)S(1)}, u32[]{:S(2)}, u32[]{:S(2)}) collective-permute-start(f32[16,8192]{1,0:T(8,128)S(1)} %get-tuple-element.136.mine_ref), channel_id=1, source_target_pairs={{0,4},{4,0},{8,12},{12,8},{16,20},{20,16},{24,28},{28,24},{32,36},... | collective-permute-start | bytes 1572872 | tf_op jit(solution)/shard_map/ppermute | solution.py:396
  382.1 1.6 collective-permute-start.43
  383.7 4.3 %collective-permute-start.44 = (f32[16,640]{1,0:T(8,128)S(1)}, f32[16,640]{1,0:T(8,128)S(1)}, u32[]{:S(2)}, u32[]{:S(2)}) collective-permute-start(f32[16,640]{1,0:T(8,128)S(1)} %pair_sum.19.refs_0_), channel_id=1, source_target_pairs={{0,1},{1,2},{2,3},{3,0},{4,5},{5,6},{6,7},{7,4},{8,9},{9,10},{10,1... | collective-permute-start | bytes 122888 | tf_op jit(solution)/shard_map/ppermute | solution.py:400
  384.1 4.4 %collective-permute-start.45 = (f32[16,640]{1,0:T(8,128)S(1)}, f32[16,640]{1,0:T(8,128)S(1)}, u32[]{:S(2)}, u32[]{:S(2)}) collective-permute-start(f32[16,640]{1,0:T(8,128)S(1)} %pair_sum.19.refs_0_), channel_id=1, source_target_pairs={{0,2},{1,3},{2,0},{3,1},{4,6},{5,7},{6,4},{7,5},{8,10},{9,11},{10,... | collective-permute-start | bytes 122888 | tf_op jit(solution)/shard_map/ppermute | solution.py:400
  386.5 3.3 collective-permute-start.46
  413.9 5.8 %collective-permute-start.47 = (f32[16,8192]{1,0:T(8,128)S(1)}, f32[16,8192]{1,0:T(8,128)S(1)}, u32[]{:S(2)}, u32[]{:S(2)}) collective-permute-start(f32[16,8192]{1,0:T(8,128)S(1)} %finish.1.mine_ref), channel_id=1, source_target_pairs={{0,4},{4,0},{8,12},{12,8},{16,20},{20,16},{24,28},{28,24},{32,36},... | collective-permute-start | bytes 1572872 | tf_op jit(solution)/shard_map/ppermute | solution.py:396
where the time goes:
time: 422 us; the launch traced here: 421 us
  blocking collectives  238 us (56%)
  starting transfers between devices  88.2 us (21%)
  Pallas kernels  53.3 us (13%)
  waiting for transfers between devices  38.6 us (9%)
    all_to_all x22, blocking collectives, exchange(): return lax.all_to_all(blocked, 'rows', 0, 0, axis_index_groups=chips)  238 us
    pallas_call x46, Pallas kernels, call(): pl.pallas_call(body, in_specs=[spec for _, spec in ins], out_specs=[VMEM]...  51.4 us
    ppermute x15, starting transfers between devices, across(): return lax.ppermute(value, 'rows', swap)  49.1 us
    ppermute x33, starting transfers between devices, around(): lax.ppermute(margins, 'feat', [(i, (i + k) % ring) for i in range(ring)])  39.1 us
    ppermute x33, waiting for transfers between devices, around(): lax.ppermute(margins, 'feat', [(i, (i + k) % ring) for i in range(ring)])  26.1 us
    ppermute x15, waiting for transfers between devices, across(): return lax.ppermute(value, 'rows', swap)  12.5 us
  transfers between devices with their start and end apart: 48, of which 42 were waited for; matrix products, arithmetic and copies ran while one was open for 0% of the time, Pallas kernels for 0%

commit v1 on v0

--- a/solution.py
+++ b/solution.py
@@ -4,6 +4,7 @@
 from jax.experimental import pallas as pl
 from jax.experimental.pallas import tpu as pltpu
 from jax.sharding import PartitionSpec as P
+
 
 FEATURES = 65536
 TRANS = 2
@@ -14,6 +15,7 @@
 CHUNKS = 4
 GROUP = 4
 WIDE = 8
+AHEAD = 3
 
 F32 = jnp.float32
 BF16 = jnp.bfloat16
@@ -27,7 +29,7 @@
     return pltpu.CompilerParams(vmem_limit_bytes=mib * 1024 * 1024)
 
 
-def call(body, name, ins, outs, scratch=(), flops=0, mib=6):
+def call(body, ins, outs, scratch=(), flops=0, mib=6):
     return pl.pallas_call(
         body,
         in_specs=[spec for _, spec in ins],
@@ -36,7 +38,6 @@
         scratch_shapes=list(scratch),
         compiler_params=limit(mib),
         cost_estimate=pl.CostEstimate(flops=flops, bytes_accessed=flops // 16, transcendentals=0),
-        name=name,
     )(*[a for a, _ in ins])
 
 
@@ -72,16 +73,16 @@
         for offset, target, coefs in ((far, away_ref, far_ref), (near, own_ref, q_ref)):
             for i in range(CHUNKS):
                 here = slice(i * step, (i + 1) * step)
-                copy = fetch(
-                    design_ref.at[:, cols(offset + i * step, step)],
-                    target.at[:, pl.ds(i * step, step)],
-                )
-                pieces.append((copy, target, coefs, here))
+                source = design_ref.at[:, cols(offset + i * step, step)]
+                pieces.append((source, target.at[:, pl.ds(i * step, step)], target, coefs, here))
+        flying = [fetch(*piece[:2]) for piece in pieces[:AHEAD]]
         for copy in first:
             copy.wait()
         total = jnp.zeros((CHAINS, rows), F32)
-        for copy, target, coefs, here in pieces:
-            copy.wait()
+        for i, (_, _, target, coefs, here) in enumerate(pieces):
+            flying[i].wait()
+            if i + AHEAD < len(pieces):
+                flying.append(fetch(*pieces[i + AHEAD][:2]))
             total = total + lax.dot_general(
                 coefs[:, here].astype(BF16), target[:, here], CROSS, preferred_element_type=F32
             )
@@ -90,7 +91,6 @@
     piece = ((rows, half), design.dtype)
     return call(
         body,
-        "prepare",
         [(start, HBM), (design, HBM)],
         [((CHAINS, rows), F32), piece, piece, ((CHAINS, half), F32)],
         [pltpu.VMEM((CHAINS, half), F32), pltpu.SemaphoreType.DMA((2 + 2 * CHUNKS,))],
@@ -131,7 +131,6 @@
     state = ((CHAINS, half), F32)
     return call(
         body,
-        "draw",
         [
             (lag_offsets, SMEM),
             (accept_bits, SMEM),
@@ -146,6 +145,21 @@
     )
 
 
+def flip(piece):
+    rows, width = piece.shape
+    step = 512
+
+    def body(piece_ref, out_ref):
+        def one(i, carry):
+            cols = pl.ds(pl.multiple_of(i * step, step), step)
+            out_ref[cols] = piece_ref[:, cols].T
+            return carry
+
+        lax.fori_loop(0, width // step, one, 0)
+
+    return call(body, vmem(piece), [((width, rows), piece.dtype)])[0]
+
+
 def pair_start(mine, other):
     rows = mine.shape[1]
 
@@ -153,7 +167,7 @@
         margins_ref[:, :rows] = mine_ref[...]
         margins_ref[:, rows:] = other_ref[...]
 
-    return call(body, "pair_start", vmem(mine, other), [((CHAINS, 2 * rows), F32)])[0]
+    return call(body, vmem(mine, other), [((CHAINS, 2 * rows), F32)])[0]
 
 
 def pair_sum(mine, other, rows):
@@ -163,7 +177,7 @@
         if mine.shape[1] > 2 * rows:
             out_ref[:, 2 * rows :] = mine_ref[:, 2 * rows :] + other_ref[:, 2 * rows :]
 
-    return call(body, "pair_sum", vmem(mine, other), [(mine.shape, F32)])[0]
+    return call(body, vmem(mine, other), [(mine.shape, F32)])[0]
 
 
 def assemble(mine, other):
@@ -195,8 +209,8 @@
     return jnp.sum(gap * gap, axis=1, keepdims=True)
 
 
-def margins_kernel(mode, held, arrived, h, state):
-    rows, width = held[0].shape
+def margins_kernel(mode, flipped, arrived, h, state):
+    width, rows = flipped[0].shape
     blocks, _, block = arrived.shape
     names = list(state)
     wide = ((CHAINS, width), F32)
@@ -215,7 +229,7 @@
         if mode in ("turn", "last"):
             keep = jnp.broadcast_to(ins["keep"][:, :1], (CHAINS, block)) != 0.0
 
-        def one(b, cols, own, other, gap):
+        def one(b, cols, gap):
             g = arrived_ref[b].astype(F32)
             q = ins["q"][:, cols]
             if mode == "first":
@@ -237,20 +251,20 @@
                 pos = jnp.where(keep, q, ins["pos"][:, cols])
                 out["pos"][:, cols] = pos
                 gap = gap + square_gap(pos)
-            rounded = q.astype(BF16)
-            own = own + lax.dot_general(
-                rounded, own_ref[:, cols], CROSS, preferred_element_type=F32
-            )
-            other = other + lax.dot_general(
-                rounded, other_ref[:, cols], CROSS, preferred_element_type=F32
-            )
-            return own, other, gap
+            return q.astype(BF16), gap
 
         def group(i, carry):
+            own, other, gap = carry
+            rounded = []
             for j in range(GROUP):
                 b = i * GROUP + j
-                carry = one(b, pl.ds(pl.multiple_of(b * block, block), block), *carry)
-            return carry
+                part, gap = one(b, pl.ds(pl.multiple_of(b * block, block), block), gap)
+                rounded.append(part)
+            rounded = jnp.concatenate(rounded, axis=1)
+            cols = pl.ds(pl.multiple_of(i * (GROUP * block), GROUP * block), GROUP * block)
+            own = own + jnp.dot(rounded, own_ref[cols], preferred_element_type=F32)
+            other = other + jnp.dot(rounded, other_ref[cols], preferred_element_type=F32)
+            return own, other, gap
 
         zero = jnp.zeros((CHAINS, rows), F32)
         *total, gap = lax.fori_loop(
@@ -266,8 +280,7 @@
 
     result = call(
         body,
-        "margins_" + mode,
-        vmem(*held, arrived, h, *state.values()),
+        vmem(*flipped, arrived, h, *state.values()),
         list(outs.values()),
         flops=4 * CHAINS * rows * width,
     )
@@ -316,13 +329,16 @@
                 rest[0][...] = jnp.sqrt(picked / FEATURES + 1e-06)
             else:
                 rest[0][...] = jnp.broadcast_to(like, (CHAINS, EXTRA))
+
         def group(i, carry):
-            for j in range(WIDE):
-                b = i * WIDE + j
-                cols = pl.ds(pl.multiple_of(b * block, block), block)
+            for j in range(0, WIDE, GROUP):
+                at = i * WIDE + j
+                cols = pl.ds(pl.multiple_of(at * block, GROUP * block), GROUP * block)
                 terms = jnp.dot(weights[:, :rows], near_ref[:, cols], preferred_element_type=F32)
                 far = jnp.dot(weights[:, rows:], far_ref[:, cols], preferred_element_type=F32)
-                out_ref[b, :, :block] = (terms + far).astype(BF16)
+                terms = (terms + far).astype(BF16)
+                for b in range(GROUP):
+                    out_ref[at + b, :, :block] = terms[:, b * block : (b + 1) * block]
             return carry
 
         lax.fori_loop(0, blocks // WIDE, group, 0)
@@ -332,7 +348,6 @@
         outs.append(((TRANS, PAIRS) if extended else (CHAINS, EXTRA), F32))
     return call(
         body,
-        "terms",
         vmem(*partials, *signs, *held, *([earlier] if extended else [])),
         outs,
         flops=4 * CHAINS * rows * width,
@@ -366,7 +381,7 @@
     outs = [((blocks, CHAINS, block), BF16), ((CHAINS, block), F32)]
     if observations:
         outs.append(((TRANS, CHAINS), F32))
-    return call(body, "sum", vmem(arrived, *([residual] if carried else [])), outs)
+    return call(body, vmem(arrived, *([residual] if carried else [])), outs)
 
 
 def finish_kernel(arrived, h, p, q):
@@ -378,7 +393,7 @@
             cols = slice(b * block, (b + 1) * block)
             out_ref[:, cols] = p_ref[:, cols] + half * (arrived_ref[b].astype(F32) - q_ref[:, cols])
 
-    return call(body, "finish", vmem(arrived, h, p, q), [((CHAINS, blocks * block), F32)])[0]
+    return call(body, vmem(arrived, h, p, q), [((CHAINS, blocks * block), F32)])[0]
 
 
 def on_device(design, labels, start_position, momenta, lag_offsets, accept_bits, step_sizes):
@@ -396,20 +411,22 @@
         return lax.ppermute(value, "rows", swap)
 
     def around(margins):
-        moved = {
-            k: lax.ppermute(margins, "feat", [(i, (i + k) % ring) for i in range(ring)])
-            for k in (1, 3, 2)
-        }
+        moved = {}
+        for k in (2, 1, 3):
+            pairs = [(i, (i + k) % ring) for i in range(ring)]
+            moved[k] = lax.ppermute(margins, "feat", pairs)
         return [margins, moved[1], moved[2], moved[3]]
 
-    def gradient(margins, residual, likes=False, earlier=None):
+    def gradient(margins, residual, likes=False, earlier=None, beside=None):
         last = earlier is not None
         out, *side = terms_kernel(around(margins), signs, held, blocks, likes, earlier)
+        if beside is not None:
+            out, beside = lax.optimization_barrier((out, beside))
         block = out.shape[2] - (EXTRA if last else 0)
         send, residual, *totals = sum_kernel(
             exchange(out), residual, block, rows * devices if last else 0
         )
-        return exchange(send), residual, side + totals
+        return exchange(send), residual, side + totals + ([] if beside is None else [beside])
 
     def paired(margins):
         return pair_sum(margins, across(margins), rows)
@@ -420,28 +437,30 @@
     margins = pair_start(margins, swapped)
     held = (own, across(away))
     mom0, mom1, h, keep0, keep1, sign = draw(labels, momenta, lag_offsets, accept_bits, step_sizes)
+    sign, own_flipped = lax.optimization_barrier((sign, flip(own)))
     signs = (sign, across(sign))
-    g0, residual, _ = gradient(margins, None)
+    g0, residual, (far_flipped,) = gradient(margins, None, beside=flip(held[1]))
+    flipped = (own_flipped, far_flipped)
     g = g0
     now = {"q": start}
     for leap in range(LEAP):
         if leap == 0:
-            now = margins_kernel("first", held, g, h, {"q": start, "mom": mom0})
+            now = margins_kernel("first", flipped, g, h, {"q": start, "mom": mom0})
         else:
-            now = margins_kernel("mid", held, g, h, {"q": now["q"], "p": now["p"]})
+            now = margins_kernel("mid", flipped, g, h, {"q": now["q"], "p": now["p"]})
         g, residual, side = gradient(paired(now["margins"]), residual, likes=leap + 1 == LEAP)
     (like,) = side
     for leap in range(LEAP):
         last = leap + 1 == LEAP
         if leap == 0:
             state = {"q": now["q"], "q0": start, "g0": g0, "mom": mom1, "keep": keep0}
-            now = margins_kernel("turn", held, g, h, state)
+            now = margins_kernel("turn", flipped, g, h, state)
             position, gap = now["pos"], now["gap"]
         elif not last:
-            now = margins_kernel("mid", held, g, h, {"q": now["q"], "p": now["p"]})
+            now = margins_kernel("mid", flipped, g, h, {"q": now["q"], "p": now["p"]})
         else:
             state = {"q": now["q"], "p": now["p"], "pos": position, "gap": gap, "keep": keep1}
-            now = margins_kernel("last", held, g, h, state)
+            now = margins_kernel("last", flipped, g, h, state)
             final_position = assemble(now["pos"], across(now["pos"]))
             sign, final_position = lax.optimization_barrier((sign, final_position))
             signs = (sign, signs[1])

time: 422 us -> 414 us (0.981)
  starting transfers between devices: 88.2 us -> 77.2 us
  waiting for transfers between devices: 38.6 us -> 47.5 us
  Pallas kernels: 53.3 us -> 46.4 us
    ppermute x33, starting transfers between devices: 39.1 us -> 27.4 us  [around(): moved[k] = lax.ppermute(margins, 'feat', pairs)]
    ppermute x33, waiting for transfers between devices: 26.1 us -> 35.8 us  [around(): moved[k] = lax.ppermute(margins, 'feat', pairs)]
    pallas_call x46 -> x48, Pallas kernels: 51.4 us -> 44.5 us  [call(): pl.pallas_call(body, in_specs=[spec for _, spec in ins], out_specs=[VMEM]...]
  transfers between devices with their start and end apart: 48 -> 48, of which waited for: 42 -> 40; matrix products, arithmetic and copies ran while one was open for 0% -> 0% of each run, Pallas kernels for 0% -> 1%
where the time goes in v1:
time: 414 us; the launch traced here: 413 us
  blocking collectives  239 us (58%)
  starting transfers between devices  77.2 us (19%)
  waiting for transfers between devices  47.5 us (11%)
  Pallas kernels  46.4 us (11%)
    all_to_all x22, blocking collectives, exchange(): return lax.all_to_all(blocked, 'rows', 0, 0, axis_index_groups=chips)  239 us
    ppermute x15, starting transfers between devices, across(): return lax.ppermute(value, 'rows', swap)  49.8 us
    pallas_call x48, Pallas kernels, call(): pl.pallas_call(body, in_specs=[spec for _, spec in ins], out_specs=[VMEM]...  44.5 us
    ppermute x33, waiting for transfers between devices, around(): moved[k] = lax.ppermute(margins, 'feat', pairs)  35.8 us
    ppermute x33, starting transfers between devices, around(): moved[k] = lax.ppermute(margins, 'feat', pairs)  27.4 us
    ppermute x15, waiting for transfers between devices, across(): return lax.ppermute(value, 'rows', swap)  11.6 us
  transfers between devices with their start and end apart: 48, of which 40 were waited for; matrix products, arithmetic and copies ran while one was open for 0% of the time, Pallas kernels for 1%

profile of v1, /device:TPU:1, one launch (start us, length us, event | category | flops | bytes accessed | tf_op | source)
XLA Modules:
  0.0 412.6 jit_solution(2014357425814703749)
XLA Ops:
  1.9 6.3 %shard_map.103 = (f32[16,256]{1,0:T(8,128)S(1)}, bf16[256,8192]{1,0:T(8,128)(2,1)S(1)}, bf16[256,8192]{1,0:T(8,128)(2,1)S(1)}, f32[16,8192]{1,0:T(8,128)S(1)}) custom-call(f32[16,16384]{1,0:T(8,128)S(1)} %copy-done.1, bf16[256,16384]{1,0:T(8,128)(2,1)} %design_ref.1), custom_call_target="tpu_custom_call" | custom-call | flops 134217728 | bytes 8388608 | tf_op jit(solution)/shard_map/pallas_call | solution.py:33
  10.8 3.9 collective-permute-start.3
  15.4 2.0 shard_map.104.own_ref
  19.4 2.0 shard_map.107.other_ref
  22.8 14.3 %all_to_all.110.refs_0_ = bf16[16,16,512]{2,1,0:T(8,128)(2,1)S(1)} all-to-all(bf16[16,16,512]{2,1,0:T(8,128)(2,1)S(1)} %shard_map.106), channel_id=1, replica_groups={{0,8,16,24,32,40,48,56,64,72,80,88,96,104,112,120},{4,12,20,28,36,44,52..., dimensions={0} | all-to-all | bytes 524288 | tf_op jit(solution)/shard_map/all_to_all | solution.py:408
  37.2 11.0 %all_to_all.111.arrived_ref.refs_2_ = bf16[16,16,512]{2,1,0:T(8,128)(2,1)S(1)} all-to-all(bf16[16,16,512]{2,1,0:T(8,128)(2,1)S(1)} %get-tuple-element.90), channel_id=1, replica_groups={{0,8,16,24,32,40,48,56,64,72,80,88,96,104,112,120},{4,12,20,28,36,44,52..., dimensions={0} | all-to-all | bytes 524288 | tf_op jit(solution)/shard_map/all_to_all | solution.py:408
  48.2 1.7 shard_map.109
  49.8 2.6 collective-permute-start.6
  53.3 2.0 collective-permute-start.9
  55.3 1.7 collective-permute-start.8
  57.1 2.5 collective-permute-done.8.refs_2_
  62.4 10.6 %all_to_all.112.refs_0_ = bf16[16,16,512]{2,1,0:T(8,128)(2,1)S(1)} all-to-all(bf16[16,16,512]{2,1,0:T(8,128)(2,1)S(1)} %shard_map.111), channel_id=1, replica_groups={{0,8,16,24,32,40,48,56,64,72,80,88,96,104,112,120},{4,12,20,28,36,44,52..., dimensions={0} | all-to-all | bytes 524288 | tf_op jit(solution)/shard_map/all_to_all | solution.py:408
  73.0 10.7 %all_to_all.113.arrived_ref = bf16[16,16,512]{2,1,0:T(8,128)(2,1)S(1)} all-to-all(bf16[16,16,512]{2,1,0:T(8,128)(2,1)S(1)} %get-tuple-element.96), channel_id=1, replica_groups={{0,8,16,24,32,40,48,56,64,72,80,88,96,104,112,120},{4,12,20,28,36,44,52..., dimensions={0} | all-to-all | bytes 524288 | tf_op jit(solution)/shard_map/all_to_all | solution.py:408
  83.7 1.6 shard_map.113
  85.4 4.6 %collective-permute-start.10 = (f32[16,512]{1,0:T(8,128)S(1)}, f32[16,512]{1,0:T(8,128)S(1)}, u32[]{:S(2)}, u32[]{:S(2)}) collective-permute-start(f32[16,512]{1,0:T(8,128)S(1)} %get-tuple-element.99.mine_ref), channel_id=1, source_target_pairs={{0,4},{4,0},{8,12},{12,8},{16,20},{20,16},{24,28},{28,24},{32,36},... | collective-permute-start | bytes 98312 | tf_op jit(solution)/shard_map/ppermute | solution.py:411
  93.6 1.6 collective-permute-done.12.refs_2_
  97.7 10.5 %all_to_all.114.refs_0_ = bf16[16,16,512]{2,1,0:T(8,128)(2,1)S(1)} all-to-all(bf16[16,16,512]{2,1,0:T(8,128)(2,1)S(1)} %shard_map.115), channel_id=1, replica_groups={{0,8,16,24,32,40,48,56,64,72,80,88,96,104,112,120},{4,12,20,28,36,44,52..., dimensions={0} | all-to-all | bytes 524288 | tf_op jit(solution)/shard_map/all_to_all | solution.py:408
  108.2 10.8 %all_to_all.115.arrived_ref = bf16[16,16,512]{2,1,0:T(8,128)(2,1)S(1)} all-to-all(bf16[16,16,512]{2,1,0:T(8,128)(2,1)S(1)} %get-tuple-element.101), channel_id=1, replica_groups={{0,8,16,24,32,40,48,56,64,72,80,88,96,104,112,120},{4,12,20,28,36,44,52..., dimensions={0} | all-to-all | bytes 524288 | tf_op jit(solution)/shard_map/all_to_all | solution.py:408
  119.1 1.6 shard_map.117
  120.7 4.0 collective-permute-start.14
  125.5 1.7 collective-permute-start.17
  128.3 3.2 collective-permute-done.16.refs_2_
  133.2 10.6 %all_to_all.116.refs_0_ = bf16[16,16,512]{2,1,0:T(8,128)(2,1)S(1)} all-to-all(bf16[16,16,512]{2,1,0:T(8,128)(2,1)S(1)} %shard_map.119), channel_id=1, replica_groups={{0,8,16,24,32,40,48,56,64,72,80,88,96,104,112,120},{4,12,20,28,36,44,52..., dimensions={0} | all-to-all | bytes 524288 | tf_op jit(solution)/shard_map/all_to_all | solution.py:408
  143.9 10.7 %all_to_all.117.arrived_ref = bf16[16,16,512]{2,1,0:T(8,128)(2,1)S(1)} all-to-all(bf16[16,16,512]{2,1,0:T(8,128)(2,1)S(1)} %get-tuple-element.106), channel_id=1, replica_groups={{0,8,16,24,32,40,48,56,64,72,80,88,96,104,112,120},{4,12,20,28,36,44,52..., dimensions={0} | all-to-all | bytes 524288 | tf_op jit(solution)/shard_map/all_to_all | solution.py:408
  154.6 1.7 shard_map.121
  156.3 4.6 %collective-permute-start.18 = (f32[16,512]{1,0:T(8,128)S(1)}, f32[16,512]{1,0:T(8,128)S(1)}, u32[]{:S(2)}, u32[]{:S(2)}) collective-permute-start(f32[16,512]{1,0:T(8,128)S(1)} %get-tuple-element.109.mine_ref), channel_id=1, source_target_pairs={{0,4},{4,0},{8,12},{12,8},{16,20},{20,16},{24,28},{28,24},{32,36},... | collective-permute-start | bytes 98312 | tf_op jit(solution)/shard_map/ppermute | solution.py:411
  164.5 1.8 collective-permute-done.20.refs_2_
  168.6 10.5 %all_to_all.118.refs_0_ = bf16[16,16,512]{2,1,0:T(8,128)(2,1)S(1)} all-to-all(bf16[16,16,512]{2,1,0:T(8,128)(2,1)S(1)} %shard_map.123), channel_id=1, replica_groups={{0,8,16,24,32,40,48,56,64,72,80,88,96,104,112,120},{4,12,20,28,36,44,52..., dimensions={0} | all-to-all | bytes 524288 | tf_op jit(solution)/shard_map/all_to_all | solution.py:408
  179.1 10.8 %all_to_all.119.arrived_ref = bf16[16,16,512]{2,1,0:T(8,128)(2,1)S(1)} all-to-all(bf16[16,16,512]{2,1,0:T(8,128)(2,1)S(1)} %get-tuple-element.111), channel_id=1, replica_groups={{0,8,16,24,32,40,48,56,64,72,80,88,96,104,112,120},{4,12,20,28,36,44,52..., dimensions={0} | all-to-all | bytes 524288 | tf_op jit(solution)/shard_map/all_to_all | solution.py:408
  190.0 2.2 shard_map.125
  192.2 4.0 collective-permute-start.22
  197.1 1.7 collective-permute-start.25
  199.8 3.2 collective-permute-done.24.refs_2_
  204.8 10.6 %all_to_all.120.refs_0_ = bf16[16,16,512]{2,1,0:T(8,128)(2,1)S(1)} all-to-all(bf16[16,16,512]{2,1,0:T(8,128)(2,1)S(1)} %get-tuple-element.115), channel_id=1, replica_groups={{0,8,16,24,32,40,48,56,64,72,80,88,96,104,112,120},{4,12,20,28,36,44,52..., dimensions={0} | all-to-all | bytes 524288 | tf_op jit(solution)/shard_map/all_to_all | solution.py:408
  215.5 10.7 %all_to_all.121.arrived_ref = bf16[16,16,512]{2,1,0:T(8,128)(2,1)S(1)} all-to-all(bf16[16,16,512]{2,1,0:T(8,128)(2,1)S(1)} %get-tuple-element.117), channel_id=1, replica_groups={{0,8,16,24,32,40,48,56,64,72,80,88,96,104,112,120},{4,12,20,28,36,44,52..., dimensions={0} | all-to-all | bytes 524288 | tf_op jit(solution)/shard_map/all_to_all | solution.py:408
  226.2 1.7 shard_map.129
  227.9 4.6 %collective-permute-start.26 = (f32[16,512]{1,0:T(8,128)S(1)}, f32[16,512]{1,0:T(8,128)S(1)}, u32[]{:S(2)}, u32[]{:S(2)}) collective-permute-start(f32[16,512]{1,0:T(8,128)S(1)} %get-tuple-element.121.mine_ref), channel_id=1, source_target_pairs={{0,4},{4,0},{8,12},{12,8},{16,20},{20,16},{24,28},{28,24},{32,36},... | collective-permute-start | bytes 98312 | tf_op jit(solution)/shard_map/ppermute | solution.py:411
  236.1 1.8 collective-permute-done.28.refs_2_
  239.9 10.6 %all_to_all.122.refs_0_ = bf16[16,16,512]{2,1,0:T(8,128)(2,1)S(1)} all-to-all(bf16[16,16,512]{2,1,0:T(8,128)(2,1)S(1)} %shard_map.131), channel_id=1, replica_groups={{0,8,16,24,32,40,48,56,64,72,80,88,96,104,112,120},{4,12,20,28,36,44,52..., dimensions={0} | all-to-all | bytes 524288 | tf_op jit(solution)/shard_map/all_to_all | solution.py:408
  250.5 10.8 %all_to_all.123.arrived_ref = bf16[16,16,512]{2,1,0:T(8,128)(2,1)S(1)} all-to-all(bf16[16,16,512]{2,1,0:T(8,128)(2,1)S(1)} %get-tuple-element.123), channel_id=1, replica_groups={{0,8,16,24,32,40,48,56,64,72,80,88,96,104,112,120},{4,12,20,28,36,44,52..., dimensions={0} | all-to-all | bytes 524288 | tf_op jit(solution)/shard_map/all_to_all | solution.py:408
  261.3 1.7 shard_map.133
  262.9 4.4 %collective-permute-start.30 = (f32[16,512]{1,0:T(8,128)S(1)}, f32[16,512]{1,0:T(8,128)S(1)}, u32[]{:S(2)}, u32[]{:S(2)}) collective-permute-start(f32[16,512]{1,0:T(8,128)S(1)} %get-tuple-element.126.mine_ref), channel_id=1, source_target_pairs={{0,4},{4,0},{8,12},{12,8},{16,20},{20,16},{24,28},{28,24},{32,36},... | collective-permute-start | bytes 98312 | tf_op jit(solution)/shard_map/ppermute | solution.py:411
  268.2 1.7 collective-permute-start.33
  270.9 3.2 collective-permute-done.32.refs_2_
  275.8 10.8 %all_to_all.124.refs_0_ = bf16[16,16,512]{2,1,0:T(8,128)(2,1)S(1)} all-to-all(bf16[16,16,512]{2,1,0:T(8,128)(2,1)S(1)} %shard_map.135), channel_id=1, replica_groups={{0,8,16,24,32,40,48,56,64,72,80,88,96,104,112,120},{4,12,20,28,36,44,52..., dimensions={0} | all-to-all | bytes 524288 | tf_op jit(solution)/shard_map/all_to_all | solution.py:408
  286.7 10.7 %all_to_all.125.arrived_ref = bf16[16,16,512]{2,1,0:T(8,128)(2,1)S(1)} all-to-all(bf16[16,16,512]{2,1,0:T(8,128)(2,1)S(1)} %get-tuple-element.128), channel_id=1, replica_groups={{0,8,16,24,32,40,48,56,64,72,80,88,96,104,112,120},{4,12,20,28,36,44,52..., dimensions={0} | all-to-all | bytes 524288 | tf_op jit(solution)/shard_map/all_to_all | solution.py:408
  297.4 1.6 shard_map.137
  299.1 4.6 %collective-permute-start.34 = (f32[16,512]{1,0:T(8,128)S(1)}, f32[16,512]{1,0:T(8,128)S(1)}, u32[]{:S(2)}, u32[]{:S(2)}) collective-permute-start(f32[16,512]{1,0:T(8,128)S(1)} %get-tuple-element.131.mine_ref), channel_id=1, source_target_pairs={{0,4},{4,0},{8,12},{12,8},{16,20},{20,16},{24,28},{28,24},{32,36},... | collective-permute-start | bytes 98312 | tf_op jit(solution)/shard_map/ppermute | solution.py:411
  307.3 1.8 collective-permute-done.36.refs_2_
  311.0 10.6 %all_to_all.126.refs_0_ = bf16[16,16,512]{2,1,0:T(8,128)(2,1)S(1)} all-to-all(bf16[16,16,512]{2,1,0:T(8,128)(2,1)S(1)} %shard_map.139), channel_id=1, replica_groups={{0,8,16,24,32,40,48,56,64,72,80,88,96,104,112,120},{4,12,20,28,36,44,52..., dimensions={0} | all-to-all | bytes 524288 | tf_op jit(solution)/shard_map/all_to_all | solution.py:408
  321.7 10.8 %all_to_all.127.arrived_ref = bf16[16,16,512]{2,1,0:T(8,128)(2,1)S(1)} all-to-all(bf16[16,16,512]{2,1,0:T(8,128)(2,1)S(1)} %get-tuple-element.133), channel_id=1, replica_groups={{0,8,16,24,32,40,48,56,64,72,80,88,96,104,112,120},{4,12,20,28,36,44,52..., dimensions={0} | all-to-all | bytes 524288 | tf_op jit(solution)/shard_map/all_to_all | solution.py:408
  332.4 1.6 shard_map.141
  334.0 4.4 %collective-permute-start.38 = (f32[16,512]{1,0:T(8,128)S(1)}, f32[16,512]{1,0:T(8,128)S(1)}, u32[]{:S(2)}, u32[]{:S(2)}) collective-permute-start(f32[16,512]{1,0:T(8,128)S(1)} %get-tuple-element.136.mine_ref), channel_id=1, source_target_pairs={{0,4},{4,0},{8,12},{12,8},{16,20},{20,16},{24,28},{28,24},{32,36},... | collective-permute-start | bytes 98312 | tf_op jit(solution)/shard_map/ppermute | solution.py:411
  339.3 1.7 collective-permute-start.41
  342.0 3.2 collective-permute-done.40.refs_2_
  346.9 10.6 %all_to_all.128.refs_0_ = bf16[16,16,512]{2,1,0:T(8,128)(2,1)S(1)} all-to-all(bf16[16,16,512]{2,1,0:T(8,128)(2,1)S(1)} %shard_map.143), channel_id=1, replica_groups={{0,8,16,24,32,40,48,56,64,72,80,88,96,104,112,120},{4,12,20,28,36,44,52..., dimensions={0} | all-to-all | bytes 524288 | tf_op jit(solution)/shard_map/all_to_all | solution.py:408
  357.6 10.7 %all_to_all.129.arrived_ref = bf16[16,16,512]{2,1,0:T(8,128)(2,1)S(1)} all-to-all(bf16[16,16,512]{2,1,0:T(8,128)(2,1)S(1)} %get-tuple-element.138), channel_id=1, replica_groups={{0,8,16,24,32,40,48,56,64,72,80,88,96,104,112,120},{4,12,20,28,36,44,52..., dimensions={0} | all-to-all | bytes 524288 | tf_op jit(solution)/shard_map/all_to_all | solution.py:408
  368.3 1.7 shard_map.145
  370.0 4.6 %collective-permute-start.42 = (f32[16,8192]{1,0:T(8,128)S(1)}, f32[16,8192]{1,0:T(8,128)S(1)}, u32[]{:S(2)}, u32[]{:S(2)}) collective-permute-start(f32[16,8192]{1,0:T(8,128)S(1)} %get-tuple-element.144.mine_ref), channel_id=1, source_target_pairs={{0,4},{4,0},{8,12},{12,8},{16,20},{20,16},{24,28},{28,24},{32,36},... | collective-permute-start | bytes 1572872 | tf_op jit(solution)/shard_map/ppermute | solution.py:411
  379.2 1.7 collective-permute-done.45.refs_2_
  383.0 10.9 %all_to_all.130.refs_0_ = bf16[16,16,640]{2,1,0:T(8,128)(2,1)S(1)} all-to-all(bf16[16,16,640]{2,1,0:T(8,128)(2,1)S(1)} %get-tuple-element.149), channel_id=1, replica_groups={{0,8,16,24,32,40,48,56,64,72,80,88,96,104,112,120},{4,12,20,28,36,44,52..., dimensions={0} | all-to-all | bytes 655360 | tf_op jit(solution)/shard_map/all_to_all | solution.py:408
  394.6 10.8 %all_to_all.131.arrived_ref = bf16[16,16,512]{2,1,0:T(8,128)(2,1)S(1)} all-to-all(bf16[16,16,512]{2,1,0:T(8,128)(2,1)S(1)} %get-tuple-element.151), channel_id=1, replica_groups={{0,8,16,24,32,40,48,56,64,72,80,88,96,104,112,120},{4,12,20,28,36,44,52..., dimensions={0} | all-to-all | bytes 524288 | tf_op jit(solution)/shard_map/all_to_all | solution.py:408
  405.5 4.5 %collective-permute-start.47 = (f32[16,8192]{1,0:T(8,128)S(1)}, f32[16,8192]{1,0:T(8,128)S(1)}, u32[]{:S(2)}, u32[]{:S(2)}) collective-permute-start(f32[16,8192]{1,0:T(8,128)S(1)} %shard_map.149.mine_ref), channel_id=1, source_target_pairs={{0,4},{4,0},{8,12},{12,8},{16,20},{20,16},{24,28},{28,24},{32,36},... | collective-permute-start | bytes 1572872 | tf_op jit(solution)/shard_map/ppermute | solution.py:411
  409.9 1.5 collective-permute-done.47.other_ref
  (116 shorter events, 58.3 us)
Async XLA Ops:
  0.6 1.2 copy-start.1
  8.1 2.3 collective-permute-start
  10.4 9.0 %collective-permute-start.5 = (bf16[256,8192]{1,0:T(8,128)(2,1)S(1)}, bf16[256,8192]{1,0:T(8,128)(2,1)S(1)}, u32[]{:S(2)}, u32[]{:S(2)}) collective-permute-start(bf16[256,8192]{1,0:T(8,128)(2,1)S(1)} %get-tuple-element.87), channel_id=1, source_target_pairs={{0,4},{4,0},{8,12},{12,8},{16,20},{20,16},{24,28},{28,24},{32,36},... | collective-permute-start | bytes 12582920 | tf_op jit(solution)/shard_map/ppermute | solution.py:411
  10.8 10.6 %collective-permute-start.3 = (f32[16,512]{1,0:T(8,128)S(1)}, f32[16,512]{1,0:T(8,128)S(1)}, u32[]{:S(2)}, u32[]{:S(2)}) collective-permute-start(f32[16,512]{1,0:T(8,128)S(1)} %shard_map.105.refs_0_), channel_id=1, source_target_pairs={{0,3},{1,0},{2,1},{3,2},{4,7},{5,4},{6,5},{7,6},{8,11},{9,8},{10,9... | collective-permute-start | bytes 98312 | tf_op jit(solution)/shard_map/ppermute | solution.py:417
  14.7 6.8 %collective-permute-start.2 = (f32[16,512]{1,0:T(8,128)S(1)}, f32[16,512]{1,0:T(8,128)S(1)}, u32[]{:S(2)}, u32[]{:S(2)}) collective-permute-start(f32[16,512]{1,0:T(8,128)S(1)} %shard_map.105.refs_0_), channel_id=1, source_target_pairs={{0,2},{1,3},{2,0},{3,1},{4,6},{5,7},{6,4},{7,5},{8,10},{9,11},{10,... | collective-permute-start | bytes 98312 | tf_op jit(solution)/shard_map/ppermute | solution.py:417
  14.7 6.8 %collective-permute-start.1 = (f32[16,512]{1,0:T(8,128)S(1)}, f32[16,512]{1,0:T(8,128)S(1)}, u32[]{:S(2)}, u32[]{:S(2)}) collective-permute-start(f32[16,512]{1,0:T(8,128)S(1)} %shard_map.105.refs_0_), channel_id=1, source_target_pairs={{0,1},{1,2},{2,3},{3,0},{4,5},{5,6},{6,7},{7,4},{8,9},{9,10},{10,1... | collective-permute-start | bytes 98312 | tf_op jit(solution)/shard_map/ppermute | solution.py:417
  15.4 2.0 copy-start
  15.4 2.0 copy-start.2
  15.4 2.0 copy-start.3
  15.4 2.0 copy-start.4
  15.4 2.0 copy-start.5
  18.3 3.1 collective-permute-start.4
  49.8 3.5 collective-permute-start.6
  53.3 3.7 collective-permute-start.9
  55.3 4.3 %collective-permute-start.8 = (f32[16,512]{1,0:T(8,128)S(1)}, f32[16,512]{1,0:T(8,128)S(1)}, u32[]{:S(2)}, u32[]{:S(2)}) collective-permute-start(f32[16,512]{1,0:T(8,128)S(1)} %shard_map.110.refs_0_), channel_id=1, source_target_pairs={{0,2},{1,3},{2,0},{3,1},{4,6},{5,7},{6,4},{7,5},{8,10},{9,11},{10,... | collective-permute-start | bytes 98312 | tf_op jit(solution)/shard_map/ppermute | solution.py:417
  57.1 4.0 collective-permute-start.7
  85.4 5.5 %collective-permute-start.10 = (f32[16,512]{1,0:T(8,128)S(1)}, f32[16,512]{1,0:T(8,128)S(1)}, u32[]{:S(2)}, u32[]{:S(2)}) collective-permute-start(f32[16,512]{1,0:T(8,128)S(1)} %get-tuple-element.99.mine_ref), channel_id=1, source_target_pairs={{0,4},{4,0},{8,12},{12,8},{16,20},{20,16},{24,28},{28,24},{32,36},... | collective-permute-start | bytes 98312 | tf_op jit(solution)/shard_map/ppermute | solution.py:411
  90.8 2.8 collective-permute-start.13
  90.8 4.3 %collective-permute-start.12 = (f32[16,512]{1,0:T(8,128)S(1)}, f32[16,512]{1,0:T(8,128)S(1)}, u32[]{:S(2)}, u32[]{:S(2)}) collective-permute-start(f32[16,512]{1,0:T(8,128)S(1)} %shard_map.114.refs_0_), channel_id=1, source_target_pairs={{0,2},{1,3},{2,0},{3,1},{4,6},{5,7},{6,4},{7,5},{8,10},{9,11},{10,... | collective-permute-start | bytes 98312 | tf_op jit(solution)/shard_map/ppermute | solution.py:417
  91.5 4.9 %collective-permute-start.11 = (f32[16,512]{1,0:T(8,128)S(1)}, f32[16,512]{1,0:T(8,128)S(1)}, u32[]{:S(2)}, u32[]{:S(2)}) collective-permute-start(f32[16,512]{1,0:T(8,128)S(1)} %shard_map.114.refs_0_), channel_id=1, source_target_pairs={{0,1},{1,2},{2,3},{3,0},{4,5},{5,6},{6,7},{7,4},{8,9},{9,10},{10,1... | collective-permute-start | bytes 98312 | tf_op jit(solution)/shard_map/ppermute | solution.py:417
  120.7 4.8 %collective-permute-start.14 = (f32[16,512]{1,0:T(8,128)S(1)}, f32[16,512]{1,0:T(8,128)S(1)}, u32[]{:S(2)}, u32[]{:S(2)}) collective-permute-start(f32[16,512]{1,0:T(8,128)S(1)} %get-tuple-element.104.mine_ref), channel_id=1, source_target_pairs={{0,4},{4,0},{8,12},{12,8},{16,20},{20,16},{24,28},{28,24},{32,36},... | collective-permute-start | bytes 98312 | tf_op jit(solution)/shard_map/ppermute | solution.py:411
  125.5 2.8 collective-permute-start.17
  127.3 4.3 %collective-permute-start.16 = (f32[16,512]{1,0:T(8,128)S(1)}, f32[16,512]{1,0:T(8,128)S(1)}, u32[]{:S(2)}, u32[]{:S(2)}) collective-permute-start(f32[16,512]{1,0:T(8,128)S(1)} %shard_map.118.refs_0_), channel_id=1, source_target_pairs={{0,2},{1,3},{2,0},{3,1},{4,6},{5,7},{6,4},{7,5},{8,10},{9,11},{10,... | collective-permute-start | bytes 98312 | tf_op jit(solution)/shard_map/ppermute | solution.py:417
  127.9 4.0 collective-permute-start.15
  156.3 5.5 %collective-permute-start.18 = (f32[16,512]{1,0:T(8,128)S(1)}, f32[16,512]{1,0:T(8,128)S(1)}, u32[]{:S(2)}, u32[]{:S(2)}) collective-permute-start(f32[16,512]{1,0:T(8,128)S(1)} %get-tuple-element.109.mine_ref), channel_id=1, source_target_pairs={{0,4},{4,0},{8,12},{12,8},{16,20},{20,16},{24,28},{28,24},{32,36},... | collective-permute-start | bytes 98312 | tf_op jit(solution)/shard_map/ppermute | solution.py:411
  161.7 2.8 collective-permute-start.21
  162.0 4.3 %collective-permute-start.20 = (f32[16,512]{1,0:T(8,128)S(1)}, f32[16,512]{1,0:T(8,128)S(1)}, u32[]{:S(2)}, u32[]{:S(2)}) collective-permute-start(f32[16,512]{1,0:T(8,128)S(1)} %shard_map.122.refs_0_), channel_id=1, source_target_pairs={{0,2},{1,3},{2,0},{3,1},{4,6},{5,7},{6,4},{7,5},{8,10},{9,11},{10,... | collective-permute-start | bytes 98312 | tf_op jit(solution)/shard_map/ppermute | solution.py:417
  163.0 4.3 %collective-permute-start.19 = (f32[16,512]{1,0:T(8,128)S(1)}, f32[16,512]{1,0:T(8,128)S(1)}, u32[]{:S(2)}, u32[]{:S(2)}) collective-permute-start(f32[16,512]{1,0:T(8,128)S(1)} %shard_map.122.refs_0_), channel_id=1, source_target_pairs={{0,1},{1,2},{2,3},{3,0},{4,5},{5,6},{6,7},{7,4},{8,9},{9,10},{10,1... | collective-permute-start | bytes 98312 | tf_op jit(solution)/shard_map/ppermute | solution.py:417
  192.2 4.9 %collective-permute-start.22 = (f32[16,512]{1,0:T(8,128)S(1)}, f32[16,512]{1,0:T(8,128)S(1)}, u32[]{:S(2)}, u32[]{:S(2)}) collective-permute-start(f32[16,512]{1,0:T(8,128)S(1)} %get-tuple-element.114.mine_ref), channel_id=1, source_target_pairs={{0,4},{4,0},{8,12},{12,8},{16,20},{20,16},{24,28},{28,24},{32,36},... | collective-permute-start | bytes 98312 | tf_op jit(solution)/shard_map/ppermute | solution.py:411
  197.1 2.8 collective-permute-start.25
  198.8 4.3 %collective-permute-start.24 = (f32[16,512]{1,0:T(8,128)S(1)}, f32[16,512]{1,0:T(8,128)S(1)}, u32[]{:S(2)}, u32[]{:S(2)}) collective-permute-start(f32[16,512]{1,0:T(8,128)S(1)} %shard_map.126.refs_0_), channel_id=1, source_target_pairs={{0,2},{1,3},{2,0},{3,1},{4,6},{5,7},{6,4},{7,5},{8,10},{9,11},{10,... | collective-permute-start | bytes 98312 | tf_op jit(solution)/shard_map/ppermute | solution.py:417
  199.4 4.0 collective-permute-start.23
  227.9 5.5 %collective-permute-start.26 = (f32[16,512]{1,0:T(8,128)S(1)}, f32[16,512]{1,0:T(8,128)S(1)}, u32[]{:S(2)}, u32[]{:S(2)}) collective-permute-start(f32[16,512]{1,0:T(8,128)S(1)} %get-tuple-element.121.mine_ref), channel_id=1, source_target_pairs={{0,4},{4,0},{8,12},{12,8},{16,20},{20,16},{24,28},{28,24},{32,36},... | collective-permute-start | bytes 98312 | tf_op jit(solution)/shard_map/ppermute | solution.py:411
  233.4 2.8 collective-permute-start.29
  233.7 4.3 %collective-permute-start.28 = (f32[16,512]{1,0:T(8,128)S(1)}, f32[16,512]{1,0:T(8,128)S(1)}, u32[]{:S(2)}, u32[]{:S(2)}) collective-permute-start(f32[16,512]{1,0:T(8,128)S(1)} %shard_map.130.refs_0_), channel_id=1, source_target_pairs={{0,2},{1,3},{2,0},{3,1},{4,6},{5,7},{6,4},{7,5},{8,10},{9,11},{10,... | collective-permute-start | bytes 98312 | tf_op jit(solution)/shard_map/ppermute | solution.py:417
  234.6 4.0 collective-permute-start.27
  262.9 5.2 %collective-permute-start.30 = (f32[16,512]{1,0:T(8,128)S(1)}, f32[16,512]{1,0:T(8,128)S(1)}, u32[]{:S(2)}, u32[]{:S(2)}) collective-permute-start(f32[16,512]{1,0:T(8,128)S(1)} %get-tuple-element.126.mine_ref), channel_id=1, source_target_pairs={{0,4},{4,0},{8,12},{12,8},{16,20},{20,16},{24,28},{28,24},{32,36},... | collective-permute-start | bytes 98312 | tf_op jit(solution)/shard_map/ppermute | solution.py:411
  268.2 2.8 collective-permute-start.33
  269.9 4.3 %collective-permute-start.32 = (f32[16,512]{1,0:T(8,128)S(1)}, f32[16,512]{1,0:T(8,128)S(1)}, u32[]{:S(2)}, u32[]{:S(2)}) collective-permute-start(f32[16,512]{1,0:T(8,128)S(1)} %shard_map.134.refs_0_), channel_id=1, source_target_pairs={{0,2},{1,3},{2,0},{3,1},{4,6},{5,7},{6,4},{7,5},{8,10},{9,11},{10,... | collective-permute-start | bytes 98312 | tf_op jit(solution)/shard_map/ppermute | solution.py:417
  270.5 4.0 collective-permute-start.31
  299.1 5.5 %collective-permute-start.34 = (f32[16,512]{1,0:T(8,128)S(1)}, f32[16,512]{1,0:T(8,128)S(1)}, u32[]{:S(2)}, u32[]{:S(2)}) collective-permute-start(f32[16,512]{1,0:T(8,128)S(1)} %get-tuple-element.131.mine_ref), channel_id=1, source_target_pairs={{0,4},{4,0},{8,12},{12,8},{16,20},{20,16},{24,28},{28,24},{32,36},... | collective-permute-start | bytes 98312 | tf_op jit(solution)/shard_map/ppermute | solution.py:411
  304.5 2.8 collective-permute-start.37
  304.8 4.3 %collective-permute-start.36 = (f32[16,512]{1,0:T(8,128)S(1)}, f32[16,512]{1,0:T(8,128)S(1)}, u32[]{:S(2)}, u32[]{:S(2)}) collective-permute-start(f32[16,512]{1,0:T(8,128)S(1)} %shard_map.138.refs_0_), channel_id=1, source_target_pairs={{0,2},{1,3},{2,0},{3,1},{4,6},{5,7},{6,4},{7,5},{8,10},{9,11},{10,... | collective-permute-start | bytes 98312 | tf_op jit(solution)/shard_map/ppermute | solution.py:417
  305.7 4.0 collective-permute-start.35
  334.0 5.2 %collective-permute-start.38 = (f32[16,512]{1,0:T(8,128)S(1)}, f32[16,512]{1,0:T(8,128)S(1)}, u32[]{:S(2)}, u32[]{:S(2)}) collective-permute-start(f32[16,512]{1,0:T(8,128)S(1)} %get-tuple-element.136.mine_ref), channel_id=1, source_target_pairs={{0,4},{4,0},{8,12},{12,8},{16,20},{20,16},{24,28},{28,24},{32,36},... | collective-permute-start | bytes 98312 | tf_op jit(solution)/shard_map/ppermute | solution.py:411
  339.3 2.8 collective-permute-start.41
  341.0 4.3 %collective-permute-start.40 = (f32[16,512]{1,0:T(8,128)S(1)}, f32[16,512]{1,0:T(8,128)S(1)}, u32[]{:S(2)}, u32[]{:S(2)}) collective-permute-start(f32[16,512]{1,0:T(8,128)S(1)} %shard_map.142.refs_0_), channel_id=1, source_target_pairs={{0,2},{1,3},{2,0},{3,1},{4,6},{5,7},{6,4},{7,5},{8,10},{9,11},{10,... | collective-permute-start | bytes 98312 | tf_op jit(solution)/shard_map/ppermute | solution.py:417
  341.6 4.0 collective-permute-start.39
  370.0 8.2 %collective-permute-start.42 = (f32[16,8192]{1,0:T(8,128)S(1)}, f32[16,8192]{1,0:T(8,128)S(1)}, u32[]{:S(2)}, u32[]{:S(2)}) collective-permute-start(f32[16,8192]{1,0:T(8,128)S(1)} %get-tuple-element.144.mine_ref), channel_id=1, source_target_pairs={{0,4},{4,0},{8,12},{12,8},{16,20},{20,16},{24,28},{28,24},{32,36},... | collective-permute-start | bytes 1572872 | tf_op jit(solution)/shard_map/ppermute | solution.py:411
  374.6 1.6 collective-permute-start.43
  376.2 3.0 collective-permute-start.46
  376.5 4.4 %collective-permute-start.45 = (f32[16,640]{1,0:T(8,128)S(1)}, f32[16,640]{1,0:T(8,128)S(1)}, u32[]{:S(2)}, u32[]{:S(2)}) collective-permute-start(f32[16,640]{1,0:T(8,128)S(1)} %shard_map.146.refs_0_), channel_id=1, source_target_pairs={{0,2},{1,3},{2,0},{3,1},{4,6},{5,7},{6,4},{7,5},{8,10},{9,11},{10,... | collective-permute-start | bytes 122888 | tf_op jit(solution)/shard_map/ppermute | solution.py:417
  377.4 4.1 collective-permute-start.44
  405.5 6.0 %collective-permute-start.47 = (f32[16,8192]{1,0:T(8,128)S(1)}, f32[16,8192]{1,0:T(8,128)S(1)}, u32[]{:S(2)}, u32[]{:S(2)}) collective-permute-start(f32[16,8192]{1,0:T(8,128)S(1)} %shard_map.149.mine_ref), channel_id=1, source_target_pairs={{0,4},{4,0},{8,12},{12,8},{16,20},{20,16},{24,28},{28,24},{32,36},... | collective-permute-start | bytes 1572872 | tf_op jit(solution)/shard_map/ppermute | solution.py:411

commit v2 on v1

--- a/solution.py
+++ b/solution.py
@@ -15,7 +15,8 @@
 CHUNKS = 4
 GROUP = 4
 WIDE = 8
-AHEAD = 3
+DEEP = 8
+LOAD = 44
 
 F32 = jnp.float32
 BF16 = jnp.bfloat16
@@ -45,58 +46,59 @@
     return [(a, VMEM) for a in arrays]
 
 
-def prepare(design, start):
+def load(design):
     rows, width = design.shape
     half = width // 2
+
+    def body(design_ref, own_ref, away_ref, sems):
+        core = lax.rem(lax.axis_index("rows"), 2)
+        copies = []
+        for n, (side, target) in enumerate(((1 - core, away_ref), (core, own_ref))):
+            source = design_ref.at[:, pl.ds(pl.multiple_of(side * half, half), half)]
+            copies.append(pltpu.make_async_copy(source, target, sems.at[n]))
+            copies[n].start()
+        for copy in copies:
+            copy.wait()
+
+    piece = ((rows, half), design.dtype)
+    ins = [(design, HBM)]
+    return call(body, ins, [piece, piece], [pltpu.SemaphoreType.DMA((2,))], 0, LOAD)
+
+
+def start_margins(own, away, start):
+    rows, half = own.shape
     step = half // CHUNKS
 
-    def body(start_ref, design_ref, margins_ref, own_ref, away_ref, q_ref, far_ref, sems):
+    def body(own_ref, away_ref, start_ref, margins_ref, q_ref):
         core = lax.rem(lax.axis_index("rows"), 2)
-        near = core * half
-        far = (1 - core) * half
-        count = [0]
-
-        def fetch(source, target):
-            copy = pltpu.make_async_copy(source, target, sems.at[count[0]])
-            count[0] += 1
-            copy.start()
-            return copy
-
-        def cols(offset, size):
-            return pl.ds(pl.multiple_of(offset, step), size)
-
-        first = [
-            fetch(start_ref.at[:, cols(far, half)], far_ref),
-            fetch(start_ref.at[:, cols(near, half)], q_ref),
-        ]
-        pieces = []
-        for offset, target, coefs in ((far, away_ref, far_ref), (near, own_ref, q_ref)):
-            for i in range(CHUNKS):
-                here = slice(i * step, (i + 1) * step)
-                source = design_ref.at[:, cols(offset + i * step, step)]
-                pieces.append((source, target.at[:, pl.ds(i * step, step)], target, coefs, here))
-        flying = [fetch(*piece[:2]) for piece in pieces[:AHEAD]]
-        for copy in first:
-            copy.wait()
-        total = jnp.zeros((CHAINS, rows), F32)
-        for i, (_, _, target, coefs, here) in enumerate(pieces):
-            flying[i].wait()
-            if i + AHEAD < len(pieces):
-                flying.append(fetch(*pieces[i + AHEAD][:2]))
-            total = total + lax.dot_general(
-                coefs[:, here].astype(BF16), target[:, here], CROSS, preferred_element_type=F32
-            )
-        margins_ref[...] = total
-
-    piece = ((rows, half), design.dtype)
-    return call(
-        body,
-        [(start, HBM), (design, HBM)],
-        [((CHAINS, rows), F32), piece, piece, ((CHAINS, half), F32)],
-        [pltpu.VMEM((CHAINS, half), F32), pltpu.SemaphoreType.DMA((2 + 2 * CHUNKS,))],
-        2 * CHAINS * rows * width,
-        38,
-    )
+
+        def one(i, total):
+            here = pl.ds(pl.multiple_of(i * step, step), step)
+            near = start_ref[:, pl.ds(pl.multiple_of(core * half + i * step, step), step)]
+            far = start_ref[:, pl.ds(pl.multiple_of((1 - core) * half + i * step, step), step)]
+            q_ref[:, here] = near
+            for value, ref in ((near, own_ref), (far, away_ref)):
+                total = total + lax.dot_general(
+                    value.astype(BF16), ref[:, here], CROSS, preferred_element_type=F32
+                )
+            return total
+
+        margins_ref[...] = lax.fori_loop(0, CHUNKS, one, jnp.zeros((CHAINS, rows), F32))
+
+    outs = [((CHAINS, rows), F32), ((CHAINS, half), F32)]
+    flops = 4 * CHAINS * rows * half
+    return call(body, vmem(own, away, start), outs, flops=flops)
+
+
+def total_of(own, one, two, three):
+    return (own + two) + (one + three)
+
+
+def ring_sum(partials):
+    def body(own, one, two, three, out_ref):
+        out_ref[...] = total_of(own[...], one[...], two[...], three[...])
+
+    return call(body, vmem(*partials), [(partials[0].shape, F32)])[0]
 
 
 def draw(labels, momenta, lag_offsets, accept_bits, step_sizes):
@@ -122,10 +124,16 @@
             keep_ref[...] = keep
         sign_ref[...] = jnp.broadcast_to(label_ref[...].astype(F32), (8, rows))
         copy.wait()
-        for s, out_ref in enumerate((mom0_ref, mom1_ref)):
-            for k in range(PAIRS):
-                out_ref[2 * k : 2 * k + 1] = draws_ref[k, pl.ds(s + lag_ref[k], 1)]
-                out_ref[2 * k + 1 : 2 * k + 2] = draws_ref[k, s : s + 1]
+
+        def pick(i, carry):
+            here = pl.ds(pl.multiple_of(i * (half // 8), half // 8), half // 8)
+            for s, out_ref in enumerate((mom0_ref, mom1_ref)):
+                for k in range(PAIRS):
+                    out_ref[2 * k : 2 * k + 1, here] = draws_ref[k, pl.ds(s + lag_ref[k], 1), here]
+                    out_ref[2 * k + 1 : 2 * k + 2, here] = draws_ref[k, s : s + 1, here]
+            return carry
+
+        lax.fori_loop(0, 8, pick, 0)
 
     small = ((CHAINS, EXTRA), F32)
     state = ((CHAINS, half), F32)
@@ -209,8 +217,10 @@
     return jnp.sum(gap * gap, axis=1, keepdims=True)
 
 
-def margins_kernel(mode, flipped, arrived, h, state):
-    width, rows = flipped[0].shape
+def margins_kernel(mode, pieces, arrived, h, state):
+    flipped = pieces[0].shape[0] > pieces[0].shape[1]
+    rows = min(pieces[0].shape)
+    width = max(pieces[0].shape)
     blocks, _, block = arrived.shape
     names = list(state)
     wide = ((CHAINS, width), F32)
@@ -256,19 +266,27 @@
         def group(i, carry):
             own, other, gap = carry
             rounded = []
-            for j in range(GROUP):
-                b = i * GROUP + j
+            for j in range(DEEP):
+                b = i * DEEP + j
                 part, gap = one(b, pl.ds(pl.multiple_of(b * block, block), block), gap)
                 rounded.append(part)
             rounded = jnp.concatenate(rounded, axis=1)
-            cols = pl.ds(pl.multiple_of(i * (GROUP * block), GROUP * block), GROUP * block)
-            own = own + jnp.dot(rounded, own_ref[cols], preferred_element_type=F32)
-            other = other + jnp.dot(rounded, other_ref[cols], preferred_element_type=F32)
+            cols = pl.ds(pl.multiple_of(i * (DEEP * block), DEEP * block), DEEP * block)
+            if flipped:
+                own = own + jnp.dot(rounded, own_ref[cols], preferred_element_type=F32)
+                other = other + jnp.dot(rounded, other_ref[cols], preferred_element_type=F32)
+            else:
+                own = own + lax.dot_general(
+                    rounded, own_ref[:, cols], CROSS, preferred_element_type=F32
+                )
+                other = other + lax.dot_general(
+                    rounded, other_ref[:, cols], CROSS, preferred_element_type=F32
+                )
             return own, other, gap
 
         zero = jnp.zeros((CHAINS, rows), F32)
         *total, gap = lax.fori_loop(
-            0, blocks // GROUP, group, (zero, zero, jnp.zeros((CHAINS, 1), F32))
+            0, blocks // DEEP, group, (zero, zero, jnp.zeros((CHAINS, 1), F32))
         )
         if mode == "turn":
             out["gap"][...] = jnp.broadcast_to(gap, (CHAINS, EXTRA))
@@ -280,7 +298,7 @@
 
     result = call(
         body,
-        vmem(*flipped, arrived, h, *state.values()),
+        vmem(*pieces, arrived, h, *state.values()),
         list(outs.values()),
         flops=4 * CHAINS * rows * width,
     )
@@ -303,11 +321,12 @@
     extended = earlier is not None
 
     def body(*refs):
-        own, one, two, three, mine_ref, theirs_ref, near_ref, far_ref = refs[:8]
-        rest = list(refs[8:])
+        sums = [ref[...] for ref in refs[: len(partials)]]
+        mine_ref, theirs_ref, near_ref, far_ref = refs[len(partials) : len(partials) + 4]
+        rest = list(refs[len(partials) + 4 :])
         earlier_ref = rest.pop(0) if extended else None
         out_ref = rest.pop(0)
-        total = (own[...] + two[...]) + (one[...] + three[...])
+        total = total_of(*sums) if len(sums) > 1 else sums[0]
         sign = jnp.concatenate([mine_ref[:1], theirs_ref[:1]], axis=1)
         signed = sign * total[:, : 2 * rows]
         weights = (sign * jax.nn.sigmoid(-signed)).astype(BF16)
@@ -417,54 +436,61 @@
             moved[k] = lax.ppermute(margins, "feat", pairs)
         return [margins, moved[1], moved[2], moved[3]]
 
-    def gradient(margins, residual, likes=False, earlier=None, beside=None):
+    def gradient(partials, residual, likes=False, earlier=None, beside=()):
         last = earlier is not None
-        out, *side = terms_kernel(around(margins), signs, held, blocks, likes, earlier)
-        if beside is not None:
-            out, beside = lax.optimization_barrier((out, beside))
+        out, *side = terms_kernel(partials, signs, held, blocks, likes, earlier)
+        out, *beside = lax.optimization_barrier((out, *beside))
         block = out.shape[2] - (EXTRA if last else 0)
         send, residual, *totals = sum_kernel(
             exchange(out), residual, block, rows * devices if last else 0
         )
-        return exchange(send), residual, side + totals + ([] if beside is None else [beside])
+        return exchange(send), residual, side + totals + beside
 
     def paired(margins):
-        return pair_sum(margins, across(margins), rows)
-
-    margins, own, away, start = prepare(design, start_position)
-    swapped = across(margins)
-    away, swapped = lax.optimization_barrier((away, swapped))
-    margins = pair_start(margins, swapped)
+        return around(pair_sum(margins, across(margins), rows))
+
+    own, away = load(design)
     held = (own, across(away))
+    margins, start = start_margins(own, away, start_position)
     mom0, mom1, h, keep0, keep1, sign = draw(labels, momenta, lag_offsets, accept_bits, step_sizes)
-    sign, own_flipped = lax.optimization_barrier((sign, flip(own)))
     signs = (sign, across(sign))
-    g0, residual, (far_flipped,) = gradient(margins, None, beside=flip(held[1]))
-    flipped = (own_flipped, far_flipped)
+    margins = ring_sum(around(margins))
+    margins = pair_start(margins, across(margins))
+    g0, residual, (mom0, mom1) = gradient([margins], None, beside=(mom0, mom1))
     g = g0
+    pieces = held
+    flips = []
     now = {"q": start}
     for leap in range(LEAP):
         if leap == 0:
-            now = margins_kernel("first", flipped, g, h, {"q": start, "mom": mom0})
+            now = margins_kernel("first", pieces, g, h, {"q": start, "mom": mom0})
         else:
-            now = margins_kernel("mid", flipped, g, h, {"q": now["q"], "p": now["p"]})
-        g, residual, side = gradient(paired(now["margins"]), residual, likes=leap + 1 == LEAP)
+            now = margins_kernel("mid", pieces, g, h, {"q": now["q"], "p": now["p"]})
+        partials = paired(now["margins"])
+        beside = (flip(held[leap]),) if leap < len(held) else ()
+        g, residual, side = gradient(partials, residual, leap + 1 == LEAP, beside=beside)
+        if beside:
+            flips += side
+        if len(flips) == len(held):
+            pieces = tuple(flips)
     (like,) = side
     for leap in range(LEAP):
         last = leap + 1 == LEAP
         if leap == 0:
             state = {"q": now["q"], "q0": start, "g0": g0, "mom": mom1, "keep": keep0}
-            now = margins_kernel("turn", flipped, g, h, state)
+            now = margins_kernel("turn", pieces, g, h, state)
             position, gap = now["pos"], now["gap"]
         elif not last:
-            now = margins_kernel("mid", flipped, g, h, {"q": now["q"], "p": now["p"]})
+            now = margins_kernel("mid", pieces, g, h, {"q": now["q"], "p": now["p"]})
         else:
             state = {"q": now["q"], "p": now["p"], "pos": position, "gap": gap, "keep": keep1}
-            now = margins_kernel("last", flipped, g, h, state)
+            now = margins_kernel("last", pieces, g, h, state)
             final_position = assemble(now["pos"], across(now["pos"]))
             sign, final_position = lax.optimization_barrier((sign, final_position))
             signs = (sign, signs[1])
-        g, residual, side = gradient(paired(now["margins"]), residual, last, like if last else None)
+        g, residual, side = gradient(
+            paired(now["margins"]), residual, last, like if last else None
+        )
     distances, likes = side
     momentum = finish_kernel(g, h, now["p"], now["q"])
     return (final_position, assemble(momentum, across(momentum)), likes, distances)

time: 414 us -> 411 us (level)
    pallas_call x48 -> x50, Pallas kernels: 44.5 us -> 44.3 us  [call(): pl.pallas_call(body, in_specs=[spec for _, spec in ins], out_specs=[VMEM]...]
  transfers between devices with their start and end apart: 48 -> 48, of which waited for: 40 -> 41; matrix products, arithmetic and copies ran while one was open for 0% -> 0% of each run, Pallas kernels for 1% -> 2%
where the time goes in v2:
time: 411 us; the launch traced here: 410 us
  blocking collectives  239 us (58%)
  starting transfers between devices  76.6 us (19%)
  waiting for transfers between devices  47.1 us (11%)
  Pallas kernels  46.2 us (11%)
    all_to_all x22, blocking collectives, exchange(): return lax.all_to_all(blocked, 'rows', 0, 0, axis_index_groups=chips)  239 us
    ppermute x15, starting transfers between devices, across(): return lax.ppermute(value, 'rows', swap)  51.8 us
    pallas_call x50, Pallas kernels, call(): pl.pallas_call(body, in_specs=[spec for _, spec in ins], out_specs=[VMEM]...  44.3 us
    ppermute x33, waiting for transfers between devices, around(): moved[k] = lax.ppermute(margins, 'feat', pairs)  35.2 us
    ppermute x33, starting transfers between devices, around(): moved[k] = lax.ppermute(margins, 'feat', pairs)  24.8 us
    ppermute x15, waiting for transfers between devices, across(): return lax.ppermute(value, 'rows', swap)  11.9 us
  transfers between devices with their start and end apart: 48, of which 41 were waited for; matrix products, arithmetic and copies ran while one was open for 0% of the time, Pallas kernels for 2%

profile of v2, /device:TPU:1, one launch (start us, length us, event | category | flops | bytes accessed | tf_op | source)
XLA Modules:
  0.0 409.8 jit_solution(15092067544890234918)
XLA Ops:
  0.6 3.6 shard_map.103
  4.2 1.5 collective-permute-start
  5.7 2.6 shard_map.104
  8.3 3.9 collective-permute-start.3
  13.1 3.2 collective-permute-done.2.two
  16.3 1.6 collective-permute-start.4
  21.6 14.3 %all_to_all.110.refs_0_ = bf16[16,16,512]{2,1,0:T(8,128)(2,1)S(1)} all-to-all(bf16[16,16,512]{2,1,0:T(8,128)(2,1)S(1)} %shard_map.107), channel_id=1, replica_groups={{0,8,16,24,32,40,48,56,64,72,80,88,96,104,112,120},{4,12,20,28,36,44,52..., dimensions={0} | all-to-all | bytes 524288 | tf_op jit(solution)/shard_map/all_to_all | solution.py:427
  36.0 10.9 %all_to_all.111.arrived_ref.refs_2_ = bf16[16,16,512]{2,1,0:T(8,128)(2,1)S(1)} all-to-all(bf16[16,16,512]{2,1,0:T(8,128)(2,1)S(1)} %get-tuple-element.88), channel_id=1, replica_groups={{0,8,16,24,32,40,48,56,64,72,80,88,96,104,112,120},{4,12,20,28,36,44,52..., dimensions={0} | all-to-all | bytes 524288 | tf_op jit(solution)/shard_map/all_to_all | solution.py:427
  46.8 2.5 shard_map.109
  49.3 2.8 collective-permute-start.6
  55.5 2.0 shard_map.112.own_ref
  57.7 1.4 collective-permute-done.7.refs_1_
  60.4 10.5 %all_to_all.112.refs_0_ = bf16[16,16,512]{2,1,0:T(8,128)(2,1)S(1)} all-to-all(bf16[16,16,512]{2,1,0:T(8,128)(2,1)S(1)} %shard_map.111), channel_id=1, replica_groups={{0,8,16,24,32,40,48,56,64,72,80,88,96,104,112,120},{4,12,20,28,36,44,52..., dimensions={0} | all-to-all | bytes 524288 | tf_op jit(solution)/shard_map/all_to_all | solution.py:427
  71.0 10.8 %all_to_all.113.arrived_ref = bf16[16,16,512]{2,1,0:T(8,128)(2,1)S(1)} all-to-all(bf16[16,16,512]{2,1,0:T(8,128)(2,1)S(1)} %get-tuple-element.96), channel_id=1, replica_groups={{0,8,16,24,32,40,48,56,64,72,80,88,96,104,112,120},{4,12,20,28,36,44,52..., dimensions={0} | all-to-all | bytes 524288 | tf_op jit(solution)/shard_map/all_to_all | solution.py:427
  81.8 2.5 shard_map.114
  84.3 4.0 collective-permute-start.10
  90.9 2.0 shard_map.117.other_ref
  92.9 1.6 collective-permute-done.12.refs_2_
  96.2 10.6 %all_to_all.114.refs_0_ = bf16[16,16,512]{2,1,0:T(8,128)(2,1)S(1)} all-to-all(bf16[16,16,512]{2,1,0:T(8,128)(2,1)S(1)} %shard_map.116), channel_id=1, replica_groups={{0,8,16,24,32,40,48,56,64,72,80,88,96,104,112,120},{4,12,20,28,36,44,52..., dimensions={0} | all-to-all | bytes 524288 | tf_op jit(solution)/shard_map/all_to_all | solution.py:427
  106.8 10.7 %all_to_all.115.arrived_ref = bf16[16,16,512]{2,1,0:T(8,128)(2,1)S(1)} all-to-all(bf16[16,16,512]{2,1,0:T(8,128)(2,1)S(1)} %get-tuple-element.103), channel_id=1, replica_groups={{0,8,16,24,32,40,48,56,64,72,80,88,96,104,112,120},{4,12,20,28,36,44,52..., dimensions={0} | all-to-all | bytes 524288 | tf_op jit(solution)/shard_map/all_to_all | solution.py:427
  118.9 4.6 %collective-permute-start.14 = (f32[16,512]{1,0:T(8,128)S(1)}, f32[16,512]{1,0:T(8,128)S(1)}, u32[]{:S(2)}, u32[]{:S(2)}) collective-permute-start(f32[16,512]{1,0:T(8,128)S(1)} %get-tuple-element.106.mine_ref), channel_id=1, source_target_pairs={{0,4},{4,0},{8,12},{12,8},{16,20},{20,16},{24,28},{28,24},{32,36},... | collective-permute-start | bytes 98312 | tf_op jit(solution)/shard_map/ppermute | solution.py:430
  127.2 2.4 collective-permute-done.16.refs_2_
  131.3 10.6 %all_to_all.116.refs_0_ = bf16[16,16,512]{2,1,0:T(8,128)(2,1)S(1)} all-to-all(bf16[16,16,512]{2,1,0:T(8,128)(2,1)S(1)} %shard_map.121), channel_id=1, replica_groups={{0,8,16,24,32,40,48,56,64,72,80,88,96,104,112,120},{4,12,20,28,36,44,52..., dimensions={0} | all-to-all | bytes 524288 | tf_op jit(solution)/shard_map/all_to_all | solution.py:427
  141.9 10.7 %all_to_all.117.arrived_ref = bf16[16,16,512]{2,1,0:T(8,128)(2,1)S(1)} all-to-all(bf16[16,16,512]{2,1,0:T(8,128)(2,1)S(1)} %get-tuple-element.108), channel_id=1, replica_groups={{0,8,16,24,32,40,48,56,64,72,80,88,96,104,112,120},{4,12,20,28,36,44,52..., dimensions={0} | all-to-all | bytes 524288 | tf_op jit(solution)/shard_map/all_to_all | solution.py:427
  152.7 1.4 shard_map.123
  154.1 4.6 %collective-permute-start.18 = (f32[16,512]{1,0:T(8,128)S(1)}, f32[16,512]{1,0:T(8,128)S(1)}, u32[]{:S(2)}, u32[]{:S(2)}) collective-permute-start(f32[16,512]{1,0:T(8,128)S(1)} %get-tuple-element.111.mine_ref), channel_id=1, source_target_pairs={{0,4},{4,0},{8,12},{12,8},{16,20},{20,16},{24,28},{28,24},{32,36},... | collective-permute-start | bytes 98312 | tf_op jit(solution)/shard_map/ppermute | solution.py:430
  162.3 2.6 collective-permute-done.20.refs_2_
  166.6 10.6 %all_to_all.118.refs_0_ = bf16[16,16,512]{2,1,0:T(8,128)(2,1)S(1)} all-to-all(bf16[16,16,512]{2,1,0:T(8,128)(2,1)S(1)} %shard_map.125), channel_id=1, replica_groups={{0,8,16,24,32,40,48,56,64,72,80,88,96,104,112,120},{4,12,20,28,36,44,52..., dimensions={0} | all-to-all | bytes 524288 | tf_op jit(solution)/shard_map/all_to_all | solution.py:427
  177.2 10.7 %all_to_all.119.arrived_ref = bf16[16,16,512]{2,1,0:T(8,128)(2,1)S(1)} all-to-all(bf16[16,16,512]{2,1,0:T(8,128)(2,1)S(1)} %get-tuple-element.113), channel_id=1, replica_groups={{0,8,16,24,32,40,48,56,64,72,80,88,96,104,112,120},{4,12,20,28,36,44,52..., dimensions={0} | all-to-all | bytes 524288 | tf_op jit(solution)/shard_map/all_to_all | solution.py:427
  188.0 2.0 shard_map.127
  190.0 4.6 %collective-permute-start.22 = (f32[16,512]{1,0:T(8,128)S(1)}, f32[16,512]{1,0:T(8,128)S(1)}, u32[]{:S(2)}, u32[]{:S(2)}) collective-permute-start(f32[16,512]{1,0:T(8,128)S(1)} %get-tuple-element.116.mine_ref), channel_id=1, source_target_pairs={{0,4},{4,0},{8,12},{12,8},{16,20},{20,16},{24,28},{28,24},{32,36},... | collective-permute-start | bytes 98312 | tf_op jit(solution)/shard_map/ppermute | solution.py:430
  198.2 2.4 collective-permute-done.24.refs_2_
  201.0 1.4 shard_map.129
  202.4 10.6 %all_to_all.120.refs_0_ = bf16[16,16,512]{2,1,0:T(8,128)(2,1)S(1)} all-to-all(bf16[16,16,512]{2,1,0:T(8,128)(2,1)S(1)} %get-tuple-element.117), channel_id=1, replica_groups={{0,8,16,24,32,40,48,56,64,72,80,88,96,104,112,120},{4,12,20,28,36,44,52..., dimensions={0} | all-to-all | bytes 524288 | tf_op jit(solution)/shard_map/all_to_all | solution.py:427
  213.1 10.7 %all_to_all.121.arrived_ref = bf16[16,16,512]{2,1,0:T(8,128)(2,1)S(1)} all-to-all(bf16[16,16,512]{2,1,0:T(8,128)(2,1)S(1)} %get-tuple-element.119), channel_id=1, replica_groups={{0,8,16,24,32,40,48,56,64,72,80,88,96,104,112,120},{4,12,20,28,36,44,52..., dimensions={0} | all-to-all | bytes 524288 | tf_op jit(solution)/shard_map/all_to_all | solution.py:427
  223.8 1.4 shard_map.131
  225.2 4.6 %collective-permute-start.26 = (f32[16,512]{1,0:T(8,128)S(1)}, f32[16,512]{1,0:T(8,128)S(1)}, u32[]{:S(2)}, u32[]{:S(2)}) collective-permute-start(f32[16,512]{1,0:T(8,128)S(1)} %get-tuple-element.123.mine_ref), channel_id=1, source_target_pairs={{0,4},{4,0},{8,12},{12,8},{16,20},{20,16},{24,28},{28,24},{32,36},... | collective-permute-start | bytes 98312 | tf_op jit(solution)/shard_map/ppermute | solution.py:430
  233.5 2.6 collective-permute-done.28.refs_2_
  237.7 10.6 %all_to_all.122.refs_0_ = bf16[16,16,512]{2,1,0:T(8,128)(2,1)S(1)} all-to-all(bf16[16,16,512]{2,1,0:T(8,128)(2,1)S(1)} %shard_map.133), channel_id=1, replica_groups={{0,8,16,24,32,40,48,56,64,72,80,88,96,104,112,120},{4,12,20,28,36,44,52..., dimensions={0} | all-to-all | bytes 524288 | tf_op jit(solution)/shard_map/all_to_all | solution.py:427
  248.4 10.7 %all_to_all.123.arrived_ref = bf16[16,16,512]{2,1,0:T(8,128)(2,1)S(1)} all-to-all(bf16[16,16,512]{2,1,0:T(8,128)(2,1)S(1)} %get-tuple-element.125), channel_id=1, replica_groups={{0,8,16,24,32,40,48,56,64,72,80,88,96,104,112,120},{4,12,20,28,36,44,52..., dimensions={0} | all-to-all | bytes 524288 | tf_op jit(solution)/shard_map/all_to_all | solution.py:427
  259.1 1.4 shard_map.135
  260.5 4.6 %collective-permute-start.30 = (f32[16,512]{1,0:T(8,128)S(1)}, f32[16,512]{1,0:T(8,128)S(1)}, u32[]{:S(2)}, u32[]{:S(2)}) collective-permute-start(f32[16,512]{1,0:T(8,128)S(1)} %get-tuple-element.128.mine_ref), channel_id=1, source_target_pairs={{0,4},{4,0},{8,12},{12,8},{16,20},{20,16},{24,28},{28,24},{32,36},... | collective-permute-start | bytes 98312 | tf_op jit(solution)/shard_map/ppermute | solution.py:430
  268.8 2.5 collective-permute-done.32.refs_2_
  272.9 10.6 %all_to_all.124.refs_0_ = bf16[16,16,512]{2,1,0:T(8,128)(2,1)S(1)} all-to-all(bf16[16,16,512]{2,1,0:T(8,128)(2,1)S(1)} %shard_map.137), channel_id=1, replica_groups={{0,8,16,24,32,40,48,56,64,72,80,88,96,104,112,120},{4,12,20,28,36,44,52..., dimensions={0} | all-to-all | bytes 524288 | tf_op jit(solution)/shard_map/all_to_all | solution.py:427
  283.6 10.7 %all_to_all.125.arrived_ref = bf16[16,16,512]{2,1,0:T(8,128)(2,1)S(1)} all-to-all(bf16[16,16,512]{2,1,0:T(8,128)(2,1)S(1)} %get-tuple-element.130), channel_id=1, replica_groups={{0,8,16,24,32,40,48,56,64,72,80,88,96,104,112,120},{4,12,20,28,36,44,52..., dimensions={0} | all-to-all | bytes 524288 | tf_op jit(solution)/shard_map/all_to_all | solution.py:427
  294.3 1.4 shard_map.139
  295.7 4.6 %collective-permute-start.34 = (f32[16,512]{1,0:T(8,128)S(1)}, f32[16,512]{1,0:T(8,128)S(1)}, u32[]{:S(2)}, u32[]{:S(2)}) collective-permute-start(f32[16,512]{1,0:T(8,128)S(1)} %get-tuple-element.133.mine_ref), channel_id=1, source_target_pairs={{0,4},{4,0},{8,12},{12,8},{16,20},{20,16},{24,28},{28,24},{32,36},... | collective-permute-start | bytes 98312 | tf_op jit(solution)/shard_map/ppermute | solution.py:430
  304.0 2.6 collective-permute-done.36.refs_2_
  308.2 10.6 %all_to_all.126.refs_0_ = bf16[16,16,512]{2,1,0:T(8,128)(2,1)S(1)} all-to-all(bf16[16,16,512]{2,1,0:T(8,128)(2,1)S(1)} %shard_map.141), channel_id=1, replica_groups={{0,8,16,24,32,40,48,56,64,72,80,88,96,104,112,120},{4,12,20,28,36,44,52..., dimensions={0} | all-to-all | bytes 524288 | tf_op jit(solution)/shard_map/all_to_all | solution.py:427
  318.9 10.7 %all_to_all.127.arrived_ref = bf16[16,16,512]{2,1,0:T(8,128)(2,1)S(1)} all-to-all(bf16[16,16,512]{2,1,0:T(8,128)(2,1)S(1)} %get-tuple-element.135), channel_id=1, replica_groups={{0,8,16,24,32,40,48,56,64,72,80,88,96,104,112,120},{4,12,20,28,36,44,52..., dimensions={0} | all-to-all | bytes 524288 | tf_op jit(solution)/shard_map/all_to_all | solution.py:427
  329.6 1.4 shard_map.143
  331.0 4.6 %collective-permute-start.38 = (f32[16,512]{1,0:T(8,128)S(1)}, f32[16,512]{1,0:T(8,128)S(1)}, u32[]{:S(2)}, u32[]{:S(2)}) collective-permute-start(f32[16,512]{1,0:T(8,128)S(1)} %get-tuple-element.138.mine_ref), channel_id=1, source_target_pairs={{0,4},{4,0},{8,12},{12,8},{16,20},{20,16},{24,28},{28,24},{32,36},... | collective-permute-start | bytes 98312 | tf_op jit(solution)/shard_map/ppermute | solution.py:430
  339.2 2.5 collective-permute-done.40.refs_2_
  343.4 10.6 %all_to_all.128.refs_0_ = bf16[16,16,512]{2,1,0:T(8,128)(2,1)S(1)} all-to-all(bf16[16,16,512]{2,1,0:T(8,128)(2,1)S(1)} %shard_map.145), channel_id=1, replica_groups={{0,8,16,24,32,40,48,56,64,72,80,88,96,104,112,120},{4,12,20,28,36,44,52..., dimensions={0} | all-to-all | bytes 524288 | tf_op jit(solution)/shard_map/all_to_all | solution.py:427
  354.0 10.7 %all_to_all.129.arrived_ref = bf16[16,16,512]{2,1,0:T(8,128)(2,1)S(1)} all-to-all(bf16[16,16,512]{2,1,0:T(8,128)(2,1)S(1)} %get-tuple-element.140), channel_id=1, replica_groups={{0,8,16,24,32,40,48,56,64,72,80,88,96,104,112,120},{4,12,20,28,36,44,52..., dimensions={0} | all-to-all | bytes 524288 | tf_op jit(solution)/shard_map/all_to_all | solution.py:427
  364.8 1.4 shard_map.147
  366.2 4.7 %collective-permute-start.42 = (f32[16,8192]{1,0:T(8,128)S(1)}, f32[16,8192]{1,0:T(8,128)S(1)}, u32[]{:S(2)}, u32[]{:S(2)}) collective-permute-start(f32[16,8192]{1,0:T(8,128)S(1)} %get-tuple-element.146.mine_ref), channel_id=1, source_target_pairs={{0,4},{4,0},{8,12},{12,8},{16,20},{20,16},{24,28},{28,24},{32,36},... | collective-permute-start | bytes 1572872 | tf_op jit(solution)/shard_map/ppermute | solution.py:430
  371.0 1.5 collective-permute-done.43.other_ref
  375.4 2.4 collective-permute-done.45.refs_2_
  378.3 1.5 shard_map.149
  379.8 10.9 %all_to_all.130.refs_0_ = bf16[16,16,640]{2,1,0:T(8,128)(2,1)S(1)} all-to-all(bf16[16,16,640]{2,1,0:T(8,128)(2,1)S(1)} %get-tuple-element.151), channel_id=1, replica_groups={{0,8,16,24,32,40,48,56,64,72,80,88,96,104,112,120},{4,12,20,28,36,44,52..., dimensions={0} | all-to-all | bytes 655360 | tf_op jit(solution)/shard_map/all_to_all | solution.py:427
  391.4 10.8 %all_to_all.131.arrived_ref = bf16[16,16,512]{2,1,0:T(8,128)(2,1)S(1)} all-to-all(bf16[16,16,512]{2,1,0:T(8,128)(2,1)S(1)} %get-tuple-element.153), channel_id=1, replica_groups={{0,8,16,24,32,40,48,56,64,72,80,88,96,104,112,120},{4,12,20,28,36,44,52..., dimensions={0} | all-to-all | bytes 524288 | tf_op jit(solution)/shard_map/all_to_all | solution.py:427
  402.3 4.8 %collective-permute-start.47 = (f32[16,8192]{1,0:T(8,128)S(1)}, f32[16,8192]{1,0:T(8,128)S(1)}, u32[]{:S(2)}, u32[]{:S(2)}) collective-permute-start(f32[16,8192]{1,0:T(8,128)S(1)} %shard_map.151.mine_ref), channel_id=1, source_target_pairs={{0,4},{4,0},{8,12},{12,8},{16,20},{20,16},{24,28},{28,24},{32,36},... | collective-permute-start | bytes 1572872 | tf_op jit(solution)/shard_map/ppermute | solution.py:430
  407.1 1.5 collective-permute-done.47.other_ref
  (118 shorter events, 56.8 us)
Async XLA Ops:
  0.6 5.0 %copy-start.1 = (f32[16,16384]{1,0:T(8,128)S(1)}, f32[16,16384]{1,0:T(8,128)}, u32[]{:S(2)}) copy-start(f32[16,16384]{1,0:T(8,128)} %start_ref.1) | copy-start | bytes 3145732
  4.2 16.0 %collective-permute-start = (bf16[256,8192]{1,0:T(8,128)(2,1)S(1)}, bf16[256,8192]{1,0:T(8,128)(2,1)S(1)}, u32[]{:S(2)}, u32[]{:S(2)}) collective-permute-start(bf16[256,8192]{1,0:T(8,128)(2,1)S(1)} %get-tuple-element.83.away_ref), channel_id=1, source_target_pairs={{0,4},{4,0},{8,12},{12,8},{16,20},{20,16},{24,28},{28,24},{32,36},... | collective-permute-start | bytes 12582920 | tf_op jit(solution)/shard_map/ppermute | solution.py:430
  5.7 12.2 %copy-start = (f32[8,4,16384]{2,1,0:T(4,128)S(1)}, f32[8,4,16384]{2,1,0:T(4,128)}, u32[]{:S(2)}) copy-start(f32[8,4,16384]{2,1,0:T(4,128)} %bank_ref.1) | copy-start | bytes 6291460
  5.7 12.2 %copy-start.2 = (s32[2,16]{1,0:T(2,128)S(1)}, s32[2,16]{1,0:T(2,128)}, u32[]{:S(2)}) copy-start(s32[2,16]{1,0:T(2,128)} %accept_ref.1) | copy-start | bytes 388
  5.7 12.2 %copy-start.3 = (s32[256]{0:T(256)S(1)}, s32[256]{0:T(256)}, u32[]{:S(2)}) copy-start(s32[256]{0:T(256)} %param.8) | copy-start | bytes 3076
  5.7 12.2 %copy-start.4 = (s32[8]{0:T(128)S(1)}, s32[8]{0:T(128)}, u32[]{:S(2)}) copy-start(s32[8]{0:T(128)} %lag_ref.1) | copy-start | bytes 100
  5.7 12.2 %copy-start.5 = (f32[8]{0:T(128)S(1)}, f32[8]{0:T(128)}, u32[]{:S(2)}) copy-start(f32[8]{0:T(128)} %steps_ref.1) | copy-start | bytes 100
  8.3 4.8 %collective-permute-start.3 = (f32[16,256]{1,0:T(8,128)S(1)}, f32[16,256]{1,0:T(8,128)S(1)}, u32[]{:S(2)}, u32[]{:S(2)}) collective-permute-start(f32[16,256]{1,0:T(8,128)S(1)} %get-tuple-element.84.own), channel_id=1, source_target_pairs={{0,3},{1,0},{2,1},{3,2},{4,7},{5,4},{6,5},{7,6},{8,11},{9,8},{10,9... | collective-permute-start | bytes 49160 | tf_op jit(solution)/shard_map/ppermute | solution.py:436
  12.2 4.1 collective-permute-start.2
  12.2 4.1 collective-permute-start.1
  16.3 2.8 collective-permute-start.4
  19.0 1.3 collective-permute-start.5
  49.3 3.7 collective-permute-start.6
  53.0 4.6 %collective-permute-start.9 = (f32[16,512]{1,0:T(8,128)S(1)}, f32[16,512]{1,0:T(8,128)S(1)}, u32[]{:S(2)}, u32[]{:S(2)}) collective-permute-start(f32[16,512]{1,0:T(8,128)S(1)} %shard_map.110.refs_0_), channel_id=1, source_target_pairs={{0,3},{1,0},{2,1},{3,2},{4,7},{5,4},{6,5},{7,6},{8,11},{9,8},{10,9... | collective-permute-start | bytes 98312 | tf_op jit(solution)/shard_map/ppermute | solution.py:436
  53.4 4.3 %collective-permute-start.8 = (f32[16,512]{1,0:T(8,128)S(1)}, f32[16,512]{1,0:T(8,128)S(1)}, u32[]{:S(2)}, u32[]{:S(2)}) collective-permute-start(f32[16,512]{1,0:T(8,128)S(1)} %shard_map.110.refs_0_), channel_id=1, source_target_pairs={{0,2},{1,3},{2,0},{3,1},{4,6},{5,7},{6,4},{7,5},{8,10},{9,11},{10,... | collective-permute-start | bytes 98312 | tf_op jit(solution)/shard_map/ppermute | solution.py:436
  54.8 4.3 %collective-permute-start.7 = (f32[16,512]{1,0:T(8,128)S(1)}, f32[16,512]{1,0:T(8,128)S(1)}, u32[]{:S(2)}, u32[]{:S(2)}) collective-permute-start(f32[16,512]{1,0:T(8,128)S(1)} %shard_map.110.refs_0_), channel_id=1, source_target_pairs={{0,1},{1,2},{2,3},{3,0},{4,5},{5,6},{6,7},{7,4},{8,9},{9,10},{10,1... | collective-permute-start | bytes 98312 | tf_op jit(solution)/shard_map/ppermute | solution.py:436
  84.3 4.8 %collective-permute-start.10 = (f32[16,512]{1,0:T(8,128)S(1)}, f32[16,512]{1,0:T(8,128)S(1)}, u32[]{:S(2)}, u32[]{:S(2)}) collective-permute-start(f32[16,512]{1,0:T(8,128)S(1)} %get-tuple-element.99.mine_ref), channel_id=1, source_target_pairs={{0,4},{4,0},{8,12},{12,8},{16,20},{20,16},{24,28},{28,24},{32,36},... | collective-permute-start | bytes 98312 | tf_op jit(solution)/shard_map/ppermute | solution.py:430
  89.1 3.7 collective-permute-start.13
  90.2 4.3 %collective-permute-start.12 = (f32[16,512]{1,0:T(8,128)S(1)}, f32[16,512]{1,0:T(8,128)S(1)}, u32[]{:S(2)}, u32[]{:S(2)}) collective-permute-start(f32[16,512]{1,0:T(8,128)S(1)} %shard_map.115.refs_0_), channel_id=1, source_target_pairs={{0,2},{1,3},{2,0},{3,1},{4,6},{5,7},{6,4},{7,5},{8,10},{9,11},{10,... | collective-permute-start | bytes 98312 | tf_op jit(solution)/shard_map/ppermute | solution.py:436
  90.8 4.0 collective-permute-start.11
  118.9 5.5 %collective-permute-start.14 = (f32[16,512]{1,0:T(8,128)S(1)}, f32[16,512]{1,0:T(8,128)S(1)}, u32[]{:S(2)}, u32[]{:S(2)}) collective-permute-start(f32[16,512]{1,0:T(8,128)S(1)} %get-tuple-element.106.mine_ref), channel_id=1, source_target_pairs={{0,4},{4,0},{8,12},{12,8},{16,20},{20,16},{24,28},{28,24},{32,36},... | collective-permute-start | bytes 98312 | tf_op jit(solution)/shard_map/ppermute | solution.py:430
  124.4 2.8 collective-permute-start.17
  125.3 4.3 %collective-permute-start.16 = (f32[16,512]{1,0:T(8,128)S(1)}, f32[16,512]{1,0:T(8,128)S(1)}, u32[]{:S(2)}, u32[]{:S(2)}) collective-permute-start(f32[16,512]{1,0:T(8,128)S(1)} %shard_map.120.refs_0_), channel_id=1, source_target_pairs={{0,2},{1,3},{2,0},{3,1},{4,6},{5,7},{6,4},{7,5},{8,10},{9,11},{10,... | collective-permute-start | bytes 98312 | tf_op jit(solution)/shard_map/ppermute | solution.py:436
  125.9 4.0 collective-permute-start.15
  154.1 5.5 %collective-permute-start.18 = (f32[16,512]{1,0:T(8,128)S(1)}, f32[16,512]{1,0:T(8,128)S(1)}, u32[]{:S(2)}, u32[]{:S(2)}) collective-permute-start(f32[16,512]{1,0:T(8,128)S(1)} %get-tuple-element.111.mine_ref), channel_id=1, source_target_pairs={{0,4},{4,0},{8,12},{12,8},{16,20},{20,16},{24,28},{28,24},{32,36},... | collective-permute-start | bytes 98312 | tf_op jit(solution)/shard_map/ppermute | solution.py:430
  159.6 2.8 collective-permute-start.21
  160.6 4.3 %collective-permute-start.20 = (f32[16,512]{1,0:T(8,128)S(1)}, f32[16,512]{1,0:T(8,128)S(1)}, u32[]{:S(2)}, u32[]{:S(2)}) collective-permute-start(f32[16,512]{1,0:T(8,128)S(1)} %shard_map.124.refs_0_), channel_id=1, source_target_pairs={{0,2},{1,3},{2,0},{3,1},{4,6},{5,7},{6,4},{7,5},{8,10},{9,11},{10,... | collective-permute-start | bytes 98312 | tf_op jit(solution)/shard_map/ppermute | solution.py:436
  161.3 4.0 collective-permute-start.19
  190.0 5.5 %collective-permute-start.22 = (f32[16,512]{1,0:T(8,128)S(1)}, f32[16,512]{1,0:T(8,128)S(1)}, u32[]{:S(2)}, u32[]{:S(2)}) collective-permute-start(f32[16,512]{1,0:T(8,128)S(1)} %get-tuple-element.116.mine_ref), channel_id=1, source_target_pairs={{0,4},{4,0},{8,12},{12,8},{16,20},{20,16},{24,28},{28,24},{32,36},... | collective-permute-start | bytes 98312 | tf_op jit(solution)/shard_map/ppermute | solution.py:430
  195.4 2.8 collective-permute-start.25
  196.4 4.3 %collective-permute-start.24 = (f32[16,512]{1,0:T(8,128)S(1)}, f32[16,512]{1,0:T(8,128)S(1)}, u32[]{:S(2)}, u32[]{:S(2)}) collective-permute-start(f32[16,512]{1,0:T(8,128)S(1)} %shard_map.128.refs_0_), channel_id=1, source_target_pairs={{0,2},{1,3},{2,0},{3,1},{4,6},{5,7},{6,4},{7,5},{8,10},{9,11},{10,... | collective-permute-start | bytes 98312 | tf_op jit(solution)/shard_map/ppermute | solution.py:436
  197.0 4.0 collective-permute-start.23
  225.2 5.5 %collective-permute-start.26 = (f32[16,512]{1,0:T(8,128)S(1)}, f32[16,512]{1,0:T(8,128)S(1)}, u32[]{:S(2)}, u32[]{:S(2)}) collective-permute-start(f32[16,512]{1,0:T(8,128)S(1)} %get-tuple-element.123.mine_ref), channel_id=1, source_target_pairs={{0,4},{4,0},{8,12},{12,8},{16,20},{20,16},{24,28},{28,24},{32,36},... | collective-permute-start | bytes 98312 | tf_op jit(solution)/shard_map/ppermute | solution.py:430
  230.7 2.8 collective-permute-start.29
  231.8 4.3 %collective-permute-start.28 = (f32[16,512]{1,0:T(8,128)S(1)}, f32[16,512]{1,0:T(8,128)S(1)}, u32[]{:S(2)}, u32[]{:S(2)}) collective-permute-start(f32[16,512]{1,0:T(8,128)S(1)} %shard_map.132.refs_0_), channel_id=1, source_target_pairs={{0,2},{1,3},{2,0},{3,1},{4,6},{5,7},{6,4},{7,5},{8,10},{9,11},{10,... | collective-permute-start | bytes 98312 | tf_op jit(solution)/shard_map/ppermute | solution.py:436
  232.4 4.0 collective-permute-start.27
  260.5 5.5 %collective-permute-start.30 = (f32[16,512]{1,0:T(8,128)S(1)}, f32[16,512]{1,0:T(8,128)S(1)}, u32[]{:S(2)}, u32[]{:S(2)}) collective-permute-start(f32[16,512]{1,0:T(8,128)S(1)} %get-tuple-element.128.mine_ref), channel_id=1, source_target_pairs={{0,4},{4,0},{8,12},{12,8},{16,20},{20,16},{24,28},{28,24},{32,36},... | collective-permute-start | bytes 98312 | tf_op jit(solution)/shard_map/ppermute | solution.py:430
  266.0 2.8 collective-permute-start.33
  267.0 4.3 %collective-permute-start.32 = (f32[16,512]{1,0:T(8,128)S(1)}, f32[16,512]{1,0:T(8,128)S(1)}, u32[]{:S(2)}, u32[]{:S(2)}) collective-permute-start(f32[16,512]{1,0:T(8,128)S(1)} %shard_map.136.refs_0_), channel_id=1, source_target_pairs={{0,2},{1,3},{2,0},{3,1},{4,6},{5,7},{6,4},{7,5},{8,10},{9,11},{10,... | collective-permute-start | bytes 98312 | tf_op jit(solution)/shard_map/ppermute | solution.py:436
  267.6 4.0 collective-permute-start.31
  295.7 5.5 %collective-permute-start.34 = (f32[16,512]{1,0:T(8,128)S(1)}, f32[16,512]{1,0:T(8,128)S(1)}, u32[]{:S(2)}, u32[]{:S(2)}) collective-permute-start(f32[16,512]{1,0:T(8,128)S(1)} %get-tuple-element.133.mine_ref), channel_id=1, source_target_pairs={{0,4},{4,0},{8,12},{12,8},{16,20},{20,16},{24,28},{28,24},{32,36},... | collective-permute-start | bytes 98312 | tf_op jit(solution)/shard_map/ppermute | solution.py:430
  301.2 2.8 collective-permute-start.37
  302.3 4.3 %collective-permute-start.36 = (f32[16,512]{1,0:T(8,128)S(1)}, f32[16,512]{1,0:T(8,128)S(1)}, u32[]{:S(2)}, u32[]{:S(2)}) collective-permute-start(f32[16,512]{1,0:T(8,128)S(1)} %shard_map.140.refs_0_), channel_id=1, source_target_pairs={{0,2},{1,3},{2,0},{3,1},{4,6},{5,7},{6,4},{7,5},{8,10},{9,11},{10,... | collective-permute-start | bytes 98312 | tf_op jit(solution)/shard_map/ppermute | solution.py:436
  302.9 4.0 collective-permute-start.35
  331.0 5.5 %collective-permute-start.38 = (f32[16,512]{1,0:T(8,128)S(1)}, f32[16,512]{1,0:T(8,128)S(1)}, u32[]{:S(2)}, u32[]{:S(2)}) collective-permute-start(f32[16,512]{1,0:T(8,128)S(1)} %get-tuple-element.138.mine_ref), channel_id=1, source_target_pairs={{0,4},{4,0},{8,12},{12,8},{16,20},{20,16},{24,28},{28,24},{32,36},... | collective-permute-start | bytes 98312 | tf_op jit(solution)/shard_map/ppermute | solution.py:430
  336.5 2.8 collective-permute-start.41
  337.4 4.3 %collective-permute-start.40 = (f32[16,512]{1,0:T(8,128)S(1)}, f32[16,512]{1,0:T(8,128)S(1)}, u32[]{:S(2)}, u32[]{:S(2)}) collective-permute-start(f32[16,512]{1,0:T(8,128)S(1)} %shard_map.144.refs_0_), channel_id=1, source_target_pairs={{0,2},{1,3},{2,0},{3,1},{4,6},{5,7},{6,4},{7,5},{8,10},{9,11},{10,... | collective-permute-start | bytes 98312 | tf_op jit(solution)/shard_map/ppermute | solution.py:436
  338.0 4.0 collective-permute-start.39
  366.2 8.2 %collective-permute-start.42 = (f32[16,8192]{1,0:T(8,128)S(1)}, f32[16,8192]{1,0:T(8,128)S(1)}, u32[]{:S(2)}, u32[]{:S(2)}) collective-permute-start(f32[16,8192]{1,0:T(8,128)S(1)} %get-tuple-element.146.mine_ref), channel_id=1, source_target_pairs={{0,4},{4,0},{8,12},{12,8},{16,20},{20,16},{24,28},{28,24},{32,36},... | collective-permute-start | bytes 1572872 | tf_op jit(solution)/shard_map/ppermute | solution.py:430
  370.9 1.6 collective-permute-start.43
  372.5 3.0 collective-permute-start.46
  373.5 4.4 %collective-permute-start.45 = (f32[16,640]{1,0:T(8,128)S(1)}, f32[16,640]{1,0:T(8,128)S(1)}, u32[]{:S(2)}, u32[]{:S(2)}) collective-permute-start(f32[16,640]{1,0:T(8,128)S(1)} %shard_map.148.refs_0_), channel_id=1, source_target_pairs={{0,2},{1,3},{2,0},{3,1},{4,6},{5,7},{6,4},{7,5},{8,10},{9,11},{10,... | collective-permute-start | bytes 122888 | tf_op jit(solution)/shard_map/ppermute | solution.py:436
  374.1 4.2 %collective-permute-start.44 = (f32[16,640]{1,0:T(8,128)S(1)}, f32[16,640]{1,0:T(8,128)S(1)}, u32[]{:S(2)}, u32[]{:S(2)}) collective-permute-start(f32[16,640]{1,0:T(8,128)S(1)} %shard_map.148.refs_0_), channel_id=1, source_target_pairs={{0,1},{1,2},{2,3},{3,0},{4,5},{5,6},{6,7},{7,4},{8,9},{9,10},{10,1... | collective-permute-start | bytes 122888 | tf_op jit(solution)/shard_map/ppermute | solution.py:436
  402.3 6.3 %collective-permute-start.47 = (f32[16,8192]{1,0:T(8,128)S(1)}, f32[16,8192]{1,0:T(8,128)S(1)}, u32[]{:S(2)}, u32[]{:S(2)}) collective-permute-start(f32[16,8192]{1,0:T(8,128)S(1)} %shard_map.151.mine_ref), channel_id=1, source_target_pairs={{0,4},{4,0},{8,12},{12,8},{16,20},{20,16},{24,28},{28,24},{32,36},... | collective-permute-start | bytes 1572872 | tf_op jit(solution)/shard_map/ppermute | solution.py:430

commit v3 on v2

--- a/solution.py
+++ b/solution.py
@@ -229,7 +229,7 @@
         outs["pos"] = wide
         outs["gap"] = ((CHAINS, EXTRA), F32)
     if mode == "last":
-        outs["pos"] = wide
+        outs = {"margins": outs["margins"], "base": wide, "pos": wide}
 
     def body(own_ref, other_ref, arrived_ref, h_ref, *refs):
         ins = dict(zip(names, refs))
@@ -255,8 +255,11 @@
             else:
                 p = ins["p"][:, cols] + h_wide * (g - q)
             q = q + h_wide * p
-            out["p"][:, cols] = p
-            out["q"][:, cols] = q
+            if mode == "last":
+                out["base"][:, cols] = p - 0.5 * h_wide * q
+            else:
+                out["p"][:, cols] = p
+                out["q"][:, cols] = q
             if mode == "last":
                 pos = jnp.where(keep, q, ins["pos"][:, cols])
                 out["pos"][:, cols] = pos
@@ -338,14 +341,7 @@
                 side = side.astype(BF16)
                 for b in range(blocks):
                     out_ref[b, :, block:] = side
-                squares = total[:, 2 * rows :].T[:2]
-                chain = lax.broadcasted_iota(jnp.int32, (CHAINS, PAIRS), 0)
-                pair = lax.broadcasted_iota(jnp.int32, (CHAINS, PAIRS), 1)
-                leaders = (chain == 2 * pair).astype(F32)
-                picked = jnp.dot(
-                    squares, leaders, precision=lax.Precision.HIGHEST, preferred_element_type=F32
-                )
-                rest[0][...] = jnp.sqrt(picked / FEATURES + 1e-06)
+                rest[0][...] = total[:, 2 * rows :]
             else:
                 rest[0][...] = jnp.broadcast_to(like, (CHAINS, EXTRA))
 
@@ -364,7 +360,7 @@
 
     outs = [((blocks, CHAINS, block + (EXTRA if extended else 0)), BF16)]
     if likes:
-        outs.append(((TRANS, PAIRS) if extended else (CHAINS, EXTRA), F32))
+        outs.append(((CHAINS, EXTRA), F32))
     return call(
         body,
         vmem(*partials, *signs, *held, *([earlier] if extended else [])),
@@ -373,46 +369,86 @@
     )
 
 
-def sum_kernel(arrived, residual, block, observations):
+def sum_kernel(arrived, residual, block, likes):
     blocks = arrived.shape[0]
     carried = residual is not None
 
     def body(*refs):
         arrived_ref = refs[0]
-        send_ref, residual_ref = refs[2 if carried else 1 :][:2]
+        send_ref, second_ref = refs[2 if carried else 1 :]
         parts = [arrived_ref[b, :, :block].astype(F32) for b in range(blocks)]
         while len(parts) > 1:
             parts = [parts[i] + parts[i + 1] for i in range(0, len(parts), 2)]
         exact = parts[0] + refs[1][...] if carried else parts[0]
         send = exact.astype(BF16)
-        residual_ref[...] = exact - send.astype(F32)
+        if not likes:
+            second_ref[...] = exact - send.astype(F32)
         for b in range(blocks):
             send_ref[b] = send
-        if observations:
+        if likes:
             side = jnp.zeros((CHAINS, EXTRA), F32)
             for b in range(blocks):
                 side = side + arrived_ref[b, :, block:].astype(F32)
-            side = side.T
-            for s in range(TRANS):
-                like = (side[3 * s : 3 * s + 1] + side[3 * s + 1 : 3 * s + 2]) + side[3 * s + 2 : 3 * s + 3]
-                refs[-1][s : s + 1] = like / observations
-
-    outs = [((blocks, CHAINS, block), BF16), ((CHAINS, block), F32)]
-    if observations:
-        outs.append(((TRANS, CHAINS), F32))
+            second_ref[...] = side
+
+    outs = [((blocks, CHAINS, block), BF16), ((CHAINS, EXTRA if likes else block), F32)]
     return call(body, vmem(arrived, *([residual] if carried else [])), outs)
 
 
-def finish_kernel(arrived, h, p, q):
-    blocks, _, block = arrived.shape
-
-    def body(arrived_ref, h_ref, p_ref, q_ref, out_ref):
-        half = 0.5 * jnp.broadcast_to(h_ref[...][:, :1], (CHAINS, block))
-        for b in range(blocks):
-            cols = slice(b * block, (b + 1) * block)
-            out_ref[:, cols] = p_ref[:, cols] + half * (arrived_ref[b].astype(F32) - q_ref[:, cols])
-
-    return call(body, vmem(arrived, h, p, q), [((CHAINS, blocks * block), F32)])[0]
+def scores(squares, sides, observations):
+    def body(square_ref, side_ref, distance_ref, like_ref):
+        chain = lax.broadcasted_iota(jnp.int32, (CHAINS, PAIRS), 0)
+        pair = lax.broadcasted_iota(jnp.int32, (CHAINS, PAIRS), 1)
+        picked = jnp.dot(
+            square_ref[...].T[:TRANS],
+            (chain == 2 * pair).astype(F32),
+            precision=lax.Precision.HIGHEST,
+            preferred_element_type=F32,
+        )
+        distance_ref[...] = jnp.sqrt(picked / FEATURES + 1e-06)
+        side = side_ref[...].T
+        for s in range(TRANS):
+            high, middle, low = (side[3 * s + i : 3 * s + i + 1] for i in range(3))
+            like_ref[s : s + 1] = ((high + middle) + low) / observations
+
+    return call(body, vmem(squares, sides), [((TRANS, PAIRS), F32), ((TRANS, CHAINS), F32)])
+
+
+def finish_kernel(mine, other, half_step, base):
+    blocks, _, block = mine.shape
+    half = blocks * block
+
+    def body(mine_ref, other_ref, h_ref, mine_base, other_base, out_ref, held_ref, sems):
+        core = lax.rem(lax.axis_index("rows"), 2)
+        step = 0.5 * jnp.broadcast_to(h_ref[...][:, :1], (CHAINS, block))
+        copies = []
+        for n, (side, ref, base_ref) in enumerate(
+            ((core, mine_ref, mine_base), (1 - core, other_ref, other_base))
+        ):
+
+            def one(i, carry):
+                for j in range(GROUP):
+                    b = i * GROUP + j
+                    cols = pl.ds(pl.multiple_of(b * block, block), block)
+                    held_ref[n, :, cols] = base_ref[:, cols] + step * ref[b].astype(F32)
+                return carry
+
+            lax.fori_loop(0, blocks // GROUP, one, 0)
+            target = out_ref.at[:, pl.ds(pl.multiple_of(side * half, half), half)]
+            copies.append(pltpu.make_async_copy(held_ref.at[n], target, sems.at[n]))
+            copies[n].start()
+        for copy in copies:
+            copy.wait()
+
+    return pl.pallas_call(
+        body,
+        in_specs=[VMEM] * 5,
+        out_specs=HBM,
+        out_shape=jax.ShapeDtypeStruct((CHAINS, 2 * half), F32),
+        scratch_shapes=[pltpu.VMEM((2, CHAINS, half), F32), pltpu.SemaphoreType.DMA((2,))],
+        compiler_params=limit(6),
+        name="finish",
+    )(mine, other, half_step, *base)
 
 
 def on_device(design, labels, start_position, momenta, lag_offsets, accept_bits, step_sizes):
@@ -441,9 +477,8 @@
         out, *side = terms_kernel(partials, signs, held, blocks, likes, earlier)
         out, *beside = lax.optimization_barrier((out, *beside))
         block = out.shape[2] - (EXTRA if last else 0)
-        send, residual, *totals = sum_kernel(
-            exchange(out), residual, block, rows * devices if last else 0
-        )
+        send, second = sum_kernel(exchange(out), residual, block, last)
+        residual, totals = (None, [second]) if last else (second, [])
         return exchange(send), residual, side + totals + beside
 
     def paired(margins):
@@ -485,15 +520,22 @@
         else:
             state = {"q": now["q"], "p": now["p"], "pos": position, "gap": gap, "keep": keep1}
             now = margins_kernel("last", pieces, g, h, state)
-            final_position = assemble(now["pos"], across(now["pos"]))
-            sign, final_position = lax.optimization_barrier((sign, final_position))
+            swapped, position, base = lax.optimization_barrier(
+                (across(now["margins"]), now["pos"], now["base"])
+            )
+            partials = around(pair_sum(now["margins"], swapped, rows))
+            final_position = assemble(position, across(position))
+            base = (base, across(base))
+            sign, final_position, base = lax.optimization_barrier((sign, final_position, base))
             signs = (sign, signs[1])
-        g, residual, side = gradient(
-            paired(now["margins"]), residual, last, like if last else None
-        )
-    distances, likes = side
-    momentum = finish_kernel(g, h, now["p"], now["q"])
-    return (final_position, assemble(momentum, across(momentum)), likes, distances)
+        if not last:
+            partials = paired(now["margins"])
+        g, residual, side = gradient(partials, residual, last, like if last else None)
+    squares, sides = side
+    g, squares, sides = lax.optimization_barrier((g, squares, sides))
+    distances, likes = scores(squares, sides, rows * devices)
+    momentum = finish_kernel(g, across(g), h, base)
+    return (final_position, momentum, likes, distances)
 
 
 def solution(mesh):

time: 411 us -> 409 us (level)
    ppermute x15 -> x16, waiting for transfers between devices: 11.9 us -> 10.1 us  [across(): return lax.ppermute(value, 'rows', swap)]
    ppermute x15 -> x16, starting transfers between devices: 51.8 us -> 52.1 us  [across(): return lax.ppermute(value, 'rows', swap)]
  transfers between devices with their start and end apart: 48 -> 49, of which waited for: 41 -> 41; matrix products, arithmetic and copies ran while one was open for 0% -> 0% of each run, Pallas kernels for 2% -> 2%
where the time goes in v3:
time: 409 us; the launch traced here: 408 us
  blocking collectives  239 us (58%)
  starting transfers between devices  76.9 us (19%)
  Pallas kernels  46.3 us (11%)
  waiting for transfers between devices  45.3 us (11%)
    all_to_all x22, blocking collectives, exchange(): return lax.all_to_all(blocked, 'rows', 0, 0, axis_index_groups=chips)  239 us
    ppermute x16, starting transfers between devices, across(): return lax.ppermute(value, 'rows', swap)  52.1 us
    pallas_call x50, Pallas kernels, call(): pl.pallas_call(body, in_specs=[spec for _, spec in ins], out_specs=[VMEM]...  44.2 us
    ppermute x33, waiting for transfers between devices, around(): moved[k] = lax.ppermute(margins, 'feat', pairs)  35.2 us
    ppermute x33, starting transfers between devices, around(): moved[k] = lax.ppermute(margins, 'feat', pairs)  24.8 us
    ppermute x16, waiting for transfers between devices, across(): return lax.ppermute(value, 'rows', swap)  10.1 us
  transfers between devices with their start and end apart: 49, of which 41 were waited for; matrix products, arithmetic and copies ran while one was open for 0% of the time, Pallas kernels for 2%

profile of v3, /device:TPU:1, one launch (start us, length us, event | category | flops | bytes accessed | tf_op | source)
XLA Modules:
  0.0 408.4 jit_solution(2290509409093136371)
XLA Ops:
  0.6 3.6 shard_map.103
  4.2 1.5 collective-permute-start
  5.7 2.6 shard_map.104
  8.3 3.9 collective-permute-start.3
  13.1 3.2 collective-permute-done.2.two
  16.3 1.6 collective-permute-start.4
  21.6 14.3 %all_to_all.110.refs_0_ = bf16[16,16,512]{2,1,0:T(8,128)(2,1)S(1)} all-to-all(bf16[16,16,512]{2,1,0:T(8,128)(2,1)S(1)} %shard_map.107), channel_id=1, replica_groups={{0,8,16,24,32,40,48,56,64,72,80,88,96,104,112,120},{4,12,20,28,36,44,52..., dimensions={0} | all-to-all | bytes 524288 | tf_op jit(solution)/shard_map/all_to_all | solution.py:463
  36.0 10.9 %all_to_all.111.arrived_ref.refs_2_ = bf16[16,16,512]{2,1,0:T(8,128)(2,1)S(1)} all-to-all(bf16[16,16,512]{2,1,0:T(8,128)(2,1)S(1)} %get-tuple-element.97), channel_id=1, replica_groups={{0,8,16,24,32,40,48,56,64,72,80,88,96,104,112,120},{4,12,20,28,36,44,52..., dimensions={0} | all-to-all | bytes 524288 | tf_op jit(solution)/shard_map/all_to_all | solution.py:463
  46.8 2.5 shard_map.109
  49.3 2.8 collective-permute-start.6
  53.4 1.4 collective-permute-start.8
  55.5 2.0 shard_map.112.own_ref
  57.7 1.4 collective-permute-done.7.refs_1_
  60.4 10.5 %all_to_all.112.refs_0_ = bf16[16,16,512]{2,1,0:T(8,128)(2,1)S(1)} all-to-all(bf16[16,16,512]{2,1,0:T(8,128)(2,1)S(1)} %shard_map.111), channel_id=1, replica_groups={{0,8,16,24,32,40,48,56,64,72,80,88,96,104,112,120},{4,12,20,28,36,44,52..., dimensions={0} | all-to-all | bytes 524288 | tf_op jit(solution)/shard_map/all_to_all | solution.py:463
  71.0 10.8 %all_to_all.113.arrived_ref = bf16[16,16,512]{2,1,0:T(8,128)(2,1)S(1)} all-to-all(bf16[16,16,512]{2,1,0:T(8,128)(2,1)S(1)} %get-tuple-element.105), channel_id=1, replica_groups={{0,8,16,24,32,40,48,56,64,72,80,88,96,104,112,120},{4,12,20,28,36,44,52..., dimensions={0} | all-to-all | bytes 524288 | tf_op jit(solution)/shard_map/all_to_all | solution.py:463
  81.8 2.5 shard_map.114
  84.3 4.0 collective-permute-start.10
  90.9 2.0 shard_map.117.other_ref
  92.9 1.6 collective-permute-done.12.refs_2_
  96.2 10.6 %all_to_all.114.refs_0_ = bf16[16,16,512]{2,1,0:T(8,128)(2,1)S(1)} all-to-all(bf16[16,16,512]{2,1,0:T(8,128)(2,1)S(1)} %shard_map.116), channel_id=1, replica_groups={{0,8,16,24,32,40,48,56,64,72,80,88,96,104,112,120},{4,12,20,28,36,44,52..., dimensions={0} | all-to-all | bytes 524288 | tf_op jit(solution)/shard_map/all_to_all | solution.py:463
  106.8 10.7 %all_to_all.115.arrived_ref = bf16[16,16,512]{2,1,0:T(8,128)(2,1)S(1)} all-to-all(bf16[16,16,512]{2,1,0:T(8,128)(2,1)S(1)} %get-tuple-element.112), channel_id=1, replica_groups={{0,8,16,24,32,40,48,56,64,72,80,88,96,104,112,120},{4,12,20,28,36,44,52..., dimensions={0} | all-to-all | bytes 524288 | tf_op jit(solution)/shard_map/all_to_all | solution.py:463
  117.6 1.4 shard_map.119
  118.9 4.6 %collective-permute-start.14 = (f32[16,512]{1,0:T(8,128)S(1)}, f32[16,512]{1,0:T(8,128)S(1)}, u32[]{:S(2)}, u32[]{:S(2)}) collective-permute-start(f32[16,512]{1,0:T(8,128)S(1)} %get-tuple-element.115.mine_ref), channel_id=1, source_target_pairs={{0,4},{4,0},{8,12},{12,8},{16,20},{20,16},{24,28},{28,24},{32,36},... | collective-permute-start | bytes 98312 | tf_op jit(solution)/shard_map/ppermute | solution.py:466
  127.2 2.4 collective-permute-done.16.refs_2_
  131.3 10.6 %all_to_all.116.refs_0_ = bf16[16,16,512]{2,1,0:T(8,128)(2,1)S(1)} all-to-all(bf16[16,16,512]{2,1,0:T(8,128)(2,1)S(1)} %shard_map.121), channel_id=1, replica_groups={{0,8,16,24,32,40,48,56,64,72,80,88,96,104,112,120},{4,12,20,28,36,44,52..., dimensions={0} | all-to-all | bytes 524288 | tf_op jit(solution)/shard_map/all_to_all | solution.py:463
  141.9 10.7 %all_to_all.117.arrived_ref = bf16[16,16,512]{2,1,0:T(8,128)(2,1)S(1)} all-to-all(bf16[16,16,512]{2,1,0:T(8,128)(2,1)S(1)} %get-tuple-element.117), channel_id=1, replica_groups={{0,8,16,24,32,40,48,56,64,72,80,88,96,104,112,120},{4,12,20,28,36,44,52..., dimensions={0} | all-to-all | bytes 524288 | tf_op jit(solution)/shard_map/all_to_all | solution.py:463
  152.7 1.4 shard_map.123
  154.1 4.6 %collective-permute-start.18 = (f32[16,512]{1,0:T(8,128)S(1)}, f32[16,512]{1,0:T(8,128)S(1)}, u32[]{:S(2)}, u32[]{:S(2)}) collective-permute-start(f32[16,512]{1,0:T(8,128)S(1)} %get-tuple-element.120.mine_ref), channel_id=1, source_target_pairs={{0,4},{4,0},{8,12},{12,8},{16,20},{20,16},{24,28},{28,24},{32,36},... | collective-permute-start | bytes 98312 | tf_op jit(solution)/shard_map/ppermute | solution.py:466
  162.3 2.6 collective-permute-done.20.refs_2_
  166.6 10.6 %all_to_all.118.refs_0_ = bf16[16,16,512]{2,1,0:T(8,128)(2,1)S(1)} all-to-all(bf16[16,16,512]{2,1,0:T(8,128)(2,1)S(1)} %shard_map.125), channel_id=1, replica_groups={{0,8,16,24,32,40,48,56,64,72,80,88,96,104,112,120},{4,12,20,28,36,44,52..., dimensions={0} | all-to-all | bytes 524288 | tf_op jit(solution)/shard_map/all_to_all | solution.py:463
  177.2 10.7 %all_to_all.119.arrived_ref = bf16[16,16,512]{2,1,0:T(8,128)(2,1)S(1)} all-to-all(bf16[16,16,512]{2,1,0:T(8,128)(2,1)S(1)} %get-tuple-element.122), channel_id=1, replica_groups={{0,8,16,24,32,40,48,56,64,72,80,88,96,104,112,120},{4,12,20,28,36,44,52..., dimensions={0} | all-to-all | bytes 524288 | tf_op jit(solution)/shard_map/all_to_all | solution.py:463
  188.0 2.0 shard_map.127
  190.0 4.6 %collective-permute-start.22 = (f32[16,512]{1,0:T(8,128)S(1)}, f32[16,512]{1,0:T(8,128)S(1)}, u32[]{:S(2)}, u32[]{:S(2)}) collective-permute-start(f32[16,512]{1,0:T(8,128)S(1)} %get-tuple-element.125.mine_ref), channel_id=1, source_target_pairs={{0,4},{4,0},{8,12},{12,8},{16,20},{20,16},{24,28},{28,24},{32,36},... | collective-permute-start | bytes 98312 | tf_op jit(solution)/shard_map/ppermute | solution.py:466
  198.2 2.4 collective-permute-done.24.refs_2_
  201.0 1.4 shard_map.129
  202.4 10.6 %all_to_all.120.refs_0_ = bf16[16,16,512]{2,1,0:T(8,128)(2,1)S(1)} all-to-all(bf16[16,16,512]{2,1,0:T(8,128)(2,1)S(1)} %get-tuple-element.126), channel_id=1, replica_groups={{0,8,16,24,32,40,48,56,64,72,80,88,96,104,112,120},{4,12,20,28,36,44,52..., dimensions={0} | all-to-all | bytes 524288 | tf_op jit(solution)/shard_map/all_to_all | solution.py:463
  213.1 10.7 %all_to_all.121.arrived_ref = bf16[16,16,512]{2,1,0:T(8,128)(2,1)S(1)} all-to-all(bf16[16,16,512]{2,1,0:T(8,128)(2,1)S(1)} %get-tuple-element.128), channel_id=1, replica_groups={{0,8,16,24,32,40,48,56,64,72,80,88,96,104,112,120},{4,12,20,28,36,44,52..., dimensions={0} | all-to-all | bytes 524288 | tf_op jit(solution)/shard_map/all_to_all | solution.py:463
  223.8 1.4 shard_map.131
  225.2 4.6 %collective-permute-start.26 = (f32[16,512]{1,0:T(8,128)S(1)}, f32[16,512]{1,0:T(8,128)S(1)}, u32[]{:S(2)}, u32[]{:S(2)}) collective-permute-start(f32[16,512]{1,0:T(8,128)S(1)} %get-tuple-element.132.mine_ref), channel_id=1, source_target_pairs={{0,4},{4,0},{8,12},{12,8},{16,20},{20,16},{24,28},{28,24},{32,36},... | collective-permute-start | bytes 98312 | tf_op jit(solution)/shard_map/ppermute | solution.py:466
  233.5 2.6 collective-permute-done.28.refs_2_
  237.7 10.6 %all_to_all.122.refs_0_ = bf16[16,16,512]{2,1,0:T(8,128)(2,1)S(1)} all-to-all(bf16[16,16,512]{2,1,0:T(8,128)(2,1)S(1)} %shard_map.133), channel_id=1, replica_groups={{0,8,16,24,32,40,48,56,64,72,80,88,96,104,112,120},{4,12,20,28,36,44,52..., dimensions={0} | all-to-all | bytes 524288 | tf_op jit(solution)/shard_map/all_to_all | solution.py:463
  248.4 10.7 %all_to_all.123.arrived_ref = bf16[16,16,512]{2,1,0:T(8,128)(2,1)S(1)} all-to-all(bf16[16,16,512]{2,1,0:T(8,128)(2,1)S(1)} %get-tuple-element.134), channel_id=1, replica_groups={{0,8,16,24,32,40,48,56,64,72,80,88,96,104,112,120},{4,12,20,28,36,44,52..., dimensions={0} | all-to-all | bytes 524288 | tf_op jit(solution)/shard_map/all_to_all | solution.py:463
  259.1 1.4 shard_map.135
  260.5 4.6 %collective-permute-start.30 = (f32[16,512]{1,0:T(8,128)S(1)}, f32[16,512]{1,0:T(8,128)S(1)}, u32[]{:S(2)}, u32[]{:S(2)}) collective-permute-start(f32[16,512]{1,0:T(8,128)S(1)} %get-tuple-element.137.mine_ref), channel_id=1, source_target_pairs={{0,4},{4,0},{8,12},{12,8},{16,20},{20,16},{24,28},{28,24},{32,36},... | collective-permute-start | bytes 98312 | tf_op jit(solution)/shard_map/ppermute | solution.py:466
  268.8 2.5 collective-permute-done.32.refs_2_
  272.9 10.6 %all_to_all.124.refs_0_ = bf16[16,16,512]{2,1,0:T(8,128)(2,1)S(1)} all-to-all(bf16[16,16,512]{2,1,0:T(8,128)(2,1)S(1)} %shard_map.137), channel_id=1, replica_groups={{0,8,16,24,32,40,48,56,64,72,80,88,96,104,112,120},{4,12,20,28,36,44,52..., dimensions={0} | all-to-all | bytes 524288 | tf_op jit(solution)/shard_map/all_to_all | solution.py:463
  283.6 10.7 %all_to_all.125.arrived_ref = bf16[16,16,512]{2,1,0:T(8,128)(2,1)S(1)} all-to-all(bf16[16,16,512]{2,1,0:T(8,128)(2,1)S(1)} %get-tuple-element.139), channel_id=1, replica_groups={{0,8,16,24,32,40,48,56,64,72,80,88,96,104,112,120},{4,12,20,28,36,44,52..., dimensions={0} | all-to-all | bytes 524288 | tf_op jit(solution)/shard_map/all_to_all | solution.py:463
  294.3 1.4 shard_map.139
  295.7 4.6 %collective-permute-start.34 = (f32[16,512]{1,0:T(8,128)S(1)}, f32[16,512]{1,0:T(8,128)S(1)}, u32[]{:S(2)}, u32[]{:S(2)}) collective-permute-start(f32[16,512]{1,0:T(8,128)S(1)} %get-tuple-element.142.mine_ref), channel_id=1, source_target_pairs={{0,4},{4,0},{8,12},{12,8},{16,20},{20,16},{24,28},{28,24},{32,36},... | collective-permute-start | bytes 98312 | tf_op jit(solution)/shard_map/ppermute | solution.py:466
  304.0 2.6 collective-permute-done.36.refs_2_
  308.2 10.6 %all_to_all.126.refs_0_ = bf16[16,16,512]{2,1,0:T(8,128)(2,1)S(1)} all-to-all(bf16[16,16,512]{2,1,0:T(8,128)(2,1)S(1)} %shard_map.141), channel_id=1, replica_groups={{0,8,16,24,32,40,48,56,64,72,80,88,96,104,112,120},{4,12,20,28,36,44,52..., dimensions={0} | all-to-all | bytes 524288 | tf_op jit(solution)/shard_map/all_to_all | solution.py:463
  318.9 10.7 %all_to_all.127.arrived_ref = bf16[16,16,512]{2,1,0:T(8,128)(2,1)S(1)} all-to-all(bf16[16,16,512]{2,1,0:T(8,128)(2,1)S(1)} %get-tuple-element.144), channel_id=1, replica_groups={{0,8,16,24,32,40,48,56,64,72,80,88,96,104,112,120},{4,12,20,28,36,44,52..., dimensions={0} | all-to-all | bytes 524288 | tf_op jit(solution)/shard_map/all_to_all | solution.py:463
  329.6 1.4 shard_map.143
  331.0 4.6 %collective-permute-start.38 = (f32[16,512]{1,0:T(8,128)S(1)}, f32[16,512]{1,0:T(8,128)S(1)}, u32[]{:S(2)}, u32[]{:S(2)}) collective-permute-start(f32[16,512]{1,0:T(8,128)S(1)} %get-tuple-element.147.mine_ref), channel_id=1, source_target_pairs={{0,4},{4,0},{8,12},{12,8},{16,20},{20,16},{24,28},{28,24},{32,36},... | collective-permute-start | bytes 98312 | tf_op jit(solution)/shard_map/ppermute | solution.py:466
  339.2 2.5 collective-permute-done.40.refs_2_
  343.4 10.6 %all_to_all.128.refs_0_ = bf16[16,16,512]{2,1,0:T(8,128)(2,1)S(1)} all-to-all(bf16[16,16,512]{2,1,0:T(8,128)(2,1)S(1)} %shard_map.145), channel_id=1, replica_groups={{0,8,16,24,32,40,48,56,64,72,80,88,96,104,112,120},{4,12,20,28,36,44,52..., dimensions={0} | all-to-all | bytes 524288 | tf_op jit(solution)/shard_map/all_to_all | solution.py:463
  354.0 10.7 %all_to_all.129.arrived_ref = bf16[16,16,512]{2,1,0:T(8,128)(2,1)S(1)} all-to-all(bf16[16,16,512]{2,1,0:T(8,128)(2,1)S(1)} %get-tuple-element.149), channel_id=1, replica_groups={{0,8,16,24,32,40,48,56,64,72,80,88,96,104,112,120},{4,12,20,28,36,44,52..., dimensions={0} | all-to-all | bytes 524288 | tf_op jit(solution)/shard_map/all_to_all | solution.py:463
  364.8 1.4 shard_map.147
  366.2 4.7 %collective-permute-start.42 = (f32[16,640]{1,0:T(8,128)S(1)}, f32[16,640]{1,0:T(8,128)S(1)}, u32[]{:S(2)}, u32[]{:S(2)}) collective-permute-start(f32[16,640]{1,0:T(8,128)S(1)} %get-tuple-element.155.mine_ref), channel_id=1, source_target_pairs={{0,4},{4,0},{8,12},{12,8},{16,20},{20,16},{24,28},{28,24},{32,36},... | collective-permute-start | bytes 122888 | tf_op jit(solution)/shard_map/ppermute | solution.py:466
  375.2 2.4 collective-permute-done.46.refs_2_
  378.1 1.4 shard_map.149
  379.5 10.9 %all_to_all.130.refs_0_ = bf16[16,16,640]{2,1,0:T(8,128)(2,1)S(1)} all-to-all(bf16[16,16,640]{2,1,0:T(8,128)(2,1)S(1)} %get-tuple-element.164), channel_id=1, replica_groups={{0,8,16,24,32,40,48,56,64,72,80,88,96,104,112,120},{4,12,20,28,36,44,52..., dimensions={0} | all-to-all | bytes 655360 | tf_op jit(solution)/shard_map/all_to_all | solution.py:463
  390.5 10.8 %all_to_all.131.mine_ref = bf16[16,16,512]{2,1,0:T(8,128)(2,1)S(1)} all-to-all(bf16[16,16,512]{2,1,0:T(8,128)(2,1)S(1)} %get-tuple-element.166), channel_id=1, replica_groups={{0,8,16,24,32,40,48,56,64,72,80,88,96,104,112,120},{4,12,20,28,36,44,52..., dimensions={0} | all-to-all | bytes 524288 | tf_op jit(solution)/shard_map/all_to_all | solution.py:463
  401.3 4.6 %collective-permute-start.48 = (bf16[16,16,512]{2,1,0:T(8,128)(2,1)S(1)}, bf16[16,16,512]{2,1,0:T(8,128)(2,1)S(1)}, u32[]{:S(2)}, u32[]{:S(2)}) collective-permute-start(bf16[16,16,512]{2,1,0:T(8,128)(2,1)S(1)} %all_to_all.131.mine_ref), channel_id=1, source_target_pairs={{0,4},{4,0},{8,12},{12,8},{16,20},{20,16},{24,28},{28,24},{32,36},... | collective-permute-start | bytes 786440 | tf_op jit(solution)/shard_map/ppermute | solution.py:466
  (120 shorter events, 56.0 us)
Async XLA Ops:
  0.6 5.0 %copy-start.1 = (f32[16,16384]{1,0:T(8,128)S(1)}, f32[16,16384]{1,0:T(8,128)}, u32[]{:S(2)}) copy-start(f32[16,16384]{1,0:T(8,128)} %start_ref.1) | copy-start | bytes 3145732
  4.2 16.0 %collective-permute-start = (bf16[256,8192]{1,0:T(8,128)(2,1)S(1)}, bf16[256,8192]{1,0:T(8,128)(2,1)S(1)}, u32[]{:S(2)}, u32[]{:S(2)}) collective-permute-start(bf16[256,8192]{1,0:T(8,128)(2,1)S(1)} %get-tuple-element.92.away_ref), channel_id=1, source_target_pairs={{0,4},{4,0},{8,12},{12,8},{16,20},{20,16},{24,28},{28,24},{32,36},... | collective-permute-start | bytes 12582920 | tf_op jit(solution)/shard_map/ppermute | solution.py:466
  5.7 12.2 %copy-start = (f32[8,4,16384]{2,1,0:T(4,128)S(1)}, f32[8,4,16384]{2,1,0:T(4,128)}, u32[]{:S(2)}) copy-start(f32[8,4,16384]{2,1,0:T(4,128)} %bank_ref.1) | copy-start | bytes 6291460
  5.7 12.2 %copy-start.2 = (s32[2,16]{1,0:T(2,128)S(1)}, s32[2,16]{1,0:T(2,128)}, u32[]{:S(2)}) copy-start(s32[2,16]{1,0:T(2,128)} %accept_ref.1) | copy-start | bytes 388
  5.7 12.2 %copy-start.3 = (s32[256]{0:T(256)S(1)}, s32[256]{0:T(256)}, u32[]{:S(2)}) copy-start(s32[256]{0:T(256)} %param.8) | copy-start | bytes 3076
  5.7 12.2 %copy-start.4 = (s32[8]{0:T(128)S(1)}, s32[8]{0:T(128)}, u32[]{:S(2)}) copy-start(s32[8]{0:T(128)} %lag_ref.1) | copy-start | bytes 100
  5.7 12.2 %copy-start.5 = (f32[8]{0:T(128)S(1)}, f32[8]{0:T(128)}, u32[]{:S(2)}) copy-start(f32[8]{0:T(128)} %steps_ref.1) | copy-start | bytes 100
  8.3 4.8 %collective-permute-start.3 = (f32[16,256]{1,0:T(8,128)S(1)}, f32[16,256]{1,0:T(8,128)S(1)}, u32[]{:S(2)}, u32[]{:S(2)}) collective-permute-start(f32[16,256]{1,0:T(8,128)S(1)} %get-tuple-element.93.own), channel_id=1, source_target_pairs={{0,3},{1,0},{2,1},{3,2},{4,7},{5,4},{6,5},{7,6},{8,11},{9,8},{10,9... | collective-permute-start | bytes 49160 | tf_op jit(solution)/shard_map/ppermute | solution.py:472
  12.2 4.1 %collective-permute-start.2 = (f32[16,256]{1,0:T(8,128)S(1)}, f32[16,256]{1,0:T(8,128)S(1)}, u32[]{:S(2)}, u32[]{:S(2)}) collective-permute-start(f32[16,256]{1,0:T(8,128)S(1)} %get-tuple-element.93.own), channel_id=1, source_target_pairs={{0,2},{1,3},{2,0},{3,1},{4,6},{5,7},{6,4},{7,5},{8,10},{9,11},{10,... | collective-permute-start | bytes 49160 | tf_op jit(solution)/shard_map/ppermute | solution.py:472
  12.2 4.1 %collective-permute-start.1 = (f32[16,256]{1,0:T(8,128)S(1)}, f32[16,256]{1,0:T(8,128)S(1)}, u32[]{:S(2)}, u32[]{:S(2)}) collective-permute-start(f32[16,256]{1,0:T(8,128)S(1)} %get-tuple-element.93.own), channel_id=1, source_target_pairs={{0,1},{1,2},{2,3},{3,0},{4,5},{5,6},{6,7},{7,4},{8,9},{9,10},{10,1... | collective-permute-start | bytes 49160 | tf_op jit(solution)/shard_map/ppermute | solution.py:472
  16.3 2.8 collective-permute-start.4
  19.0 1.3 collective-permute-start.5
  49.3 3.7 collective-permute-start.6
  53.0 4.6 %collective-permute-start.9 = (f32[16,512]{1,0:T(8,128)S(1)}, f32[16,512]{1,0:T(8,128)S(1)}, u32[]{:S(2)}, u32[]{:S(2)}) collective-permute-start(f32[16,512]{1,0:T(8,128)S(1)} %shard_map.110.refs_0_), channel_id=1, source_target_pairs={{0,3},{1,0},{2,1},{3,2},{4,7},{5,4},{6,5},{7,6},{8,11},{9,8},{10,9... | collective-permute-start | bytes 98312 | tf_op jit(solution)/shard_map/ppermute | solution.py:472
  53.4 4.3 %collective-permute-start.8 = (f32[16,512]{1,0:T(8,128)S(1)}, f32[16,512]{1,0:T(8,128)S(1)}, u32[]{:S(2)}, u32[]{:S(2)}) collective-permute-start(f32[16,512]{1,0:T(8,128)S(1)} %shard_map.110.refs_0_), channel_id=1, source_target_pairs={{0,2},{1,3},{2,0},{3,1},{4,6},{5,7},{6,4},{7,5},{8,10},{9,11},{10,... | collective-permute-start | bytes 98312 | tf_op jit(solution)/shard_map/ppermute | solution.py:472
  54.8 4.3 %collective-permute-start.7 = (f32[16,512]{1,0:T(8,128)S(1)}, f32[16,512]{1,0:T(8,128)S(1)}, u32[]{:S(2)}, u32[]{:S(2)}) collective-permute-start(f32[16,512]{1,0:T(8,128)S(1)} %shard_map.110.refs_0_), channel_id=1, source_target_pairs={{0,1},{1,2},{2,3},{3,0},{4,5},{5,6},{6,7},{7,4},{8,9},{9,10},{10,1... | collective-permute-start | bytes 98312 | tf_op jit(solution)/shard_map/ppermute | solution.py:472
  84.3 4.8 %collective-permute-start.10 = (f32[16,512]{1,0:T(8,128)S(1)}, f32[16,512]{1,0:T(8,128)S(1)}, u32[]{:S(2)}, u32[]{:S(2)}) collective-permute-start(f32[16,512]{1,0:T(8,128)S(1)} %get-tuple-element.108.mine_ref), channel_id=1, source_target_pairs={{0,4},{4,0},{8,12},{12,8},{16,20},{20,16},{24,28},{28,24},{32,36},... | collective-permute-start | bytes 98312 | tf_op jit(solution)/shard_map/ppermute | solution.py:466
  89.1 3.7 collective-permute-start.13
  90.2 4.3 %collective-permute-start.12 = (f32[16,512]{1,0:T(8,128)S(1)}, f32[16,512]{1,0:T(8,128)S(1)}, u32[]{:S(2)}, u32[]{:S(2)}) collective-permute-start(f32[16,512]{1,0:T(8,128)S(1)} %shard_map.115.refs_0_), channel_id=1, source_target_pairs={{0,2},{1,3},{2,0},{3,1},{4,6},{5,7},{6,4},{7,5},{8,10},{9,11},{10,... | collective-permute-start | bytes 98312 | tf_op jit(solution)/shard_map/ppermute | solution.py:472
  90.8 4.0 collective-permute-start.11
  118.9 5.5 %collective-permute-start.14 = (f32[16,512]{1,0:T(8,128)S(1)}, f32[16,512]{1,0:T(8,128)S(1)}, u32[]{:S(2)}, u32[]{:S(2)}) collective-permute-start(f32[16,512]{1,0:T(8,128)S(1)} %get-tuple-element.115.mine_ref), channel_id=1, source_target_pairs={{0,4},{4,0},{8,12},{12,8},{16,20},{20,16},{24,28},{28,24},{32,36},... | collective-permute-start | bytes 98312 | tf_op jit(solution)/shard_map/ppermute | solution.py:466
  124.4 2.8 collective-permute-start.17
  125.3 4.3 %collective-permute-start.16 = (f32[16,512]{1,0:T(8,128)S(1)}, f32[16,512]{1,0:T(8,128)S(1)}, u32[]{:S(2)}, u32[]{:S(2)}) collective-permute-start(f32[16,512]{1,0:T(8,128)S(1)} %shard_map.120.refs_0_), channel_id=1, source_target_pairs={{0,2},{1,3},{2,0},{3,1},{4,6},{5,7},{6,4},{7,5},{8,10},{9,11},{10,... | collective-permute-start | bytes 98312 | tf_op jit(solution)/shard_map/ppermute | solution.py:472
  125.9 4.0 collective-permute-start.15
  154.1 5.5 %collective-permute-start.18 = (f32[16,512]{1,0:T(8,128)S(1)}, f32[16,512]{1,0:T(8,128)S(1)}, u32[]{:S(2)}, u32[]{:S(2)}) collective-permute-start(f32[16,512]{1,0:T(8,128)S(1)} %get-tuple-element.120.mine_ref), channel_id=1, source_target_pairs={{0,4},{4,0},{8,12},{12,8},{16,20},{20,16},{24,28},{28,24},{32,36},... | collective-permute-start | bytes 98312 | tf_op jit(solution)/shard_map/ppermute | solution.py:466
  159.6 2.8 collective-permute-start.21
  160.6 4.3 %collective-permute-start.20 = (f32[16,512]{1,0:T(8,128)S(1)}, f32[16,512]{1,0:T(8,128)S(1)}, u32[]{:S(2)}, u32[]{:S(2)}) collective-permute-start(f32[16,512]{1,0:T(8,128)S(1)} %shard_map.124.refs_0_), channel_id=1, source_target_pairs={{0,2},{1,3},{2,0},{3,1},{4,6},{5,7},{6,4},{7,5},{8,10},{9,11},{10,... | collective-permute-start | bytes 98312 | tf_op jit(solution)/shard_map/ppermute | solution.py:472
  161.3 4.0 collective-permute-start.19
  190.0 5.5 %collective-permute-start.22 = (f32[16,512]{1,0:T(8,128)S(1)}, f32[16,512]{1,0:T(8,128)S(1)}, u32[]{:S(2)}, u32[]{:S(2)}) collective-permute-start(f32[16,512]{1,0:T(8,128)S(1)} %get-tuple-element.125.mine_ref), channel_id=1, source_target_pairs={{0,4},{4,0},{8,12},{12,8},{16,20},{20,16},{24,28},{28,24},{32,36},... | collective-permute-start | bytes 98312 | tf_op jit(solution)/shard_map/ppermute | solution.py:466
  195.4 2.8 collective-permute-start.25
  196.4 4.3 %collective-permute-start.24 = (f32[16,512]{1,0:T(8,128)S(1)}, f32[16,512]{1,0:T(8,128)S(1)}, u32[]{:S(2)}, u32[]{:S(2)}) collective-permute-start(f32[16,512]{1,0:T(8,128)S(1)} %shard_map.128.refs_0_), channel_id=1, source_target_pairs={{0,2},{1,3},{2,0},{3,1},{4,6},{5,7},{6,4},{7,5},{8,10},{9,11},{10,... | collective-permute-start | bytes 98312 | tf_op jit(solution)/shard_map/ppermute | solution.py:472
  197.0 4.0 collective-permute-start.23
  225.2 5.5 %collective-permute-start.26 = (f32[16,512]{1,0:T(8,128)S(1)}, f32[16,512]{1,0:T(8,128)S(1)}, u32[]{:S(2)}, u32[]{:S(2)}) collective-permute-start(f32[16,512]{1,0:T(8,128)S(1)} %get-tuple-element.132.mine_ref), channel_id=1, source_target_pairs={{0,4},{4,0},{8,12},{12,8},{16,20},{20,16},{24,28},{28,24},{32,36},... | collective-permute-start | bytes 98312 | tf_op jit(solution)/shard_map/ppermute | solution.py:466
  230.7 2.8 collective-permute-start.29
  231.8 4.3 %collective-permute-start.28 = (f32[16,512]{1,0:T(8,128)S(1)}, f32[16,512]{1,0:T(8,128)S(1)}, u32[]{:S(2)}, u32[]{:S(2)}) collective-permute-start(f32[16,512]{1,0:T(8,128)S(1)} %shard_map.132.refs_0_), channel_id=1, source_target_pairs={{0,2},{1,3},{2,0},{3,1},{4,6},{5,7},{6,4},{7,5},{8,10},{9,11},{10,... | collective-permute-start | bytes 98312 | tf_op jit(solution)/shard_map/ppermute | solution.py:472
  232.4 4.0 collective-permute-start.27
  260.5 5.5 %collective-permute-start.30 = (f32[16,512]{1,0:T(8,128)S(1)}, f32[16,512]{1,0:T(8,128)S(1)}, u32[]{:S(2)}, u32[]{:S(2)}) collective-permute-start(f32[16,512]{1,0:T(8,128)S(1)} %get-tuple-element.137.mine_ref), channel_id=1, source_target_pairs={{0,4},{4,0},{8,12},{12,8},{16,20},{20,16},{24,28},{28,24},{32,36},... | collective-permute-start | bytes 98312 | tf_op jit(solution)/shard_map/ppermute | solution.py:466
  266.0 2.8 collective-permute-start.33
  267.0 4.3 %collective-permute-start.32 = (f32[16,512]{1,0:T(8,128)S(1)}, f32[16,512]{1,0:T(8,128)S(1)}, u32[]{:S(2)}, u32[]{:S(2)}) collective-permute-start(f32[16,512]{1,0:T(8,128)S(1)} %shard_map.136.refs_0_), channel_id=1, source_target_pairs={{0,2},{1,3},{2,0},{3,1},{4,6},{5,7},{6,4},{7,5},{8,10},{9,11},{10,... | collective-permute-start | bytes 98312 | tf_op jit(solution)/shard_map/ppermute | solution.py:472
  267.6 4.0 collective-permute-start.31
  295.7 5.5 %collective-permute-start.34 = (f32[16,512]{1,0:T(8,128)S(1)}, f32[16,512]{1,0:T(8,128)S(1)}, u32[]{:S(2)}, u32[]{:S(2)}) collective-permute-start(f32[16,512]{1,0:T(8,128)S(1)} %get-tuple-element.142.mine_ref), channel_id=1, source_target_pairs={{0,4},{4,0},{8,12},{12,8},{16,20},{20,16},{24,28},{28,24},{32,36},... | collective-permute-start | bytes 98312 | tf_op jit(solution)/shard_map/ppermute | solution.py:466
  301.2 2.8 collective-permute-start.37
  302.3 4.3 %collective-permute-start.36 = (f32[16,512]{1,0:T(8,128)S(1)}, f32[16,512]{1,0:T(8,128)S(1)}, u32[]{:S(2)}, u32[]{:S(2)}) collective-permute-start(f32[16,512]{1,0:T(8,128)S(1)} %shard_map.140.refs_0_), channel_id=1, source_target_pairs={{0,2},{1,3},{2,0},{3,1},{4,6},{5,7},{6,4},{7,5},{8,10},{9,11},{10,... | collective-permute-start | bytes 98312 | tf_op jit(solution)/shard_map/ppermute | solution.py:472
  302.9 4.0 collective-permute-start.35
  331.0 5.5 %collective-permute-start.38 = (f32[16,512]{1,0:T(8,128)S(1)}, f32[16,512]{1,0:T(8,128)S(1)}, u32[]{:S(2)}, u32[]{:S(2)}) collective-permute-start(f32[16,512]{1,0:T(8,128)S(1)} %get-tuple-element.147.mine_ref), channel_id=1, source_target_pairs={{0,4},{4,0},{8,12},{12,8},{16,20},{20,16},{24,28},{28,24},{32,36},... | collective-permute-start | bytes 98312 | tf_op jit(solution)/shard_map/ppermute | solution.py:466
  336.5 2.8 collective-permute-start.41
  337.4 4.3 %collective-permute-start.40 = (f32[16,512]{1,0:T(8,128)S(1)}, f32[16,512]{1,0:T(8,128)S(1)}, u32[]{:S(2)}, u32[]{:S(2)}) collective-permute-start(f32[16,512]{1,0:T(8,128)S(1)} %shard_map.144.refs_0_), channel_id=1, source_target_pairs={{0,2},{1,3},{2,0},{3,1},{4,6},{5,7},{6,4},{7,5},{8,10},{9,11},{10,... | collective-permute-start | bytes 98312 | tf_op jit(solution)/shard_map/ppermute | solution.py:472
  338.0 4.0 collective-permute-start.39
  366.2 5.5 %collective-permute-start.42 = (f32[16,640]{1,0:T(8,128)S(1)}, f32[16,640]{1,0:T(8,128)S(1)}, u32[]{:S(2)}, u32[]{:S(2)}) collective-permute-start(f32[16,640]{1,0:T(8,128)S(1)} %get-tuple-element.155.mine_ref), channel_id=1, source_target_pairs={{0,4},{4,0},{8,12},{12,8},{16,20},{20,16},{24,28},{28,24},{32,36},... | collective-permute-start | bytes 122888 | tf_op jit(solution)/shard_map/ppermute | solution.py:466
  371.7 2.5 collective-permute-start.43
  372.1 3.1 collective-permute-start.44
  372.2 3.0 collective-permute-start.47
  373.3 4.4 %collective-permute-start.46 = (f32[16,640]{1,0:T(8,128)S(1)}, f32[16,640]{1,0:T(8,128)S(1)}, u32[]{:S(2)}, u32[]{:S(2)}) collective-permute-start(f32[16,640]{1,0:T(8,128)S(1)} %shard_map.148.refs_0_), channel_id=1, source_target_pairs={{0,2},{1,3},{2,0},{3,1},{4,6},{5,7},{6,4},{7,5},{8,10},{9,11},{10,... | collective-permute-start | bytes 122888 | tf_op jit(solution)/shard_map/ppermute | solution.py:472
  373.9 4.2 %collective-permute-start.45 = (f32[16,640]{1,0:T(8,128)S(1)}, f32[16,640]{1,0:T(8,128)S(1)}, u32[]{:S(2)}, u32[]{:S(2)}) collective-permute-start(f32[16,640]{1,0:T(8,128)S(1)} %shard_map.148.refs_0_), channel_id=1, source_target_pairs={{0,1},{1,2},{2,3},{3,0},{4,5},{5,6},{6,7},{7,4},{8,9},{9,10},{10,1... | collective-permute-start | bytes 122888 | tf_op jit(solution)/shard_map/ppermute | solution.py:472
  401.3 5.8 %collective-permute-start.48 = (bf16[16,16,512]{2,1,0:T(8,128)(2,1)S(1)}, bf16[16,16,512]{2,1,0:T(8,128)(2,1)S(1)}, u32[]{:S(2)}, u32[]{:S(2)}) collective-permute-start(bf16[16,16,512]{2,1,0:T(8,128)(2,1)S(1)} %all_to_all.131.mine_ref), channel_id=1, source_target_pairs={{0,4},{4,0},{8,12},{12,8},{16,20},{20,16},{24,28},{28,24},{32,36},... | collective-permute-start | bytes 786440 | tf_op jit(solution)/shard_map/ppermute | solution.py:466

commit v4 on v3

--- a/solution.py
+++ b/solution.py
@@ -488,8 +488,9 @@
     held = (own, across(away))
     margins, start = start_margins(own, away, start_position)
     mom0, mom1, h, keep0, keep1, sign = draw(labels, momenta, lag_offsets, accept_bits, step_sizes)
-    signs = (sign, across(sign))
-    margins = ring_sum(around(margins))
+    partials, signs = lax.optimization_barrier((around(margins), (sign, across(sign))))
+    sign = signs[0]
+    margins = ring_sum(partials)
     margins = pair_start(margins, across(margins))
     g0, residual, (mom0, mom1) = gradient([margins], None, beside=(mom0, mom1))
     g = g0

time: 409 us -> 408 us (level)
  no operation moved by 1% of the time
where the time goes in v4:
time: 408 us; the launch traced here: 407 us
  blocking collectives  239 us (59%)
  starting transfers between devices  78.5 us (19%)
  Pallas kernels  46.3 us (11%)
  waiting for transfers between devices  42.2 us (10%)
    all_to_all x22, blocking collectives, exchange(): return lax.all_to_all(blocked, 'rows', 0, 0, axis_index_groups=chips)  239 us
    ppermute x16, starting transfers between devices, across(): return lax.ppermute(value, 'rows', swap)  53.2 us
    pallas_call x50, Pallas kernels, call(): pl.pallas_call(body, in_specs=[spec for _, spec in ins], out_specs=[VMEM]...  44.2 us
    ppermute x33, waiting for transfers between devices, around(): moved[k] = lax.ppermute(margins, 'feat', pairs)  31.5 us
    ppermute x33, starting transfers between devices, around(): moved[k] = lax.ppermute(margins, 'feat', pairs)  25.3 us
    ppermute x16, waiting for transfers between devices, across(): return lax.ppermute(value, 'rows', swap)  10.7 us
  transfers between devices with their start and end apart: 49, of which 41 were waited for; matrix products, arithmetic and copies ran while one was open for 0% of the time, Pallas kernels for 2%

profile of v4, /device:TPU:1, one launch (start us, length us, event | category | flops | bytes accessed | tf_op | source)
XLA Modules:
  0.0 406.7 jit_solution(1829432945512812282)
XLA Ops:
  0.6 3.6 shard_map.102
  4.2 1.5 collective-permute-start.4
  5.7 2.6 shard_map.103
  8.3 3.9 collective-permute-start.2
  16.3 1.6 collective-permute-start.5
  20.1 14.2 %all_to_all.110.refs_0_ = bf16[16,16,512]{2,1,0:T(8,128)(2,1)S(1)} all-to-all(bf16[16,16,512]{2,1,0:T(8,128)(2,1)S(1)} %shard_map.107), channel_id=1, replica_groups={{0,8,16,24,32,40,48,56,64,72,80,88,96,104,112,120},{4,12,20,28,36,44,52..., dimensions={0} | all-to-all | bytes 524288 | tf_op jit(solution)/shard_map/all_to_all | solution.py:463
  34.3 10.9 %all_to_all.111.arrived_ref.refs_2_ = bf16[16,16,512]{2,1,0:T(8,128)(2,1)S(1)} all-to-all(bf16[16,16,512]{2,1,0:T(8,128)(2,1)S(1)} %get-tuple-element.109), channel_id=1, replica_groups={{0,8,16,24,32,40,48,56,64,72,80,88,96,104,112,120},{4,12,20,28,36,44,52..., dimensions={0} | all-to-all | bytes 524288 | tf_op jit(solution)/shard_map/all_to_all | solution.py:463
  45.1 2.5 shard_map.109
  47.6 2.9 collective-permute-start.6
  51.8 1.7 collective-permute-start.8
  54.0 2.0 shard_map.112.own_ref
  56.1 1.4 collective-permute-done.7.refs_1_
  58.9 10.6 %all_to_all.112.refs_0_ = bf16[16,16,512]{2,1,0:T(8,128)(2,1)S(1)} all-to-all(bf16[16,16,512]{2,1,0:T(8,128)(2,1)S(1)} %shard_map.111), channel_id=1, replica_groups={{0,8,16,24,32,40,48,56,64,72,80,88,96,104,112,120},{4,12,20,28,36,44,52..., dimensions={0} | all-to-all | bytes 524288 | tf_op jit(solution)/shard_map/all_to_all | solution.py:463
  69.5 10.8 %all_to_all.113.arrived_ref = bf16[16,16,512]{2,1,0:T(8,128)(2,1)S(1)} all-to-all(bf16[16,16,512]{2,1,0:T(8,128)(2,1)S(1)} %get-tuple-element.117), channel_id=1, replica_groups={{0,8,16,24,32,40,48,56,64,72,80,88,96,104,112,120},{4,12,20,28,36,44,52..., dimensions={0} | all-to-all | bytes 524288 | tf_op jit(solution)/shard_map/all_to_all | solution.py:463
  80.3 2.5 shard_map.114
  82.7 4.6 %collective-permute-start.10 = (f32[16,512]{1,0:T(8,128)S(1)}, f32[16,512]{1,0:T(8,128)S(1)}, u32[]{:S(2)}, u32[]{:S(2)}) collective-permute-start(f32[16,512]{1,0:T(8,128)S(1)} %get-tuple-element.120.mine_ref), channel_id=1, source_target_pairs={{0,4},{4,0},{8,12},{12,8},{16,20},{20,16},{24,28},{28,24},{32,36},... | collective-permute-start | bytes 98312 | tf_op jit(solution)/shard_map/ppermute | solution.py:466
  89.7 2.0 shard_map.117.other_ref
  94.7 10.6 %all_to_all.114.refs_0_ = bf16[16,16,512]{2,1,0:T(8,128)(2,1)S(1)} all-to-all(bf16[16,16,512]{2,1,0:T(8,128)(2,1)S(1)} %shard_map.116), channel_id=1, replica_groups={{0,8,16,24,32,40,48,56,64,72,80,88,96,104,112,120},{4,12,20,28,36,44,52..., dimensions={0} | all-to-all | bytes 524288 | tf_op jit(solution)/shard_map/all_to_all | solution.py:463
  105.3 10.8 %all_to_all.115.arrived_ref = bf16[16,16,512]{2,1,0:T(8,128)(2,1)S(1)} all-to-all(bf16[16,16,512]{2,1,0:T(8,128)(2,1)S(1)} %get-tuple-element.124), channel_id=1, replica_groups={{0,8,16,24,32,40,48,56,64,72,80,88,96,104,112,120},{4,12,20,28,36,44,52..., dimensions={0} | all-to-all | bytes 524288 | tf_op jit(solution)/shard_map/all_to_all | solution.py:463
  117.4 4.6 %collective-permute-start.14 = (f32[16,512]{1,0:T(8,128)S(1)}, f32[16,512]{1,0:T(8,128)S(1)}, u32[]{:S(2)}, u32[]{:S(2)}) collective-permute-start(f32[16,512]{1,0:T(8,128)S(1)} %get-tuple-element.127.mine_ref), channel_id=1, source_target_pairs={{0,4},{4,0},{8,12},{12,8},{16,20},{20,16},{24,28},{28,24},{32,36},... | collective-permute-start | bytes 98312 | tf_op jit(solution)/shard_map/ppermute | solution.py:466
  122.9 1.5 collective-permute-start.17
  125.6 3.0 collective-permute-done.16.refs_2_
  130.3 10.6 %all_to_all.116.refs_0_ = bf16[16,16,512]{2,1,0:T(8,128)(2,1)S(1)} all-to-all(bf16[16,16,512]{2,1,0:T(8,128)(2,1)S(1)} %shard_map.121), channel_id=1, replica_groups={{0,8,16,24,32,40,48,56,64,72,80,88,96,104,112,120},{4,12,20,28,36,44,52..., dimensions={0} | all-to-all | bytes 524288 | tf_op jit(solution)/shard_map/all_to_all | solution.py:463
  141.0 10.7 %all_to_all.117.arrived_ref = bf16[16,16,512]{2,1,0:T(8,128)(2,1)S(1)} all-to-all(bf16[16,16,512]{2,1,0:T(8,128)(2,1)S(1)} %get-tuple-element.129), channel_id=1, replica_groups={{0,8,16,24,32,40,48,56,64,72,80,88,96,104,112,120},{4,12,20,28,36,44,52..., dimensions={0} | all-to-all | bytes 524288 | tf_op jit(solution)/shard_map/all_to_all | solution.py:463
  151.7 1.4 shard_map.123
  153.1 4.6 %collective-permute-start.18 = (f32[16,512]{1,0:T(8,128)S(1)}, f32[16,512]{1,0:T(8,128)S(1)}, u32[]{:S(2)}, u32[]{:S(2)}) collective-permute-start(f32[16,512]{1,0:T(8,128)S(1)} %get-tuple-element.132.mine_ref), channel_id=1, source_target_pairs={{0,4},{4,0},{8,12},{12,8},{16,20},{20,16},{24,28},{28,24},{32,36},... | collective-permute-start | bytes 98312 | tf_op jit(solution)/shard_map/ppermute | solution.py:466
  161.4 2.0 collective-permute-done.20.refs_2_
  165.1 10.6 %all_to_all.118.refs_0_ = bf16[16,16,512]{2,1,0:T(8,128)(2,1)S(1)} all-to-all(bf16[16,16,512]{2,1,0:T(8,128)(2,1)S(1)} %shard_map.125), channel_id=1, replica_groups={{0,8,16,24,32,40,48,56,64,72,80,88,96,104,112,120},{4,12,20,28,36,44,52..., dimensions={0} | all-to-all | bytes 524288 | tf_op jit(solution)/shard_map/all_to_all | solution.py:463
  175.8 10.8 %all_to_all.119.arrived_ref = bf16[16,16,512]{2,1,0:T(8,128)(2,1)S(1)} all-to-all(bf16[16,16,512]{2,1,0:T(8,128)(2,1)S(1)} %get-tuple-element.134), channel_id=1, replica_groups={{0,8,16,24,32,40,48,56,64,72,80,88,96,104,112,120},{4,12,20,28,36,44,52..., dimensions={0} | all-to-all | bytes 524288 | tf_op jit(solution)/shard_map/all_to_all | solution.py:463
  186.5 2.0 shard_map.127
  188.5 4.5 %collective-permute-start.22 = (f32[16,512]{1,0:T(8,128)S(1)}, f32[16,512]{1,0:T(8,128)S(1)}, u32[]{:S(2)}, u32[]{:S(2)}) collective-permute-start(f32[16,512]{1,0:T(8,128)S(1)} %get-tuple-element.137.mine_ref), channel_id=1, source_target_pairs={{0,4},{4,0},{8,12},{12,8},{16,20},{20,16},{24,28},{28,24},{32,36},... | collective-permute-start | bytes 98312 | tf_op jit(solution)/shard_map/ppermute | solution.py:466
  193.9 1.5 collective-permute-start.25
  196.7 3.0 collective-permute-done.24.refs_2_
  200.0 1.4 shard_map.129
  201.5 10.6 %all_to_all.120.refs_0_ = bf16[16,16,512]{2,1,0:T(8,128)(2,1)S(1)} all-to-all(bf16[16,16,512]{2,1,0:T(8,128)(2,1)S(1)} %get-tuple-element.138), channel_id=1, replica_groups={{0,8,16,24,32,40,48,56,64,72,80,88,96,104,112,120},{4,12,20,28,36,44,52..., dimensions={0} | all-to-all | bytes 524288 | tf_op jit(solution)/shard_map/all_to_all | solution.py:463
  212.1 10.7 %all_to_all.121.arrived_ref = bf16[16,16,512]{2,1,0:T(8,128)(2,1)S(1)} all-to-all(bf16[16,16,512]{2,1,0:T(8,128)(2,1)S(1)} %get-tuple-element.140), channel_id=1, replica_groups={{0,8,16,24,32,40,48,56,64,72,80,88,96,104,112,120},{4,12,20,28,36,44,52..., dimensions={0} | all-to-all | bytes 524288 | tf_op jit(solution)/shard_map/all_to_all | solution.py:463
  222.8 1.4 shard_map.131
  224.3 4.6 %collective-permute-start.26 = (f32[16,512]{1,0:T(8,128)S(1)}, f32[16,512]{1,0:T(8,128)S(1)}, u32[]{:S(2)}, u32[]{:S(2)}) collective-permute-start(f32[16,512]{1,0:T(8,128)S(1)} %get-tuple-element.144.mine_ref), channel_id=1, source_target_pairs={{0,4},{4,0},{8,12},{12,8},{16,20},{20,16},{24,28},{28,24},{32,36},... | collective-permute-start | bytes 98312 | tf_op jit(solution)/shard_map/ppermute | solution.py:466
  232.5 2.0 collective-permute-done.28.refs_2_
  236.3 10.6 %all_to_all.122.refs_0_ = bf16[16,16,512]{2,1,0:T(8,128)(2,1)S(1)} all-to-all(bf16[16,16,512]{2,1,0:T(8,128)(2,1)S(1)} %shard_map.133), channel_id=1, replica_groups={{0,8,16,24,32,40,48,56,64,72,80,88,96,104,112,120},{4,12,20,28,36,44,52..., dimensions={0} | all-to-all | bytes 524288 | tf_op jit(solution)/shard_map/all_to_all | solution.py:463
  246.9 10.8 %all_to_all.123.arrived_ref = bf16[16,16,512]{2,1,0:T(8,128)(2,1)S(1)} all-to-all(bf16[16,16,512]{2,1,0:T(8,128)(2,1)S(1)} %get-tuple-element.146), channel_id=1, replica_groups={{0,8,16,24,32,40,48,56,64,72,80,88,96,104,112,120},{4,12,20,28,36,44,52..., dimensions={0} | all-to-all | bytes 524288 | tf_op jit(solution)/shard_map/all_to_all | solution.py:463
  257.7 1.4 shard_map.135
  259.1 4.5 %collective-permute-start.30 = (f32[16,512]{1,0:T(8,128)S(1)}, f32[16,512]{1,0:T(8,128)S(1)}, u32[]{:S(2)}, u32[]{:S(2)}) collective-permute-start(f32[16,512]{1,0:T(8,128)S(1)} %get-tuple-element.149.mine_ref), channel_id=1, source_target_pairs={{0,4},{4,0},{8,12},{12,8},{16,20},{20,16},{24,28},{28,24},{32,36},... | collective-permute-start | bytes 98312 | tf_op jit(solution)/shard_map/ppermute | solution.py:466
  264.5 1.5 collective-permute-start.33
  267.3 3.0 collective-permute-done.32.refs_2_
  272.0 10.6 %all_to_all.124.refs_0_ = bf16[16,16,512]{2,1,0:T(8,128)(2,1)S(1)} all-to-all(bf16[16,16,512]{2,1,0:T(8,128)(2,1)S(1)} %shard_map.137), channel_id=1, replica_groups={{0,8,16,24,32,40,48,56,64,72,80,88,96,104,112,120},{4,12,20,28,36,44,52..., dimensions={0} | all-to-all | bytes 524288 | tf_op jit(solution)/shard_map/all_to_all | solution.py:463
  282.6 10.7 %all_to_all.125.arrived_ref = bf16[16,16,512]{2,1,0:T(8,128)(2,1)S(1)} all-to-all(bf16[16,16,512]{2,1,0:T(8,128)(2,1)S(1)} %get-tuple-element.151), channel_id=1, replica_groups={{0,8,16,24,32,40,48,56,64,72,80,88,96,104,112,120},{4,12,20,28,36,44,52..., dimensions={0} | all-to-all | bytes 524288 | tf_op jit(solution)/shard_map/all_to_all | solution.py:463
  293.3 1.4 shard_map.139
  294.7 4.6 %collective-permute-start.34 = (f32[16,512]{1,0:T(8,128)S(1)}, f32[16,512]{1,0:T(8,128)S(1)}, u32[]{:S(2)}, u32[]{:S(2)}) collective-permute-start(f32[16,512]{1,0:T(8,128)S(1)} %get-tuple-element.154.mine_ref), channel_id=1, source_target_pairs={{0,4},{4,0},{8,12},{12,8},{16,20},{20,16},{24,28},{28,24},{32,36},... | collective-permute-start | bytes 98312 | tf_op jit(solution)/shard_map/ppermute | solution.py:466
  303.0 2.0 collective-permute-done.36.refs_2_
  306.7 10.6 %all_to_all.126.refs_0_ = bf16[16,16,512]{2,1,0:T(8,128)(2,1)S(1)} all-to-all(bf16[16,16,512]{2,1,0:T(8,128)(2,1)S(1)} %shard_map.141), channel_id=1, replica_groups={{0,8,16,24,32,40,48,56,64,72,80,88,96,104,112,120},{4,12,20,28,36,44,52..., dimensions={0} | all-to-all | bytes 524288 | tf_op jit(solution)/shard_map/all_to_all | solution.py:463
  317.4 10.8 %all_to_all.127.arrived_ref = bf16[16,16,512]{2,1,0:T(8,128)(2,1)S(1)} all-to-all(bf16[16,16,512]{2,1,0:T(8,128)(2,1)S(1)} %get-tuple-element.156), channel_id=1, replica_groups={{0,8,16,24,32,40,48,56,64,72,80,88,96,104,112,120},{4,12,20,28,36,44,52..., dimensions={0} | all-to-all | bytes 524288 | tf_op jit(solution)/shard_map/all_to_all | solution.py:463
  329.5 4.5 %collective-permute-start.38 = (f32[16,512]{1,0:T(8,128)S(1)}, f32[16,512]{1,0:T(8,128)S(1)}, u32[]{:S(2)}, u32[]{:S(2)}) collective-permute-start(f32[16,512]{1,0:T(8,128)S(1)} %get-tuple-element.159.mine_ref), channel_id=1, source_target_pairs={{0,4},{4,0},{8,12},{12,8},{16,20},{20,16},{24,28},{28,24},{32,36},... | collective-permute-start | bytes 98312 | tf_op jit(solution)/shard_map/ppermute | solution.py:466
  334.9 1.5 collective-permute-start.41
  337.7 3.0 collective-permute-done.40.refs_2_
  342.4 10.6 %all_to_all.128.refs_0_ = bf16[16,16,512]{2,1,0:T(8,128)(2,1)S(1)} all-to-all(bf16[16,16,512]{2,1,0:T(8,128)(2,1)S(1)} %shard_map.145), channel_id=1, replica_groups={{0,8,16,24,32,40,48,56,64,72,80,88,96,104,112,120},{4,12,20,28,36,44,52..., dimensions={0} | all-to-all | bytes 524288 | tf_op jit(solution)/shard_map/all_to_all | solution.py:463
  353.0 10.7 %all_to_all.129.arrived_ref = bf16[16,16,512]{2,1,0:T(8,128)(2,1)S(1)} all-to-all(bf16[16,16,512]{2,1,0:T(8,128)(2,1)S(1)} %get-tuple-element.161), channel_id=1, replica_groups={{0,8,16,24,32,40,48,56,64,72,80,88,96,104,112,120},{4,12,20,28,36,44,52..., dimensions={0} | all-to-all | bytes 524288 | tf_op jit(solution)/shard_map/all_to_all | solution.py:463
  363.8 1.4 shard_map.147
  365.2 4.6 %collective-permute-start.42 = (f32[16,640]{1,0:T(8,128)S(1)}, f32[16,640]{1,0:T(8,128)S(1)}, u32[]{:S(2)}, u32[]{:S(2)}) collective-permute-start(f32[16,640]{1,0:T(8,128)S(1)} %get-tuple-element.167.mine_ref), channel_id=1, source_target_pairs={{0,4},{4,0},{8,12},{12,8},{16,20},{20,16},{24,28},{28,24},{32,36},... | collective-permute-start | bytes 122888 | tf_op jit(solution)/shard_map/ppermute | solution.py:466
  374.2 1.9 collective-permute-done.46.refs_2_
  376.5 1.4 shard_map.149
  378.0 10.9 %all_to_all.130.refs_0_ = bf16[16,16,640]{2,1,0:T(8,128)(2,1)S(1)} all-to-all(bf16[16,16,640]{2,1,0:T(8,128)(2,1)S(1)} %get-tuple-element.176), channel_id=1, replica_groups={{0,8,16,24,32,40,48,56,64,72,80,88,96,104,112,120},{4,12,20,28,36,44,52..., dimensions={0} | all-to-all | bytes 655360 | tf_op jit(solution)/shard_map/all_to_all | solution.py:463
  388.9 10.8 %all_to_all.131.mine_ref = bf16[16,16,512]{2,1,0:T(8,128)(2,1)S(1)} all-to-all(bf16[16,16,512]{2,1,0:T(8,128)(2,1)S(1)} %get-tuple-element.178), channel_id=1, replica_groups={{0,8,16,24,32,40,48,56,64,72,80,88,96,104,112,120},{4,12,20,28,36,44,52..., dimensions={0} | all-to-all | bytes 524288 | tf_op jit(solution)/shard_map/all_to_all | solution.py:463
  399.7 4.5 %collective-permute-start.48 = (bf16[16,16,512]{2,1,0:T(8,128)(2,1)S(1)}, bf16[16,16,512]{2,1,0:T(8,128)(2,1)S(1)}, u32[]{:S(2)}, u32[]{:S(2)}) collective-permute-start(bf16[16,16,512]{2,1,0:T(8,128)(2,1)S(1)} %all_to_all.131.mine_ref), channel_id=1, source_target_pairs={{0,4},{4,0},{8,12},{12,8},{16,20},{20,16},{24,28},{28,24},{32,36},... | collective-permute-start | bytes 786440 | tf_op jit(solution)/shard_map/ppermute | solution.py:466
  (120 shorter events, 55.3 us)
Async XLA Ops:
  0.6 5.0 %copy-start.1 = (f32[16,16384]{1,0:T(8,128)S(1)}, f32[16,16384]{1,0:T(8,128)}, u32[]{:S(2)}) copy-start(f32[16,16384]{1,0:T(8,128)} %start_ref.1) | copy-start | bytes 3145732
  4.2 14.5 %collective-permute-start.4 = (bf16[256,8192]{1,0:T(8,128)(2,1)S(1)}, bf16[256,8192]{1,0:T(8,128)(2,1)S(1)}, u32[]{:S(2)}, u32[]{:S(2)}) collective-permute-start(bf16[256,8192]{1,0:T(8,128)(2,1)S(1)} %get-tuple-element.97.away_ref), channel_id=1, source_target_pairs={{0,4},{4,0},{8,12},{12,8},{16,20},{20,16},{24,28},{28,24},{32,36},... | collective-permute-start | bytes 12582920 | tf_op jit(solution)/shard_map/ppermute | solution.py:466
  5.7 7.3 %copy-start = (f32[8,4,16384]{2,1,0:T(4,128)S(1)}, f32[8,4,16384]{2,1,0:T(4,128)}, u32[]{:S(2)}) copy-start(f32[8,4,16384]{2,1,0:T(4,128)} %bank_ref.1) | copy-start | bytes 6291460
  5.7 7.3 %copy-start.2 = (s32[2,16]{1,0:T(2,128)S(1)}, s32[2,16]{1,0:T(2,128)}, u32[]{:S(2)}) copy-start(s32[2,16]{1,0:T(2,128)} %accept_ref.1) | copy-start | bytes 388
  5.7 7.3 %copy-start.3 = (s32[256]{0:T(256)S(1)}, s32[256]{0:T(256)}, u32[]{:S(2)}) copy-start(s32[256]{0:T(256)} %param.8) | copy-start | bytes 3076
  5.7 7.3 %copy-start.4 = (s32[8]{0:T(128)S(1)}, s32[8]{0:T(128)}, u32[]{:S(2)}) copy-start(s32[8]{0:T(128)} %lag_ref.1) | copy-start | bytes 100
  5.7 7.2 %copy-start.5 = (f32[8]{0:T(128)S(1)}, f32[8]{0:T(128)}, u32[]{:S(2)}) copy-start(f32[8]{0:T(128)} %steps_ref.1) | copy-start | bytes 100
  8.3 7.5 %collective-permute-start.2 = (f32[16,256]{1,0:T(8,128)S(1)}, f32[16,256]{1,0:T(8,128)S(1)}, u32[]{:S(2)}, u32[]{:S(2)}) collective-permute-start(f32[16,256]{1,0:T(8,128)S(1)} %get-tuple-element.101.own), channel_id=1, source_target_pairs={{0,3},{1,0},{2,1},{3,2},{4,7},{5,4},{6,5},{7,6},{8,11},{9,8},{10,9... | collective-permute-start | bytes 49160 | tf_op jit(solution)/shard_map/ppermute | solution.py:472
  12.2 4.1 %collective-permute-start.1 = (f32[16,256]{1,0:T(8,128)S(1)}, f32[16,256]{1,0:T(8,128)S(1)}, u32[]{:S(2)}, u32[]{:S(2)}) collective-permute-start(f32[16,256]{1,0:T(8,128)S(1)} %get-tuple-element.101.own), channel_id=1, source_target_pairs={{0,2},{1,3},{2,0},{3,1},{4,6},{5,7},{6,4},{7,5},{8,10},{9,11},{10,... | collective-permute-start | bytes 49160 | tf_op jit(solution)/shard_map/ppermute | solution.py:472
  12.2 4.1 %collective-permute-start = (f32[16,256]{1,0:T(8,128)S(1)}, f32[16,256]{1,0:T(8,128)S(1)}, u32[]{:S(2)}, u32[]{:S(2)}) collective-permute-start(f32[16,256]{1,0:T(8,128)S(1)} %get-tuple-element.101.own), channel_id=1, source_target_pairs={{0,1},{1,2},{2,3},{3,0},{4,5},{5,6},{6,7},{7,4},{8,9},{9,10},{10,1... | collective-permute-start | bytes 49160 | tf_op jit(solution)/shard_map/ppermute | solution.py:472
  14.0 1.8 collective-permute-start.3
  16.3 2.4 collective-permute-start.5
  47.6 3.8 collective-permute-start.6
  51.4 4.6 %collective-permute-start.9 = (f32[16,512]{1,0:T(8,128)S(1)}, f32[16,512]{1,0:T(8,128)S(1)}, u32[]{:S(2)}, u32[]{:S(2)}) collective-permute-start(f32[16,512]{1,0:T(8,128)S(1)} %shard_map.110.refs_0_), channel_id=1, source_target_pairs={{0,3},{1,0},{2,1},{3,2},{4,7},{5,4},{6,5},{7,6},{8,11},{9,8},{10,9... | collective-permute-start | bytes 98312 | tf_op jit(solution)/shard_map/ppermute | solution.py:472
  51.8 4.3 %collective-permute-start.8 = (f32[16,512]{1,0:T(8,128)S(1)}, f32[16,512]{1,0:T(8,128)S(1)}, u32[]{:S(2)}, u32[]{:S(2)}) collective-permute-start(f32[16,512]{1,0:T(8,128)S(1)} %shard_map.110.refs_0_), channel_id=1, source_target_pairs={{0,2},{1,3},{2,0},{3,1},{4,6},{5,7},{6,4},{7,5},{8,10},{9,11},{10,... | collective-permute-start | bytes 98312 | tf_op jit(solution)/shard_map/ppermute | solution.py:472
  53.5 4.0 collective-permute-start.7
  82.7 5.5 %collective-permute-start.10 = (f32[16,512]{1,0:T(8,128)S(1)}, f32[16,512]{1,0:T(8,128)S(1)}, u32[]{:S(2)}, u32[]{:S(2)}) collective-permute-start(f32[16,512]{1,0:T(8,128)S(1)} %get-tuple-element.120.mine_ref), channel_id=1, source_target_pairs={{0,4},{4,0},{8,12},{12,8},{16,20},{20,16},{24,28},{28,24},{32,36},... | collective-permute-start | bytes 98312 | tf_op jit(solution)/shard_map/ppermute | solution.py:466
  88.2 3.4 collective-permute-start.13
  88.7 4.3 %collective-permute-start.12 = (f32[16,512]{1,0:T(8,128)S(1)}, f32[16,512]{1,0:T(8,128)S(1)}, u32[]{:S(2)}, u32[]{:S(2)}) collective-permute-start(f32[16,512]{1,0:T(8,128)S(1)} %shard_map.115.refs_0_), channel_id=1, source_target_pairs={{0,2},{1,3},{2,0},{3,1},{4,6},{5,7},{6,4},{7,5},{8,10},{9,11},{10,... | collective-permute-start | bytes 98312 | tf_op jit(solution)/shard_map/ppermute | solution.py:472
  89.3 4.0 collective-permute-start.11
  117.4 5.4 %collective-permute-start.14 = (f32[16,512]{1,0:T(8,128)S(1)}, f32[16,512]{1,0:T(8,128)S(1)}, u32[]{:S(2)}, u32[]{:S(2)}) collective-permute-start(f32[16,512]{1,0:T(8,128)S(1)} %get-tuple-element.127.mine_ref), channel_id=1, source_target_pairs={{0,4},{4,0},{8,12},{12,8},{16,20},{20,16},{24,28},{28,24},{32,36},... | collective-permute-start | bytes 98312 | tf_op jit(solution)/shard_map/ppermute | solution.py:466
  122.9 2.8 collective-permute-start.17
  124.4 4.3 %collective-permute-start.16 = (f32[16,512]{1,0:T(8,128)S(1)}, f32[16,512]{1,0:T(8,128)S(1)}, u32[]{:S(2)}, u32[]{:S(2)}) collective-permute-start(f32[16,512]{1,0:T(8,128)S(1)} %shard_map.120.refs_0_), channel_id=1, source_target_pairs={{0,2},{1,3},{2,0},{3,1},{4,6},{5,7},{6,4},{7,5},{8,10},{9,11},{10,... | collective-permute-start | bytes 98312 | tf_op jit(solution)/shard_map/ppermute | solution.py:472
  125.0 4.0 collective-permute-start.15
  153.1 5.5 %collective-permute-start.18 = (f32[16,512]{1,0:T(8,128)S(1)}, f32[16,512]{1,0:T(8,128)S(1)}, u32[]{:S(2)}, u32[]{:S(2)}) collective-permute-start(f32[16,512]{1,0:T(8,128)S(1)} %get-tuple-element.132.mine_ref), channel_id=1, source_target_pairs={{0,4},{4,0},{8,12},{12,8},{16,20},{20,16},{24,28},{28,24},{32,36},... | collective-permute-start | bytes 98312 | tf_op jit(solution)/shard_map/ppermute | solution.py:466
  158.6 2.8 collective-permute-start.21
  159.1 4.3 %collective-permute-start.20 = (f32[16,512]{1,0:T(8,128)S(1)}, f32[16,512]{1,0:T(8,128)S(1)}, u32[]{:S(2)}, u32[]{:S(2)}) collective-permute-start(f32[16,512]{1,0:T(8,128)S(1)} %shard_map.124.refs_0_), channel_id=1, source_target_pairs={{0,2},{1,3},{2,0},{3,1},{4,6},{5,7},{6,4},{7,5},{8,10},{9,11},{10,... | collective-permute-start | bytes 98312 | tf_op jit(solution)/shard_map/ppermute | solution.py:472
  159.8 4.0 collective-permute-start.19
  188.5 5.4 %collective-permute-start.22 = (f32[16,512]{1,0:T(8,128)S(1)}, f32[16,512]{1,0:T(8,128)S(1)}, u32[]{:S(2)}, u32[]{:S(2)}) collective-permute-start(f32[16,512]{1,0:T(8,128)S(1)} %get-tuple-element.137.mine_ref), channel_id=1, source_target_pairs={{0,4},{4,0},{8,12},{12,8},{16,20},{20,16},{24,28},{28,24},{32,36},... | collective-permute-start | bytes 98312 | tf_op jit(solution)/shard_map/ppermute | solution.py:466
  193.9 2.8 collective-permute-start.25
  195.4 4.3 %collective-permute-start.24 = (f32[16,512]{1,0:T(8,128)S(1)}, f32[16,512]{1,0:T(8,128)S(1)}, u32[]{:S(2)}, u32[]{:S(2)}) collective-permute-start(f32[16,512]{1,0:T(8,128)S(1)} %shard_map.128.refs_0_), channel_id=1, source_target_pairs={{0,2},{1,3},{2,0},{3,1},{4,6},{5,7},{6,4},{7,5},{8,10},{9,11},{10,... | collective-permute-start | bytes 98312 | tf_op jit(solution)/shard_map/ppermute | solution.py:472
  196.0 4.0 collective-permute-start.23
  224.3 5.5 %collective-permute-start.26 = (f32[16,512]{1,0:T(8,128)S(1)}, f32[16,512]{1,0:T(8,128)S(1)}, u32[]{:S(2)}, u32[]{:S(2)}) collective-permute-start(f32[16,512]{1,0:T(8,128)S(1)} %get-tuple-element.144.mine_ref), channel_id=1, source_target_pairs={{0,4},{4,0},{8,12},{12,8},{16,20},{20,16},{24,28},{28,24},{32,36},... | collective-permute-start | bytes 98312 | tf_op jit(solution)/shard_map/ppermute | solution.py:466
  229.8 2.8 collective-permute-start.29
  230.3 4.3 %collective-permute-start.28 = (f32[16,512]{1,0:T(8,128)S(1)}, f32[16,512]{1,0:T(8,128)S(1)}, u32[]{:S(2)}, u32[]{:S(2)}) collective-permute-start(f32[16,512]{1,0:T(8,128)S(1)} %shard_map.132.refs_0_), channel_id=1, source_target_pairs={{0,2},{1,3},{2,0},{3,1},{4,6},{5,7},{6,4},{7,5},{8,10},{9,11},{10,... | collective-permute-start | bytes 98312 | tf_op jit(solution)/shard_map/ppermute | solution.py:472
  231.0 4.0 collective-permute-start.27
  259.1 5.4 %collective-permute-start.30 = (f32[16,512]{1,0:T(8,128)S(1)}, f32[16,512]{1,0:T(8,128)S(1)}, u32[]{:S(2)}, u32[]{:S(2)}) collective-permute-start(f32[16,512]{1,0:T(8,128)S(1)} %get-tuple-element.149.mine_ref), channel_id=1, source_target_pairs={{0,4},{4,0},{8,12},{12,8},{16,20},{20,16},{24,28},{28,24},{32,36},... | collective-permute-start | bytes 98312 | tf_op jit(solution)/shard_map/ppermute | solution.py:466
  264.5 2.8 collective-permute-start.33
  266.0 4.3 %collective-permute-start.32 = (f32[16,512]{1,0:T(8,128)S(1)}, f32[16,512]{1,0:T(8,128)S(1)}, u32[]{:S(2)}, u32[]{:S(2)}) collective-permute-start(f32[16,512]{1,0:T(8,128)S(1)} %shard_map.136.refs_0_), channel_id=1, source_target_pairs={{0,2},{1,3},{2,0},{3,1},{4,6},{5,7},{6,4},{7,5},{8,10},{9,11},{10,... | collective-permute-start | bytes 98312 | tf_op jit(solution)/shard_map/ppermute | solution.py:472
  266.6 4.0 collective-permute-start.31
  294.7 5.5 %collective-permute-start.34 = (f32[16,512]{1,0:T(8,128)S(1)}, f32[16,512]{1,0:T(8,128)S(1)}, u32[]{:S(2)}, u32[]{:S(2)}) collective-permute-start(f32[16,512]{1,0:T(8,128)S(1)} %get-tuple-element.154.mine_ref), channel_id=1, source_target_pairs={{0,4},{4,0},{8,12},{12,8},{16,20},{20,16},{24,28},{28,24},{32,36},... | collective-permute-start | bytes 98312 | tf_op jit(solution)/shard_map/ppermute | solution.py:466
  300.2 2.8 collective-permute-start.37
  300.7 4.3 %collective-permute-start.36 = (f32[16,512]{1,0:T(8,128)S(1)}, f32[16,512]{1,0:T(8,128)S(1)}, u32[]{:S(2)}, u32[]{:S(2)}) collective-permute-start(f32[16,512]{1,0:T(8,128)S(1)} %shard_map.140.refs_0_), channel_id=1, source_target_pairs={{0,2},{1,3},{2,0},{3,1},{4,6},{5,7},{6,4},{7,5},{8,10},{9,11},{10,... | collective-permute-start | bytes 98312 | tf_op jit(solution)/shard_map/ppermute | solution.py:472
  301.4 4.0 collective-permute-start.35
  329.5 5.4 %collective-permute-start.38 = (f32[16,512]{1,0:T(8,128)S(1)}, f32[16,512]{1,0:T(8,128)S(1)}, u32[]{:S(2)}, u32[]{:S(2)}) collective-permute-start(f32[16,512]{1,0:T(8,128)S(1)} %get-tuple-element.159.mine_ref), channel_id=1, source_target_pairs={{0,4},{4,0},{8,12},{12,8},{16,20},{20,16},{24,28},{28,24},{32,36},... | collective-permute-start | bytes 98312 | tf_op jit(solution)/shard_map/ppermute | solution.py:466
  334.9 2.8 collective-permute-start.41
  336.4 4.3 %collective-permute-start.40 = (f32[16,512]{1,0:T(8,128)S(1)}, f32[16,512]{1,0:T(8,128)S(1)}, u32[]{:S(2)}, u32[]{:S(2)}) collective-permute-start(f32[16,512]{1,0:T(8,128)S(1)} %shard_map.144.refs_0_), channel_id=1, source_target_pairs={{0,2},{1,3},{2,0},{3,1},{4,6},{5,7},{6,4},{7,5},{8,10},{9,11},{10,... | collective-permute-start | bytes 98312 | tf_op jit(solution)/shard_map/ppermute | solution.py:472
  337.1 4.0 collective-permute-start.39
  365.2 5.5 %collective-permute-start.42 = (f32[16,640]{1,0:T(8,128)S(1)}, f32[16,640]{1,0:T(8,128)S(1)}, u32[]{:S(2)}, u32[]{:S(2)}) collective-permute-start(f32[16,640]{1,0:T(8,128)S(1)} %get-tuple-element.167.mine_ref), channel_id=1, source_target_pairs={{0,4},{4,0},{8,12},{12,8},{16,20},{20,16},{24,28},{28,24},{32,36},... | collective-permute-start | bytes 122888 | tf_op jit(solution)/shard_map/ppermute | solution.py:466
  370.7 2.5 collective-permute-start.43
  371.1 3.2 collective-permute-start.44
  371.2 3.0 collective-permute-start.47
  371.7 4.4 %collective-permute-start.46 = (f32[16,640]{1,0:T(8,128)S(1)}, f32[16,640]{1,0:T(8,128)S(1)}, u32[]{:S(2)}, u32[]{:S(2)}) collective-permute-start(f32[16,640]{1,0:T(8,128)S(1)} %shard_map.148.refs_0_), channel_id=1, source_target_pairs={{0,2},{1,3},{2,0},{3,1},{4,6},{5,7},{6,4},{7,5},{8,10},{9,11},{10,... | collective-permute-start | bytes 122888 | tf_op jit(solution)/shard_map/ppermute | solution.py:472
  372.4 4.1 %collective-permute-start.45 = (f32[16,640]{1,0:T(8,128)S(1)}, f32[16,640]{1,0:T(8,128)S(1)}, u32[]{:S(2)}, u32[]{:S(2)}) collective-permute-start(f32[16,640]{1,0:T(8,128)S(1)} %shard_map.148.refs_0_), channel_id=1, source_target_pairs={{0,1},{1,2},{2,3},{3,0},{4,5},{5,6},{6,7},{7,4},{8,9},{9,10},{10,1... | collective-permute-start | bytes 122888 | tf_op jit(solution)/shard_map/ppermute | solution.py:472
  399.7 5.7 %collective-permute-start.48 = (bf16[16,16,512]{2,1,0:T(8,128)(2,1)S(1)}, bf16[16,16,512]{2,1,0:T(8,128)(2,1)S(1)}, u32[]{:S(2)}, u32[]{:S(2)}) collective-permute-start(bf16[16,16,512]{2,1,0:T(8,128)(2,1)S(1)} %all_to_all.131.mine_ref), channel_id=1, source_target_pairs={{0,4},{4,0},{8,12},{12,8},{16,20},{20,16},{24,28},{28,24},{32,36},... | collective-permute-start | bytes 786440 | tf_op jit(solution)/shard_map/ppermute | solution.py:466
